TPU v7x, 128 devices: a whole 4x4x4 slice. The times are simulated.
128 devices in a mesh: gz: 16 (over z, y), gy: 8 (over x, core).
Axes of the slice: x: 4, y: 4, z: 4, core: 2. Of those that a mesh axis runs over, the one named last changes fastest.
Arguments:
- species_field: float32 [4, 512, 512, 512], P(None, 'gz', 'gy'), may hold values from -100 to 100
Outputs:
- core_tensor: float32 [4, 512, 4096], P(None, ('gz', 'gy'))
- basis_z: float32 [512, 64], replicated
- basis_y: float32 [512, 64], replicated
All inputs are finite; a program needn't handle non-finite values.
Results may differ from a plain program's by a relative error of at most 0.0003.
Values sent between devices are 32-bit elements; how exact they have to be, the bound alone decides.
A program may use at most 192 MiB of HBM per device.

v0:
```python
import math

import jax
import jax.numpy as jnp
from jax import lax
from jax.sharding import PartitionSpec as P

GRID = 512
RANK = 64
ITERS = 4


def start_table(order, width):
    row_index = jnp.arange(order).astype(jnp.float32)
    col_index = jnp.arange(width).astype(jnp.float32)
    return jnp.cos(math.pi * (row_index[:, None] + 0.5) * col_index[None, :] / order)


def solve_factor(product, inner_gram):
    factor = jnp.linalg.cholesky(inner_gram)
    return lax.linalg.triangular_solve(
        factor, product, left_side=False, lower=True, transpose_a=True
    )


def inner_products(left, right):
    return lax.dot_general(left, right, (((0,), (0,)), ((), ())), precision=lax.Precision.HIGHEST)


def mode_products(left, right, mode):
    others = tuple((d for d in range(4) if d != mode))
    return lax.dot_general(
        left, right, ((others, others), ((), ())), precision=lax.Precision.HIGHEST
    )


def leaf_basis(fibres, mode):
    basis_now = start_table(GRID, RANK)
    gram_total = lax.psum(mode_products(fibres, fibres, mode), ("gz", "gy"))
    for iteration in range(ITERS):
        product = jnp.dot(gram_total, basis_now, precision=lax.Precision.HIGHEST)
        basis_now = solve_factor(product, inner_products(product, product))
    return basis_now


def body(species_field):
    fibres_z = lax.all_to_all(species_field, "gz", split_axis=2, concat_axis=1, tiled=True)
    basis_z = leaf_basis(fibres_z, 1)
    reduced = jnp.einsum("szyx,zr->sryx", fibres_z, basis_z, precision=lax.Precision.HIGHEST)
    mixed = lax.all_to_all(reduced, ("gz", "gy"), split_axis=3, concat_axis=2, tiled=True)
    count_gz = lax.axis_size("gz")
    count_gy = lax.axis_size("gy")
    shape_now = mixed.shape
    y_local = shape_now[2] // (count_gz * count_gy)
    blocks = mixed.reshape(shape_now[0], shape_now[1], count_gz, count_gy, y_local, shape_now[3])
    fibres_y = jnp.transpose(blocks, (0, 1, 3, 2, 4, 5)).reshape(shape_now)
    basis_y = leaf_basis(fibres_y, 2)
    core_tensor = jnp.einsum("sryx,yq->sxrq", fibres_y, basis_y, precision=lax.Precision.HIGHEST)
    core_tensor = core_tensor.reshape(fibres_y.shape[0], fibres_y.shape[3], RANK * RANK)
    return (core_tensor, basis_z, basis_y)


def solution(mesh):
    in_specs = (P(None, "gz", "gy", None),)
    out_specs = (P(None, ("gz", "gy"), None), P(), P())
    return jax.shard_map(body, mesh=mesh, in_specs=in_specs, out_specs=out_specs, check_vma=False)
```

profile of v0, /device:TPU:1, one launch (start us, length us, event | category | flops | bytes accessed | tf_op | source)
XLA Modules:
  0.0 767.0 jit_solution(3029973958028382066)
XLA Ops:
  7.2 15.2 %copy.29 = f32[4,32,64,512]{3,1,0,2:T(8,128)S(1)} copy(f32[4,32,64,512]{3,2,1,0:T(8,128)} %param.4) | data formatting | bytes 33554432 | tf_op args[0]
  22.5 193.2 %all_to_all.33 = f32[4,32,64,512]{3,1,0,2:T(8,128)} all-to-all(f32[4,32,64,512]{3,1,0,2:T(8,128)S(1)} %copy.29), channel_id=1, replica_groups=mesh['gz'=16,'gy'=8] {'gz'}, dimensions={2} | all-to-all | bytes 33554432 | tf_op jit(solution)/shard_map/all_to_all | solution.py:47
  215.6 6.9 copy.30
  222.5 5.7 copy-done
  228.2 28.8 %convolution_bitcast_fusion.2 = f32[512,512]{1,0:T(8,128)} fusion(f32[4,512,4,512]{3,1,2,0:T(8,128)S(1)} %bitcast.170), kind=kOutput, calls=%fused_computation.2 | convolution fusion | flops 25769803776 | bytes 17825792 | tf_op jit(solution)/shard_map/dot_general | solution.py:32
  257.3 146.0 %all-reduce.3.cloned.1.call-done = f32[512,512]{1,0:T(8,128)} async-done(((f32[512,512]{1,0:T(8,128)}), f32[512,512]{1,0:T(8,128)}) %all-reduce.3.cloned.1.call-update) | async-done | bytes 1048592 | tf_op jit(solution)/shard_map/psum | solution.py:39
  407.0 5.8 cholesky.134
  414.2 4.9 custom-call.12
  422.2 5.8 cholesky.145
  429.4 4.9 custom-call.13
  436.1 5.8 cholesky.156
  443.3 4.9 custom-call.14
  450.1 5.8 cholesky.167
  462.8 14.2 %convolution_bitcast_fusion = f32[4,64,4,512]{3,1,2,0:T(8,128)S(1)} fusion(f32[4,512,4,512]{3,1,2,0:T(8,128)} %bitcast.171, f32[64,512]{1,0:T(8,128)S(1)} %fusion.27), kind=kOutput, calls=%fused_computation | convolution fusion | flops 3221225472 | bytes 19005440 | tf_op jit(solution)/shard_map/szyx,zr->sryx/dot_general | solution.py:49
  480.5 5.3 reshape.76
  485.8 37.2 %all_to_all.34 = f32[128,1,4096]{2,1,0:T(1,128)} all-to-all(f32[128,1,4096]{2,1,0:T(1,128)S(1)} %reshape.76), channel_id=1, replica_groups=mesh['gz'=16,'gy'=8] {'gz','gy'}, dimensions={0} | all-to-all | bytes 4194304 | tf_op jit(solution)/shard_map/all_to_all | solution.py:50
  523.6 7.3 reduce.4
  543.4 8.0 %convolution_bitcast_fusion.1 = f32[512,512]{1,0:T(8,128)} fusion(f32[4,64,512,4]{1,2,3,0:T(8,128)S(1)} %bitcast.172), kind=kOutput, calls=%fused_computation.1 | convolution fusion | flops 3221225472 | bytes 3145728 | tf_op jit(solution)/shard_map/dot_general | solution.py:32
  551.4 143.0 %all-reduce.5.cloned.1.call-done = f32[512,512]{1,0:T(8,128)} async-done(((f32[512,512]{1,0:T(8,128)}), f32[512,512]{1,0:T(8,128)}) %all-reduce.5.cloned.1.call-update) | async-done | bytes 1048592 | tf_op jit(solution)/shard_map/psum | solution.py:39
  698.4 5.8 cholesky.178
  713.5 5.8 cholesky.189
  727.4 5.8 cholesky.200
  734.6 4.9 custom-call.18
  741.4 5.8 cholesky.211
  (93 shorter events, 75.0 us)
Async XLA Ops:
  7.2 396.1 %all-reduce.3.cloned.1.call-start = ((), (), s32[]{:S(2)}) async-start(), calls=%async_computation.2 | async-start | bytes 2097152 | tf_op jit(solution)/shard_map/psum | solution.py:39
  222.5 5.7 copy-start
  257.0 437.4 %all-reduce.5.cloned.1.call-start = ((), (), s32[]{:S(2)}) async-start(), calls=%async_computation.3 | async-start | bytes 2097152 | tf_op jit(solution)/shard_map/psum | solution.py:39
  403.3 31.3 %copy-start.2 = (f32[512,512]{1,0:T(8,128)S(1)}, f32[512,512]{1,0:T(8,128)}, u32[]{:S(2)}) copy-start(f32[512,512]{1,0:T(8,128)} %all-reduce.3.cloned.1.call-done) | copy-start | bytes 3145732
  462.8 14.2 %copy-start.4 = (f32[64,512]{1,0:T(8,128)}, f32[64,512]{1,0:T(8,128)S(1)}, u32[]{:S(2)}) copy-start(f32[64,512]{1,0:T(8,128)S(1)} %fusion.27) | copy-start | bytes 393220
  541.5 1.9 copy-start.1
  694.4 31.5 %copy-start.3 = (f32[512,512]{1,0:T(8,128)S(1)}, f32[512,512]{1,0:T(8,128)}, u32[]{:S(2)}) copy-start(f32[512,512]{1,0:T(8,128)} %all-reduce.5.cloned.1.call-done) | copy-start | bytes 3145732
  753.8 6.0 copy-start.5
Sparse Core Ops, SparseCore 0:
  257.1 146.1 all-reduce.2
  551.5 142.8 all-reduce.4
where the time goes:
time: 776 us; the launch traced here: 767 us
  waiting for transfers between devices  289 us (37%)
  blocking collectives  230 us (30%)
  other arithmetic  104 us (13%)
  matrix products  76.8 us (10%)
  local copies, waits for them, and re-layouts  51.3 us (7%)
  between operations  14.9 us (2%)
    psum x2, waiting for transfers between devices, leaf_basis(): gram_total = lax.psum(mode_products(fibres, fibres, mode), ('gz', 'gy'))  289 us
    all_to_all x1, blocking collectives, body(): lax.all_to_all(species_field, 'gz', split_axis=2, concat_axis=1, tiled=True)  193 us
    another operation x24, other arithmetic, solve_factor(): factor = jnp.linalg.cholesky(inner_gram)  52.2 us
    another operation x16, other arithmetic, solve_factor(): lax.linalg.triangular_solve(factor, product, left_side=False, lower=True,...  44.7 us
    all_to_all x1, blocking collectives, body(): lax.all_to_all(reduced, ('gz', 'gy'), split_axis=3, concat_axis=2, tiled=...  37.2 us
    dot_general x2, matrix products, mode_products(): lax.dot_general(left, right, ((others, others), ((), ())), precision=lax....  36.7 us
    unnamed x15, local copies, waits for them, and re-layouts  32.5 us
    dot_general x8, matrix products, leaf_basis(): product = jnp.dot(gram_total, basis_now, precision=lax.Precision.HIGHEST)  16.2 us
  transfers between devices with their start and end apart: 2, of which 2 were waited for; matrix products, arithmetic and copies ran while one was open for 0% of the time, Pallas kernels for 0%

commit v1 on v0

--- a/solution.py
+++ b/solution.py
@@ -34,9 +34,21 @@
     )
 
 
+def sum_over_mesh(gram):
+    axes = ("gz", "gy")
+    count = lax.axis_size("gz") * lax.axis_size("gy")
+    rows = gram.shape[0]
+    parts = lax.all_to_all(
+        gram.reshape(count, rows // count, rows), axes, 0, 0, tiled=True
+    )
+    mine = parts.sum(0)
+    tiled = jnp.broadcast_to(mine[None], (count,) + mine.shape)
+    return lax.all_to_all(tiled, axes, 0, 0, tiled=True).reshape(rows, rows)
+
+
 def leaf_basis(fibres, mode):
     basis_now = start_table(GRID, RANK)
-    gram_total = lax.psum(mode_products(fibres, fibres, mode), ("gz", "gy"))
+    gram_total = sum_over_mesh(mode_products(fibres, fibres, mode))
     for iteration in range(ITERS):
         product = jnp.dot(gram_total, basis_now, precision=lax.Precision.HIGHEST)
         basis_now = solve_factor(product, inner_products(product, product))

time: 776 us -> 575 us (0.74)
  waiting for transfers between devices: 289 us -> 19.2 us
  blocking collectives: 230 us -> 301 us
  local copies, waits for them, and re-layouts: 51.3 us -> 65.4 us
  between operations: 14.9 us -> 1.37 us
    psum x2 -> x0, waiting for transfers between devices: 289 us -> none  [leaf_basis(): gram_total = lax.psum(mode_products(fibres, fibres, mode), ('gz', 'gy'))]
    all_to_all x0 -> x3, blocking collectives: none -> 72.9 us  [the longest x2 49.4 us: sum_over_mesh(): lax.all_to_all(gram.reshape(count, rows // count, rows), axes, 0, 0, tile...]
    dot_general x0 -> x3, local copies, waits for them, and re-layouts: none -> 20.4 us  [mode_products(): lax.dot_general(left, right, ((others, others), ((), ())), precision=lax....]
    all_to_all x0 -> x1, waiting for transfers between devices: none -> 19.2 us  [sum_over_mesh(): return lax.all_to_all(tiled, axes, 0, 0, tiled=True).reshape(rows, rows)]
    unnamed x15 -> x9, local copies, waits for them, and re-layouts: 32.5 us -> 24.9 us
  transfers between devices with their start and end apart: 2 -> 1, of which waited for: 2 -> 1; matrix products, arithmetic and copies ran while one was open for 0% -> 0% of each run, Pallas kernels for 0% -> 0%
where the time goes in v1:
time: 575 us; the launch traced here: 571 us
  blocking collectives  301 us (52%)
  other arithmetic  105 us (18%)
  matrix products  74.2 us (13%)
  local copies, waits for them, and re-layouts  65.4 us (11%)
  waiting for transfers between devices  19.2 us (3%)
    all_to_all x1, blocking collectives, body(): lax.all_to_all(species_field, 'gz', split_axis=2, concat_axis=1, tiled=True)  194 us
    another operation x24, other arithmetic, solve_factor(): factor = jnp.linalg.cholesky(inner_gram)  52.8 us
    all_to_all x2, blocking collectives, sum_over_mesh(): lax.all_to_all(gram.reshape(count, rows // count, rows), axes, 0, 0, tile...  49.4 us
    another operation x16, other arithmetic, solve_factor(): lax.linalg.triangular_solve(factor, product, left_side=False, lower=True,...  44.4 us
    dot_general x2, matrix products, mode_products(): lax.dot_general(left, right, ((others, others), ((), ())), precision=lax....  39.4 us
    all_to_all x1, blocking collectives, body(): lax.all_to_all(reduced, ('gz', 'gy'), split_axis=3, concat_axis=2, tiled=...  35 us
    unnamed x9, local copies, waits for them, and re-layouts  24.9 us
    all_to_all x1, blocking collectives, sum_over_mesh(): return lax.all_to_all(tiled, axes, 0, 0, tiled=True).reshape(rows, rows)  23.5 us
  transfers between devices with their start and end apart: 1, of which 1 were waited for; matrix products, arithmetic and copies ran while one was open for 0% of the time, Pallas kernels for 0%

profile of v1, /device:TPU:1, one launch (start us, length us, event | category | flops | bytes accessed | tf_op | source)
XLA Modules:
  0.0 571.2 jit_solution(17424222337443661387)
XLA Ops:
  0.6 15.2 %copy.32 = f32[4,32,64,512]{3,1,0,2:T(8,128)S(1)} copy(f32[4,32,64,512]{3,2,1,0:T(8,128)} %param.4) | data formatting | bytes 33554432 | tf_op args[0]
  15.9 193.6 %all_to_all.53 = f32[4,32,64,512]{3,1,0,2:T(8,128)S(1)} all-to-all(f32[4,32,64,512]{3,1,0,2:T(8,128)S(1)} %copy.32), channel_id=1, replica_groups=mesh['gz'=16,'gy'=8] {'gz'}, dimensions={2} | all-to-all | bytes 33554432 | tf_op jit(solution)/shard_map/all_to_all | solution.py:59
  209.5 6.3 %copy.33 = f32[4,32,16,4,512]{4,1,2,3,0:T(8,128)} copy(f32[4,32,16,4,512]{4,1,0,3,2:T(8,128)S(1)} %bitcast.185) | data formatting | bytes 33554432 | tf_op jit(solution)/shard_map/all_to_all | solution.py:59
  215.8 19.0 %dot_general.69 = f32[128,4,4,4,512]{4,1,0,3,2:T(4,128)} reshape(f32[512,4,4,512]{3,0,2,1:T(8,128)} %bitcast.182) | data formatting | bytes 33554432 | tf_op jit(solution)/shard_map/dot_general | solution.py:32
  234.8 32.4 %fusion.7 = f32[128,4,512]{2,0,1:T(8,128)S(1)} fusion(f32[4,512,4,512,1]{3,1,2,0,4:T(8,128)} %bitcast.183, f32[128,4,4,4,512]{4,1,0,3,2:T(4,128)} %dot_general.69), kind=kOutput, calls=%fused_computation.6 | convolution fusion | flops 25769803776 | bytes 34603008 | tf_op jit(solution)/shard_map/dot_general | solution.py:32
  267.9 26.2 %all_to_all.54 = f32[128,4,512]{2,1,0:T(4,128)S(1)} all-to-all(f32[128,4,512]{2,1,0:T(4,128)S(1)} %copy.35), channel_id=1, replica_groups=mesh['gz'=16,'gy'=8] {'gz','gy'}, dimensions={0} | all-to-all | bytes 2097152 | tf_op jit(solution)/shard_map/all_to_all | solution.py:41
  299.9 19.2 %all-to-all-done.2 = f32[128,4,512]{2,1,0:T(4,128)S(1)} async-done(((f32[128,4,512]{2,1,0:T(4,128)}), f32[128,4,512]{2,1,0:T(4,128)S(1)}, u32[]{:S(2)}, u32[]{:S(2)}) %all-to-all-start.2) | async-done | bytes 1048608 | tf_op jit(solution)/shard_map/all_to_all | solution.py:46
  322.0 5.8 %cholesky.134 = f32[64,64]{1,0:T(8,128)S(1)} custom-call(f32[64,64]{1,0:T(8,128)S(1)} %fusion.45), custom_call_target="Cholesky" | custom-call | tf_op jit(solution)/shard_map/jit(cholesky)/cholesky | solution.py:20
  335.9 5.8 %cholesky.145 = f32[64,64]{1,0:T(8,128)S(1)} custom-call(f32[64,64]{1,0:T(8,128)S(1)} %fusion.43), custom_call_target="Cholesky" | custom-call | tf_op jit(solution)/shard_map/jit(cholesky)/cholesky | solution.py:20
  349.8 5.8 %cholesky.156 = f32[64,64]{1,0:T(8,128)S(1)} custom-call(f32[64,64]{1,0:T(8,128)S(1)} %fusion.41), custom_call_target="Cholesky" | custom-call | tf_op jit(solution)/shard_map/jit(cholesky)/cholesky | solution.py:20
  357.0 4.9 custom-call.14
  363.8 6.2 %cholesky.167 = f32[64,64]{1,0:T(8,128)S(1)} custom-call(f32[64,64]{1,0:T(8,128)S(1)} %fusion.39), custom_call_target="Cholesky" | custom-call | tf_op jit(solution)/shard_map/jit(cholesky)/cholesky | solution.py:20
  376.6 14.2 %convolution_bitcast_fusion = f32[4,64,4,512]{3,1,2,0:T(8,128)S(1)} fusion(f32[4,512,4,512]{3,1,2,0:T(8,128)} %bitcast.184, f32[64,512]{1,0:T(8,128)S(1)} %fusion.37), kind=kOutput, calls=%fused_computation.4 | convolution fusion | flops 3221225472 | bytes 19005440 | tf_op jit(solution)/shard_map/szyx,zr->sryx/dot_general | solution.py:61
  394.3 5.3 reshape.92
  399.6 35.0 %all_to_all.55 = f32[128,1,4096]{2,1,0:T(1,128)} all-to-all(f32[128,1,4096]{2,1,0:T(1,128)S(1)} %reshape.92), channel_id=1, replica_groups=mesh['gz'=16,'gy'=8] {'gz','gy'}, dimensions={0} | all-to-all | bytes 4194304 | tf_op jit(solution)/shard_map/all_to_all | solution.py:62
  435.1 7.3 %reduce.4 = f32[128,4096]{1,0:T(8,128)S(1)} reduce(f32[128,1,4096]{2,1,0:T(1,128)} %all_to_all.55, f32[]{:T(128)} %broadcast.82), dimensions={1}, to_apply=%all_to_all.42.reduce_sub_computation | reduce | bytes 4194308 | tf_op jit(solution)/shard_map/all_to_all | solution.py:62
  453.0 7.0 %fusion.4 = f32[128,4,512]{2,0,1:T(8,128)S(1)} fusion(f32[4,64,512,4,1]{1,2,3,0,4:T(8,128)S(1)} %bitcast.186, f32[128,4,4,64,4]{3,1,0,4,2:T(4,128)S(1)} %bitcast.187), kind=kOutput, calls=%fused_computation.5 | convolution fusion | flops 3221225472 | bytes 5242880 | tf_op jit(solution)/shard_map/dot_general | solution.py:32
  460.7 23.2 %all_to_all.56 = f32[128,4,512]{2,1,0:T(4,128)S(1)} all-to-all(f32[128,4,512]{2,1,0:T(4,128)S(1)} %copy.45), channel_id=1, replica_groups=mesh['gz'=16,'gy'=8] {'gz','gy'}, dimensions={0} | all-to-all | bytes 2097152 | tf_op jit(solution)/shard_map/all_to_all | solution.py:41
  484.2 23.5 %all_to_all.57 = f32[128,4,512]{2,1,0:T(4,128)S(1)} all-to-all(f32[128,4,512]{2,1,0:T(4,128)S(1)} %broadcast_in_dim.5), channel_id=1, replica_groups=mesh['gz'=16,'gy'=8] {'gz','gy'}, dimensions={0} | all-to-all | bytes 2097152 | tf_op jit(solution)/shard_map/all_to_all | solution.py:46
  510.5 5.8 %cholesky.178 = f32[64,64]{1,0:T(8,128)S(1)} custom-call(f32[64,64]{1,0:T(8,128)S(1)} %fusion.36), custom_call_target="Cholesky" | custom-call | tf_op jit(solution)/shard_map/jit(cholesky)/cholesky | solution.py:20
  524.4 5.8 %cholesky.189 = f32[64,64]{1,0:T(8,128)S(1)} custom-call(f32[64,64]{1,0:T(8,128)S(1)} %fusion.34), custom_call_target="Cholesky" | custom-call | tf_op jit(solution)/shard_map/jit(cholesky)/cholesky | solution.py:20
  538.4 5.8 %cholesky.200 = f32[64,64]{1,0:T(8,128)S(1)} custom-call(f32[64,64]{1,0:T(8,128)S(1)} %fusion.32), custom_call_target="Cholesky" | custom-call | tf_op jit(solution)/shard_map/jit(cholesky)/cholesky | solution.py:20
  552.3 6.1 %cholesky.211 = f32[64,64]{1,0:T(8,128)S(1)} custom-call(f32[64,64]{1,0:T(8,128)S(1)} %fusion.30), custom_call_target="Cholesky" | custom-call | tf_op jit(solution)/shard_map/jit(cholesky)/cholesky | solution.py:20
  559.7 4.9 custom-call.19
  (95 shorter events, 85.2 us)
Async XLA Ops:
  295.4 23.8 %all-to-all-start.2 = ((f32[128,4,512]{2,1,0:T(4,128)}), f32[128,4,512]{2,1,0:T(4,128)S(1)}, u32[]{:S(2)}, u32[]{:S(2)}) async-start(f32[128,4,512]{2,1,0:T(4,128)} %broadcast_in_dim.4), calls=%async_computation.2 | async-start | bytes 2097152 | tf_op jit(solution)/shard_map/all_to_all | solution.py:46
  376.6 14.2 %copy-start.1 = (f32[64,512]{1,0:T(8,128)}, f32[64,512]{1,0:T(8,128)S(1)}, u32[]{:S(2)}) copy-start(f32[64,512]{1,0:T(8,128)S(1)} %fusion.37) | copy-start | bytes 393220
  453.0 7.0 %copy-start = (f32[4,64,16,8,4,4]{1,4,2,3,5,0:T(4,128)}, f32[4,64,16,8,4,4]{1,4,2,3,5,0:T(4,128)S(1)}, u32[]{:S(2)}) copy-start(f32[4,64,16,8,4,4]{1,4,2,3,5,0:T(4,128)S(1)} %copy.42) | copy-start | bytes 6291460
  564.9 6.0 %copy-start.2 = (f32[64,512]{1,0:T(8,128)}, f32[64,512]{1,0:T(8,128)S(1)}, u32[]{:S(2)}) copy-start(f32[64,512]{1,0:T(8,128)S(1)} %fusion.28) | copy-start | bytes 393220

commit v2 on v1

--- a/solution.py
+++ b/solution.py
@@ -30,7 +30,7 @@
 def mode_products(left, right, mode):
     others = tuple((d for d in range(4) if d != mode))
     return lax.dot_general(
-        left, right, ((others, others), ((), ())), precision=lax.Precision.HIGHEST
+        left, right, ((others, others), ((), ())), precision=lax.Precision.HIGH
     )
 
 
@@ -58,7 +58,7 @@
 def body(species_field):
     fibres_z = lax.all_to_all(species_field, "gz", split_axis=2, concat_axis=1, tiled=True)
     basis_z = leaf_basis(fibres_z, 1)
-    reduced = jnp.einsum("szyx,zr->sryx", fibres_z, basis_z, precision=lax.Precision.HIGHEST)
+    reduced = jnp.einsum("szyx,zr->sryx", fibres_z, basis_z, precision=lax.Precision.HIGH)
     mixed = lax.all_to_all(reduced, ("gz", "gy"), split_axis=3, concat_axis=2, tiled=True)
     count_gz = lax.axis_size("gz")
     count_gy = lax.axis_size("gy")
@@ -67,7 +67,7 @@
     blocks = mixed.reshape(shape_now[0], shape_now[1], count_gz, count_gy, y_local, shape_now[3])
     fibres_y = jnp.transpose(blocks, (0, 1, 3, 2, 4, 5)).reshape(shape_now)
     basis_y = leaf_basis(fibres_y, 2)
-    core_tensor = jnp.einsum("sryx,yq->sxrq", fibres_y, basis_y, precision=lax.Precision.HIGHEST)
+    core_tensor = jnp.einsum("sryx,yq->sxrq", fibres_y, basis_y, precision=lax.Precision.HIGH)
     core_tensor = core_tensor.reshape(fibres_y.shape[0], fibres_y.shape[3], RANK * RANK)
     return (core_tensor, basis_z, basis_y)
 

time: 575 us -> 554 us (0.963)
  matrix products: 74.2 us -> 53.8 us
    dot_general x2, matrix products: 39.4 us -> 25.2 us  [mode_products(): lax.dot_general(left, right, ((others, others), ((), ())), precision=lax....]
    dot_general x2, matrix products: 19.1 us -> 12.8 us  [the longest x1 9.16 us: body(): jnp.einsum('szyx,zr->sryx', fibres_z, basis_z, precision=lax.Precision.HIGH)]
where the time goes in v2:
time: 554 us; the launch traced here: 550 us
  blocking collectives  301 us (54%)
  other arithmetic  105 us (19%)
  local copies, waits for them, and re-layouts  65.5 us (12%)
  matrix products  53.8 us (10%)
  waiting for transfers between devices  18.9 us (3%)
    all_to_all x1, blocking collectives, body(): lax.all_to_all(species_field, 'gz', split_axis=2, concat_axis=1, tiled=True)  193 us
    another operation x24, other arithmetic, solve_factor(): factor = jnp.linalg.cholesky(inner_gram)  52.5 us
    all_to_all x2, blocking collectives, sum_over_mesh(): lax.all_to_all(gram.reshape(count, rows // count, rows), axes, 0, 0, tile...  49.4 us
    another operation x16, other arithmetic, solve_factor(): lax.linalg.triangular_solve(factor, product, left_side=False, lower=True,...  44.4 us
    all_to_all x1, blocking collectives, body(): lax.all_to_all(reduced, ('gz', 'gy'), split_axis=3, concat_axis=2, tiled=...  35 us
    dot_general x2, matrix products, mode_products(): lax.dot_general(left, right, ((others, others), ((), ())), precision=lax....  25.2 us
    unnamed x9, local copies, waits for them, and re-layouts  24.9 us
    all_to_all x1, blocking collectives, sum_over_mesh(): return lax.all_to_all(tiled, axes, 0, 0, tiled=True).reshape(rows, rows)  23.5 us
  transfers between devices with their start and end apart: 1, of which 1 were waited for; matrix products, arithmetic and copies ran while one was open for 0% of the time, Pallas kernels for 0%

profile of v2, /device:TPU:1, one launch (start us, length us, event | category | flops | bytes accessed | tf_op | source)
XLA Modules:
  0.0 550.2 jit_solution(17963719491719686985)
XLA Ops:
  0.6 15.2 %copy.32 = f32[4,32,64,512]{3,1,0,2:T(8,128)S(1)} copy(f32[4,32,64,512]{3,2,1,0:T(8,128)} %param.4) | data formatting | bytes 33554432 | tf_op args[0]
  15.9 193.4 %all_to_all.53 = f32[4,32,64,512]{3,1,0,2:T(8,128)S(1)} all-to-all(f32[4,32,64,512]{3,1,0,2:T(8,128)S(1)} %copy.32), channel_id=1, replica_groups=mesh['gz'=16,'gy'=8] {'gz'}, dimensions={2} | all-to-all | bytes 33554432 | tf_op jit(solution)/shard_map/all_to_all | solution.py:59
  209.3 6.3 %copy.33 = f32[4,32,16,4,512]{4,1,2,3,0:T(8,128)} copy(f32[4,32,16,4,512]{4,1,0,3,2:T(8,128)S(1)} %bitcast.185) | data formatting | bytes 33554432 | tf_op jit(solution)/shard_map/all_to_all | solution.py:59
  215.5 19.0 %dot_general.69 = f32[128,4,4,4,512]{4,1,0,3,2:T(4,128)} reshape(f32[512,4,4,512]{3,0,2,1:T(8,128)} %bitcast.182) | data formatting | bytes 33554432 | tf_op jit(solution)/shard_map/dot_general | solution.py:32
  234.6 21.7 %fusion.7 = f32[128,4,512]{2,0,1:T(8,128)S(1)} fusion(f32[4,512,4,512,1]{3,1,2,0,4:T(8,128)} %bitcast.183, f32[128,4,4,4,512]{4,1,0,3,2:T(4,128)} %dot_general.69), kind=kOutput, calls=%fused_computation.6 | convolution fusion | flops 12884901888 | bytes 34603008 | tf_op jit(solution)/shard_map/dot_general | solution.py:32
  256.9 26.2 %all_to_all.54 = f32[128,4,512]{2,1,0:T(4,128)S(1)} all-to-all(f32[128,4,512]{2,1,0:T(4,128)S(1)} %copy.35), channel_id=1, replica_groups=mesh['gz'=16,'gy'=8] {'gz','gy'}, dimensions={0} | all-to-all | bytes 2097152 | tf_op jit(solution)/shard_map/all_to_all | solution.py:41
  289.3 18.9 %all-to-all-done.2 = f32[128,4,512]{2,1,0:T(4,128)S(1)} async-done(((f32[128,4,512]{2,1,0:T(4,128)}), f32[128,4,512]{2,1,0:T(4,128)S(1)}, u32[]{:S(2)}, u32[]{:S(2)}) %all-to-all-start.2) | async-done | bytes 1048608 | tf_op jit(solution)/shard_map/all_to_all | solution.py:46
  311.0 5.8 %cholesky.134 = f32[64,64]{1,0:T(8,128)S(1)} custom-call(f32[64,64]{1,0:T(8,128)S(1)} %fusion.45), custom_call_target="Cholesky" | custom-call | tf_op jit(solution)/shard_map/jit(cholesky)/cholesky | solution.py:20
  318.2 4.9 custom-call.12
  325.0 5.8 %cholesky.145 = f32[64,64]{1,0:T(8,128)S(1)} custom-call(f32[64,64]{1,0:T(8,128)S(1)} %fusion.43), custom_call_target="Cholesky" | custom-call | tf_op jit(solution)/shard_map/jit(cholesky)/cholesky | solution.py:20
  338.9 5.8 %cholesky.156 = f32[64,64]{1,0:T(8,128)S(1)} custom-call(f32[64,64]{1,0:T(8,128)S(1)} %fusion.41), custom_call_target="Cholesky" | custom-call | tf_op jit(solution)/shard_map/jit(cholesky)/cholesky | solution.py:20
  352.8 6.0 %cholesky.167 = f32[64,64]{1,0:T(8,128)S(1)} custom-call(f32[64,64]{1,0:T(8,128)S(1)} %fusion.39), custom_call_target="Cholesky" | custom-call | tf_op jit(solution)/shard_map/jit(cholesky)/cholesky | solution.py:20
  360.2 4.9 custom-call.15
  365.4 9.2 %convolution_bitcast_fusion = f32[4,64,4,512]{3,1,2,0:T(8,128)S(1)} fusion(f32[4,512,4,512]{3,1,2,0:T(8,128)} %bitcast.184, f32[64,512]{1,0:T(8,128)S(1)} %fusion.37), kind=kOutput, calls=%fused_computation.4 | convolution fusion | flops 1610612736 | bytes 19005440 | tf_op jit(solution)/shard_map/szyx,zr->sryx/dot_general | solution.py:61
  378.0 5.3 reshape.92
  383.4 35.0 %all_to_all.55 = f32[128,1,4096]{2,1,0:T(1,128)} all-to-all(f32[128,1,4096]{2,1,0:T(1,128)S(1)} %reshape.92), channel_id=1, replica_groups=mesh['gz'=16,'gy'=8] {'gz','gy'}, dimensions={0} | all-to-all | bytes 4194304 | tf_op jit(solution)/shard_map/all_to_all | solution.py:62
  418.9 7.3 %reduce.4 = f32[128,4096]{1,0:T(8,128)S(1)} reduce(f32[128,1,4096]{2,1,0:T(1,128)} %all_to_all.55, f32[]{:T(128)} %broadcast.82), dimensions={1}, to_apply=%all_to_all.42.reduce_sub_computation | reduce | bytes 4194308 | tf_op jit(solution)/shard_map/all_to_all | solution.py:62
  441.0 23.2 %all_to_all.56 = f32[128,4,512]{2,1,0:T(4,128)S(1)} all-to-all(f32[128,4,512]{2,1,0:T(4,128)S(1)} %copy.45), channel_id=1, replica_groups=mesh['gz'=16,'gy'=8] {'gz','gy'}, dimensions={0} | all-to-all | bytes 2097152 | tf_op jit(solution)/shard_map/all_to_all | solution.py:41
  464.6 23.5 %all_to_all.57 = f32[128,4,512]{2,1,0:T(4,128)S(1)} all-to-all(f32[128,4,512]{2,1,0:T(4,128)S(1)} %broadcast_in_dim.5), channel_id=1, replica_groups=mesh['gz'=16,'gy'=8] {'gz','gy'}, dimensions={0} | all-to-all | bytes 2097152 | tf_op jit(solution)/shard_map/all_to_all | solution.py:46
  490.8 5.8 %cholesky.178 = f32[64,64]{1,0:T(8,128)S(1)} custom-call(f32[64,64]{1,0:T(8,128)S(1)} %fusion.36), custom_call_target="Cholesky" | custom-call | tf_op jit(solution)/shard_map/jit(cholesky)/cholesky | solution.py:20
  504.8 5.8 %cholesky.189 = f32[64,64]{1,0:T(8,128)S(1)} custom-call(f32[64,64]{1,0:T(8,128)S(1)} %fusion.34), custom_call_target="Cholesky" | custom-call | tf_op jit(solution)/shard_map/jit(cholesky)/cholesky | solution.py:20
  518.7 5.8 %cholesky.200 = f32[64,64]{1,0:T(8,128)S(1)} custom-call(f32[64,64]{1,0:T(8,128)S(1)} %fusion.32), custom_call_target="Cholesky" | custom-call | tf_op jit(solution)/shard_map/jit(cholesky)/cholesky | solution.py:20
  532.6 6.0 %cholesky.211 = f32[64,64]{1,0:T(8,128)S(1)} custom-call(f32[64,64]{1,0:T(8,128)S(1)} %fusion.30), custom_call_target="Cholesky" | custom-call | tf_op jit(solution)/shard_map/jit(cholesky)/cholesky | solution.py:20
  540.0 4.9 custom-call.19
  (95 shorter events, 83.0 us)
Async XLA Ops:
  284.5 23.8 %all-to-all-start.2 = ((f32[128,4,512]{2,1,0:T(4,128)}), f32[128,4,512]{2,1,0:T(4,128)S(1)}, u32[]{:S(2)}, u32[]{:S(2)}) async-start(f32[128,4,512]{2,1,0:T(4,128)} %broadcast_in_dim.4), calls=%async_computation.2 | async-start | bytes 2097152 | tf_op jit(solution)/shard_map/all_to_all | solution.py:46
  365.4 9.2 %copy-start.1 = (f32[64,512]{1,0:T(8,128)}, f32[64,512]{1,0:T(8,128)S(1)}, u32[]{:S(2)}) copy-start(f32[64,512]{1,0:T(8,128)S(1)} %fusion.37) | copy-start | bytes 393220
  436.8 3.5 copy-start
  545.2 4.8 copy-start.2

commit v3 on v2

--- a/solution.py
+++ b/solution.py
@@ -3,7 +3,10 @@
 import jax
 import jax.numpy as jnp
 from jax import lax
+from jax.experimental import pallas as pl
+from jax.experimental.pallas import tpu as pltpu
 from jax.sharding import PartitionSpec as P
+import functools
 
 GRID = 512
 RANK = 64
@@ -46,13 +49,56 @@
     return lax.all_to_all(tiled, axes, 0, 0, tiled=True).reshape(rows, rows)
 
 
+def _eliminate(c):
+    n = c.shape[0]
+    row = lax.broadcasted_iota(jnp.int32, (n, n), 0)
+    lane = lax.broadcasted_iota(jnp.int32, (n, n), 1)
+    right = (row == lane).astype(jnp.float32)
+
+    def step(j, carry):
+        left, right = carry
+        at_row = row == j
+        row_l = jnp.sum(jnp.where(at_row, left, 0.0), axis=0, keepdims=True)
+        row_r = jnp.sum(jnp.where(at_row, right, 0.0), axis=0, keepdims=True)
+        col = jnp.sum(jnp.where(lane == j, left, 0.0), axis=1, keepdims=True)
+        pivot = jnp.sum(jnp.where(row[:, :1] == j, col, 0.0), axis=0, keepdims=True)
+        factor = jnp.where(row[:, :1] > j, col / pivot, 0.0)
+        left = left - factor * row_l
+        right = right - factor * row_r
+        return left, right
+
+    left, right = lax.fori_loop(0, n, step, (c, right), unroll=8)
+    diag = jnp.sum(jnp.where(row == lane, left, 0.0), axis=1, keepdims=True)
+    return right / jnp.sqrt(diag)
+
+
+def _basis_kernel(iters, g_ref, q_ref, out_ref):
+    gram = g_ref[...]
+    basis = q_ref[...]
+    for _ in range(iters):
+        product = jnp.dot(gram, basis, precision=lax.Precision.HIGHEST, preferred_element_type=jnp.float32)
+        inner = lax.dot_general(product, product, (((0,), (0,)), ((), ())),
+                                precision=lax.Precision.HIGHEST, preferred_element_type=jnp.float32)
+        inverse = _eliminate(inner)
+        basis = lax.dot_general(product, inverse, (((1,), (1,)), ((), ())),
+                                precision=lax.Precision.HIGHEST, preferred_element_type=jnp.float32)
+    out_ref[...] = basis
+
+
+def basis_pallas(gram, start, iters=4):
+    n, r = start.shape
+    return pl.pallas_call(
+        functools.partial(_basis_kernel, iters),
+        out_shape=jax.ShapeDtypeStruct((n, r), jnp.float32),
+        in_specs=[pl.BlockSpec(memory_space=pltpu.VMEM)] * 2,
+        out_specs=pl.BlockSpec(memory_space=pltpu.VMEM),
+    )(gram, start)
+
+
 def leaf_basis(fibres, mode):
     basis_now = start_table(GRID, RANK)
     gram_total = sum_over_mesh(mode_products(fibres, fibres, mode))
-    for iteration in range(ITERS):
-        product = jnp.dot(gram_total, basis_now, precision=lax.Precision.HIGHEST)
-        basis_now = solve_factor(product, inner_products(product, product))
-    return basis_now
+    return basis_pallas(gram_total, basis_now, ITERS)
 
 
 def body(species_field):

time: 554 us -> 524 us (0.946)
  other arithmetic: 105 us -> 9.37 us
  Pallas kernels: 0 us -> 77 us
  blocking collectives: 301 us -> 278 us
  waiting for transfers between devices: 18.9 us -> 36.3 us
  matrix products: 53.8 us -> 38.2 us
    another operation x40 -> x0, other arithmetic: 96.8 us -> none  [the longest x24 52.5 us: solve_factor(): factor = jnp.linalg.cholesky(inner_gram)]
    pallas_call x0 -> x2, Pallas kernels: none -> 77 us  [basis_pallas(): pl.pallas_call(functools.partial(_basis_kernel, iters), out_shape=jax.Sha...]
    all_to_all x1 -> x0, blocking collectives: 23.5 us -> none  [sum_over_mesh(): return lax.all_to_all(tiled, axes, 0, 0, tiled=True).reshape(rows, rows)]
    all_to_all x1 -> x2, waiting for transfers between devices: 18.9 us -> 36.3 us  [sum_over_mesh(): return lax.all_to_all(tiled, axes, 0, 0, tiled=True).reshape(rows, rows)]
    dot_general x16 -> x0, matrix products: 13.1 us -> none  [the longest x8 11 us: leaf_basis(): product = jnp.dot(gram_total, basis_now, precision=lax.Precision.HIGHEST)]
  transfers between devices with their start and end apart: 1 -> 2, of which waited for: 1 -> 2; matrix products, arithmetic and copies ran while one was open for 0% -> 0% of each run, Pallas kernels for 0% -> 0%
where the time goes in v3:
time: 524 us; the launch traced here: 520 us
  blocking collectives  278 us (53%)
  Pallas kernels  77 us (15%)
  local copies, waits for them, and re-layouts  70.7 us (13%)
  matrix products  38.2 us (7%)
  waiting for transfers between devices  36.3 us (7%)
  other arithmetic  9.37 us (2%)
  starting transfers between devices  9.24 us (2%)
    all_to_all x1, blocking collectives, body(): lax.all_to_all(species_field, 'gz', split_axis=2, concat_axis=1, tiled=True)  194 us
    pallas_call x2, Pallas kernels, basis_pallas(): pl.pallas_call(functools.partial(_basis_kernel, iters), out_shape=jax.Sha...  77 us
    all_to_all x2, blocking collectives, sum_over_mesh(): lax.all_to_all(gram.reshape(count, rows // count, rows), axes, 0, 0, tile...  49.4 us
    all_to_all x2, waiting for transfers between devices, sum_over_mesh(): return lax.all_to_all(tiled, axes, 0, 0, tiled=True).reshape(rows, rows)  36.3 us
    all_to_all x1, blocking collectives, body(): lax.all_to_all(reduced, ('gz', 'gy'), split_axis=3, concat_axis=2, tiled=...  35 us
    unnamed x9, local copies, waits for them, and re-layouts  27.6 us
    dot_general x2, matrix products, mode_products(): lax.dot_general(left, right, ((others, others), ((), ())), precision=lax....  25.2 us
    dot_general x3, local copies, waits for them, and re-layouts, mode_products(): lax.dot_general(left, right, ((others, others), ((), ())), precision=lax....  20.4 us
  transfers between devices with their start and end apart: 2, of which 2 were waited for; matrix products, arithmetic and copies ran while one was open for 0% of the time, Pallas kernels for 0%

profile of v3, /device:TPU:1, one launch (start us, length us, event | category | flops | bytes accessed | tf_op | source)
XLA Modules:
  0.0 519.8 jit_solution(6696529250657945198)
XLA Ops:
  0.6 15.2 %copy.24 = f32[4,32,64,512]{3,1,0,2:T(8,128)S(1)} copy(f32[4,32,64,512]{3,2,1,0:T(8,128)} %param.1) | data formatting | bytes 33554432 | tf_op args[0]
  15.9 193.6 %all_to_all.53 = f32[4,32,64,512]{3,1,0,2:T(8,128)S(1)} all-to-all(f32[4,32,64,512]{3,1,0,2:T(8,128)S(1)} %copy.24), channel_id=1, replica_groups=mesh['gz'=16,'gy'=8] {'gz'}, dimensions={2} | all-to-all | bytes 33554432 | tf_op jit(solution)/shard_map/all_to_all | solution.py:105
  209.5 6.3 %copy.25 = f32[4,32,16,4,512]{4,1,2,3,0:T(8,128)} copy(f32[4,32,16,4,512]{4,1,0,3,2:T(8,128)S(1)} %bitcast.55) | data formatting | bytes 33554432 | tf_op jit(solution)/shard_map/all_to_all | solution.py:105
  215.8 19.0 %dot_general.21 = f32[128,4,4,4,512]{4,1,0,3,2:T(4,128)} reshape(f32[512,4,4,512]{3,0,2,1:T(8,128)} %bitcast.52) | data formatting | bytes 33554432 | tf_op jit(solution)/shard_map/dot_general | solution.py:35
  234.8 21.7 %fusion.7 = f32[128,4,512]{2,0,1:T(8,128)S(1)} fusion(f32[4,512,4,512,1]{3,1,2,0,4:T(8,128)} %bitcast.53, f32[128,4,4,4,512]{4,1,0,3,2:T(4,128)} %dot_general.21), kind=kOutput, calls=%fused_computation.6 | convolution fusion | flops 12884901888 | bytes 34603008 | tf_op jit(solution)/shard_map/dot_general | solution.py:35
  257.2 26.2 %all_to_all.54 = f32[128,4,512]{2,1,0:T(4,128)S(1)} all-to-all(f32[128,4,512]{2,1,0:T(4,128)S(1)} %copy.27), channel_id=1, replica_groups=mesh['gz'=16,'gy'=8] {'gz','gy'}, dimensions={0} | all-to-all | bytes 2097152 | tf_op jit(solution)/shard_map/all_to_all | solution.py:44
  284.7 4.6 all-to-all-start.2
  291.0 17.7 %all-to-all-done.2 = f32[128,4,512]{2,1,0:T(4,128)S(1)} async-done(((f32[128,4,512]{2,1,0:T(4,128)}), f32[128,4,512]{2,1,0:T(4,128)S(1)}, u32[]{:S(2)}, u32[]{:S(2)}) %all-to-all-start.2) | async-done | bytes 1048608 | tf_op jit(solution)/shard_map/all_to_all | solution.py:49
  310.0 38.5 %shard_map.38 = f32[512,64]{1,0:T(8,128)} custom-call(f32[512,512]{1,0:T(8,128)} %reshape.40.g_ref, f32[512,64]{1,0:T(8,128)} %multiply_cosine_fusion.q_ref), custom_call_target="tpu_custom_call" | custom-call | tf_op jit(solution)/shard_map/pallas_call | solution.py:90
  348.5 9.3 %convolution_bitcast_fusion = f32[4,64,4,512]{3,1,2,0:T(8,128)S(1)} fusion(f32[4,512,4,512]{3,1,2,0:T(8,128)} %bitcast.54, f32[512,64]{1,0:T(8,128)} %shard_map.38), kind=kOutput, calls=%fused_computation.4 | convolution fusion | flops 1610612736 | bytes 19005440 | tf_op jit(solution)/shard_map/szyx,zr->sryx/dot_general | solution.py:107
  357.9 3.7 copy.29
  361.6 5.3 %reshape.51 = f32[128,1,4096]{2,1,0:T(1,128)S(1)} reshape(f32[512,4,4,64]{3,2,1,0:T(4,128)} %bitcast.59) | data formatting | bytes 4194304
  366.9 35.0 %all_to_all.55 = f32[128,1,4096]{2,1,0:T(1,128)} all-to-all(f32[128,1,4096]{2,1,0:T(1,128)S(1)} %reshape.51), channel_id=1, replica_groups=mesh['gz'=16,'gy'=8] {'gz','gy'}, dimensions={0} | all-to-all | bytes 4194304 | tf_op jit(solution)/shard_map/all_to_all | solution.py:108
  402.4 7.3 %reduce = f32[128,4096]{1,0:T(8,128)S(1)} reduce(f32[128,1,4096]{2,1,0:T(1,128)} %all_to_all.55, f32[]{:T(128)} %broadcast.28), dimensions={1}, to_apply=%all_to_all.42.reduce_sub_computation | reduce | bytes 4194308 | tf_op jit(solution)/shard_map/all_to_all | solution.py:108
  409.7 4.6 reshape.52
  414.2 3.5 copy.30
  417.8 2.7 copy.31
  420.5 3.5 fusion.4
  424.7 23.2 %all_to_all.56 = f32[128,4,512]{2,1,0:T(4,128)S(1)} all-to-all(f32[128,4,512]{2,1,0:T(4,128)S(1)} %copy.34), channel_id=1, replica_groups=mesh['gz'=16,'gy'=8] {'gz','gy'}, dimensions={0} | all-to-all | bytes 2097152 | tf_op jit(solution)/shard_map/all_to_all | solution.py:44
  449.2 4.6 all-to-all-start.5
  454.6 18.6 %all-to-all-done.5 = f32[128,4,512]{2,1,0:T(4,128)S(1)} async-done(((f32[128,4,512]{2,1,0:T(4,128)}), f32[128,4,512]{2,1,0:T(4,128)S(1)}, u32[]{:S(2)}, u32[]{:S(2)}) %all-to-all-start.5) | async-done | bytes 1048608 | tf_op jit(solution)/shard_map/all_to_all | solution.py:49
  474.5 38.5 %shard_map.39 = f32[512,64]{1,0:T(8,128)} custom-call(f32[512,512]{1,0:T(8,128)} %reshape.43.g_ref, f32[512,64]{1,0:T(8,128)} %multiply_cosine_fusion.q_ref), custom_call_target="tpu_custom_call" | custom-call | tf_op jit(solution)/shard_map/pallas_call | solution.py:90
  513.1 1.7 copy.39
  514.8 3.7 convolution_bitcast_fusion.1
  (19 shorter events, 10.8 us)
Async XLA Ops:
  284.7 24.0 %all-to-all-start.2 = ((f32[128,4,512]{2,1,0:T(4,128)}), f32[128,4,512]{2,1,0:T(4,128)S(1)}, u32[]{:S(2)}, u32[]{:S(2)}) async-start(f32[128,4,512]{2,1,0:T(4,128)} %broadcast_in_dim.4), calls=%async_computation.2 | async-start | bytes 2097152 | tf_op jit(solution)/shard_map/all_to_all | solution.py:49
  420.5 3.5 copy-start
  424.0 29.8 %copy-start.1 = (f32[512,64]{1,0:T(8,128)S(1)}, f32[512,64]{1,0:T(8,128)}, u32[]{:S(2)}) copy-start(f32[512,64]{1,0:T(8,128)} %shard_map.38) | copy-start | bytes 393220
  449.2 24.0 %all-to-all-start.5 = ((f32[128,4,512]{2,1,0:T(4,128)}), f32[128,4,512]{2,1,0:T(4,128)S(1)}, u32[]{:S(2)}, u32[]{:S(2)}) async-start(f32[128,4,512]{2,1,0:T(4,128)} %broadcast_in_dim.5), calls=%async_computation.5 | async-start | bytes 2097152 | tf_op jit(solution)/shard_map/all_to_all | solution.py:49

commit v4 on v3

--- a/solution.py
+++ b/solution.py
@@ -11,6 +11,7 @@
 GRID = 512
 RANK = 64
 ITERS = 4
+CHUNK = 1
 
 
 def start_table(order, width):
@@ -95,16 +96,31 @@
     )(gram, start)
 
 
-def leaf_basis(fibres, mode):
+def leaf_basis(gram_part):
     basis_now = start_table(GRID, RANK)
-    gram_total = sum_over_mesh(mode_products(fibres, fibres, mode))
+    gram_total = sum_over_mesh(gram_part)
     return basis_pallas(gram_total, basis_now, ITERS)
 
 
 def body(species_field):
-    fibres_z = lax.all_to_all(species_field, "gz", split_axis=2, concat_axis=1, tiled=True)
-    basis_z = leaf_basis(fibres_z, 1)
-    reduced = jnp.einsum("szyx,zr->sryx", fibres_z, basis_z, precision=lax.Precision.HIGH)
+    pieces = species_field.shape[0] // CHUNK
+    fibres = [
+        lax.all_to_all(
+            species_field[CHUNK * k : CHUNK * (k + 1)], "gz", split_axis=2, concat_axis=1, tiled=True
+        )
+        for k in range(pieces)
+    ]
+    gram_z = mode_products(fibres[0], fibres[0], 1)
+    for part in fibres[1:]:
+        gram_z = gram_z + mode_products(part, part, 1)
+    basis_z = leaf_basis(gram_z)
+    reduced = jnp.concatenate(
+        [
+            jnp.einsum("szyx,zr->sryx", part, basis_z, precision=lax.Precision.HIGH)
+            for part in fibres
+        ],
+        axis=0,
+    )
     mixed = lax.all_to_all(reduced, ("gz", "gy"), split_axis=3, concat_axis=2, tiled=True)
     count_gz = lax.axis_size("gz")
     count_gy = lax.axis_size("gy")
@@ -112,7 +128,7 @@
     y_local = shape_now[2] // (count_gz * count_gy)
     blocks = mixed.reshape(shape_now[0], shape_now[1], count_gz, count_gy, y_local, shape_now[3])
     fibres_y = jnp.transpose(blocks, (0, 1, 3, 2, 4, 5)).reshape(shape_now)
-    basis_y = leaf_basis(fibres_y, 2)
+    basis_y = leaf_basis(mode_products(fibres_y, fibres_y, 2))
     core_tensor = jnp.einsum("sryx,yq->sxrq", fibres_y, basis_y, precision=lax.Precision.HIGH)
     core_tensor = core_tensor.reshape(fibres_y.shape[0], fibres_y.shape[3], RANK * RANK)
     return (core_tensor, basis_z, basis_y)

time: 524 us -> 557 us (1.063)
  waiting for transfers between devices: 36.3 us -> 228 us
  blocking collectives: 278 us -> 88.9 us
  starting transfers between devices: 9.24 us -> 31.5 us
  local copies, waits for them, and re-layouts: 70.7 us -> 80.7 us
  matrix products: 38.2 us -> 31.7 us
    all_to_all x1 -> x0, blocking collectives: 194 us -> none  [body(): lax.all_to_all(species_field, 'gz', split_axis=2, concat_axis=1, tiled=True)]
    all_to_all x0 -> x4, waiting for transfers between devices: none -> 192 us  [body(): lax.all_to_all(species_field[CHUNK * k:CHUNK * (k + 1)], 'gz', split_axis...]
    all_to_all x0 -> x4, starting transfers between devices: none -> 22.5 us  [body(): lax.all_to_all(species_field[CHUNK * k:CHUNK * (k + 1)], 'gz', split_axis...]
    dot_general x3 -> x1, local copies, waits for them, and re-layouts: 20.4 us -> 0.68 us  [mode_products(): lax.dot_general(left, right, ((others, others), ((), ())), precision=lax....]
    slice x0 -> x1, local copies, waits for them, and re-layouts: none -> 11.4 us  [body(): species_field[CHUNK * k:CHUNK * (k + 1)]]
    unnamed x9 -> x26, local copies, waits for them, and re-layouts: 27.6 us -> 36.9 us
    all_to_all x1 -> x4, local copies, waits for them, and re-layouts: 6.26 us -> 15.3 us  [body(): lax.all_to_all(species_field[CHUNK * k:CHUNK * (k + 1)], 'gz', split_axis...]
    dot_general x2 -> x5, matrix products: 25.2 us -> 18.2 us  [mode_products(): lax.dot_general(left, right, ((others, others), ((), ())), precision=lax....]
  transfers between devices with their start and end apart: 2 -> 6, of which waited for: 2 -> 6; matrix products, arithmetic and copies ran while one was open for 0% -> 8% of each run, Pallas kernels for 0% -> 0%
where the time goes in v4:
time: 557 us; the launch traced here: 549 us
  waiting for transfers between devices  228 us (41%)
  blocking collectives  88.9 us (16%)
  local copies, waits for them, and re-layouts  80.7 us (14%)
  Pallas kernels  77.2 us (14%)
  matrix products  31.7 us (6%)
  starting transfers between devices  31.5 us (6%)
  other arithmetic  9.58 us (2%)
    all_to_all x4, waiting for transfers between devices, body(): lax.all_to_all(species_field[CHUNK * k:CHUNK * (k + 1)], 'gz', split_axis...  192 us
    pallas_call x2, Pallas kernels, basis_pallas(): pl.pallas_call(functools.partial(_basis_kernel, iters), out_shape=jax.Sha...  77.2 us
    all_to_all x2, blocking collectives, sum_over_mesh(): lax.all_to_all(gram.reshape(count, rows // count, rows), axes, 0, 0, tile...  53.7 us
    unnamed x26, local copies, waits for them, and re-layouts  36.9 us
    all_to_all x2, waiting for transfers between devices, sum_over_mesh(): return lax.all_to_all(tiled, axes, 0, 0, tiled=True).reshape(rows, rows)  36.4 us
    all_to_all x1, blocking collectives, body(): lax.all_to_all(reduced, ('gz', 'gy'), split_axis=3, concat_axis=2, tiled=...  35.2 us
    all_to_all x4, starting transfers between devices, body(): lax.all_to_all(species_field[CHUNK * k:CHUNK * (k + 1)], 'gz', split_axis...  22.5 us
    dot_general x5, matrix products, mode_products(): lax.dot_general(left, right, ((others, others), ((), ())), precision=lax....  18.2 us
  transfers between devices with their start and end apart: 6, of which 6 were waited for; matrix products, arithmetic and copies ran while one was open for 8% of the time, Pallas kernels for 0%

profile of v4, /device:TPU:1, one launch (start us, length us, event | category | flops | bytes accessed | tf_op | source)
XLA Modules:
  0.0 549.5 jit_solution(16993776917398618411)
XLA Ops:
  0.6 11.4 %fusion.13 = (f32[1,32,64,512]{3,2,1,0:T(8,128)S(1)}, f32[1,32,64,512]{3,2,1,0:T(8,128)}, f32[1,32,64,512]{3,2,1,0:T(8,128)}, f32[1,32,64,512]{3,2,1,0:T(8,128)}) fusion(f32[4,32,64,512]{3,2,1,0:T(8,128)} %param.1), kind=kLoop, calls=%fused_computation.24 | loop fusion | bytes 33554432 | tf_op jit(solution)/shard_map/slice | solution.py:109
  16.4 8.6 %all-to-all-start = ((f32[1,32,64,512]{3,1,0,2:T(8,128)}), f32[1,32,64,512]{3,1,0,2:T(8,128)}, u32[]{:S(2)}, u32[]{:S(2)}) async-start(f32[1,32,64,512]{3,1,0,2:T(8,128)} %copy.71), calls=%async_computation | async-start | bytes 8388608 | tf_op jit(solution)/shard_map/all_to_all | solution.py:108
  25.0 6.6 %copy.73 = f32[1,32,64,512]{3,1,0,2:T(8,128)} copy(f32[1,32,64,512]{3,2,1,0:T(8,128)} %get-tuple-element.13) | data formatting | bytes 8388608
  31.6 55.8 %all-to-all-done = f32[1,32,64,512]{3,1,0,2:T(8,128)} async-done(((f32[1,32,64,512]{3,1,0,2:T(8,128)}), f32[1,32,64,512]{3,1,0,2:T(8,128)}, u32[]{:S(2)}, u32[]{:S(2)}) %all-to-all-start) | async-done | bytes 4194336 | tf_op jit(solution)/shard_map/all_to_all | solution.py:108
  87.4 4.6 all-to-all-start.2
  92.0 6.6 %copy.72 = f32[1,32,64,512]{3,1,0,2:T(8,128)} copy(f32[1,32,64,512]{3,2,1,0:T(8,128)} %get-tuple-element.14) | data formatting | bytes 8388608
  98.6 52.9 %all-to-all-done.2 = f32[1,32,64,512]{3,1,0,2:T(8,128)} async-done(((f32[1,32,64,512]{3,1,0,2:T(8,128)}), f32[1,32,64,512]{3,1,0,2:T(8,128)}, u32[]{:S(2)}, u32[]{:S(2)}) %all-to-all-start.2) | async-done | bytes 4194336 | tf_op jit(solution)/shard_map/all_to_all | solution.py:108
  151.5 4.7 all-to-all-start.1
  156.2 6.5 %copy.74 = f32[1,32,64,512]{3,1,0,2:T(8,128)} copy(f32[1,32,64,512]{3,2,1,0:T(8,128)} %get-tuple-element.15) | data formatting | bytes 8388608
  162.8 50.0 %all-to-all-done.1 = f32[1,32,64,512]{3,1,0,2:T(8,128)} async-done(((f32[1,32,64,512]{3,1,0,2:T(8,128)}), f32[1,32,64,512]{3,1,0,2:T(8,128)}, u32[]{:S(2)}, u32[]{:S(2)}) %all-to-all-start.1) | async-done | bytes 4194336 | tf_op jit(solution)/shard_map/all_to_all | solution.py:108
  212.8 4.5 all-to-all-start.3
  217.3 4.9 copy.35
  225.3 4.5 copy.37
  236.7 33.2 %all-to-all-done.3 = f32[1,32,64,512]{3,1,0,2:T(8,128)} async-done(((f32[1,32,64,512]{3,1,0,2:T(8,128)}), f32[1,32,64,512]{3,1,0,2:T(8,128)}, u32[]{:S(2)}, u32[]{:S(2)}) %all-to-all-start.3) | async-done | bytes 4194336 | tf_op jit(solution)/shard_map/all_to_all | solution.py:108
  281.5 30.5 %all_to_all.95 = f32[128,4,512]{2,1,0:T(4,128)S(1)} all-to-all(f32[128,4,512]{2,1,0:T(4,128)S(1)} %reshape.85), channel_id=1, replica_groups=mesh['gz'=16,'gy'=8] {'gz','gy'}, dimensions={0} | all-to-all | bytes 2097152 | tf_op jit(solution)/shard_map/all_to_all | solution.py:45
  319.4 17.8 %all-to-all-done.5 = f32[128,4,512]{2,1,0:T(4,128)S(1)} async-done(((f32[128,4,512]{2,1,0:T(4,128)}), f32[128,4,512]{2,1,0:T(4,128)S(1)}, u32[]{:S(2)}, u32[]{:S(2)}) %all-to-all-start.5) | async-done | bytes 1048608 | tf_op jit(solution)/shard_map/all_to_all | solution.py:50
  338.5 38.7 %shard_map.38 = f32[512,64]{1,0:T(8,128)} custom-call(f32[512,512]{1,0:T(8,128)} %reshape.86.g_ref, f32[512,64]{1,0:T(8,128)} %multiply_cosine_fusion.q_ref), custom_call_target="tpu_custom_call" | custom-call | tf_op jit(solution)/shard_map/pallas_call | solution.py:91
  390.7 5.3 reshape.102
  396.0 35.2 %all_to_all.96 = f32[128,1,4096]{2,1,0:T(1,128)} all-to-all(f32[128,1,4096]{2,1,0:T(1,128)S(1)} %reshape.102), channel_id=1, replica_groups=mesh['gz'=16,'gy'=8] {'gz','gy'}, dimensions={0} | all-to-all | bytes 4194304 | tf_op jit(solution)/shard_map/all_to_all | solution.py:124
  431.7 7.3 %reduce = f32[128,4096]{1,0:T(8,128)S(1)} reduce(f32[128,1,4096]{2,1,0:T(1,128)} %all_to_all.96, f32[]{:T(128)} %broadcast.28), dimensions={1}, to_apply=%all_to_all.81.reduce_sub_computation | reduce | bytes 4194308 | tf_op jit(solution)/shard_map/all_to_all | solution.py:124
  453.9 23.2 %all_to_all.97 = f32[128,4,512]{2,1,0:T(4,128)S(1)} all-to-all(f32[128,4,512]{2,1,0:T(4,128)S(1)} %copy.51), channel_id=1, replica_groups=mesh['gz'=16,'gy'=8] {'gz','gy'}, dimensions={0} | all-to-all | bytes 2097152 | tf_op jit(solution)/shard_map/all_to_all | solution.py:45
  478.5 4.7 all-to-all-start.8
  484.0 18.6 %all-to-all-done.8 = f32[128,4,512]{2,1,0:T(4,128)S(1)} async-done(((f32[128,4,512]{2,1,0:T(4,128)}), f32[128,4,512]{2,1,0:T(4,128)S(1)}, u32[]{:S(2)}, u32[]{:S(2)}) %all-to-all-start.8) | async-done | bytes 1048608 | tf_op jit(solution)/shard_map/all_to_all | solution.py:50
  503.9 38.5 %shard_map.39 = f32[512,64]{1,0:T(8,128)} custom-call(f32[512,512]{1,0:T(8,128)} %reshape.89.g_ref, f32[512,64]{1,0:T(8,128)} %multiply_cosine_fusion.q_ref), custom_call_target="tpu_custom_call" | custom-call | tf_op jit(solution)/shard_map/pallas_call | solution.py:91
  (53 shorter events, 73.2 us)
Async XLA Ops:
  16.4 71.0 %all-to-all-start = ((f32[1,32,64,512]{3,1,0,2:T(8,128)}), f32[1,32,64,512]{3,1,0,2:T(8,128)}, u32[]{:S(2)}, u32[]{:S(2)}) async-start(f32[1,32,64,512]{3,1,0,2:T(8,128)} %copy.71), calls=%async_computation | async-start | bytes 8388608 | tf_op jit(solution)/shard_map/all_to_all | solution.py:108
  87.4 64.1 %all-to-all-start.2 = ((f32[1,32,64,512]{3,1,0,2:T(8,128)}), f32[1,32,64,512]{3,1,0,2:T(8,128)}, u32[]{:S(2)}, u32[]{:S(2)}) async-start(f32[1,32,64,512]{3,1,0,2:T(8,128)} %copy.73), calls=%async_computation.2 | async-start | bytes 8388608 | tf_op jit(solution)/shard_map/all_to_all | solution.py:108
  151.5 61.3 %all-to-all-start.1 = ((f32[1,32,64,512]{3,1,0,2:T(8,128)}), f32[1,32,64,512]{3,1,0,2:T(8,128)}, u32[]{:S(2)}, u32[]{:S(2)}) async-start(f32[1,32,64,512]{3,1,0,2:T(8,128)} %copy.72), calls=%async_computation.1 | async-start | bytes 8388608 | tf_op jit(solution)/shard_map/all_to_all | solution.py:108
  212.8 57.2 %all-to-all-start.3 = ((f32[1,32,64,512]{3,1,0,2:T(8,128)}), f32[1,32,64,512]{3,1,0,2:T(8,128)}, u32[]{:S(2)}, u32[]{:S(2)}) async-start(f32[1,32,64,512]{3,1,0,2:T(8,128)} %copy.74), calls=%async_computation.3 | async-start | bytes 8388608 | tf_op jit(solution)/shard_map/all_to_all | solution.py:108
  225.2 4.5 copy-start
  229.8 3.5 copy-start.2
  270.0 3.4 copy-start.5
  272.9 4.7 copy-start.3
  313.4 23.8 %all-to-all-start.5 = ((f32[128,4,512]{2,1,0:T(4,128)}), f32[128,4,512]{2,1,0:T(4,128)S(1)}, u32[]{:S(2)}, u32[]{:S(2)}) async-start(f32[128,4,512]{2,1,0:T(4,128)} %broadcast_in_dim.4), calls=%async_computation.5 | async-start | bytes 2097152 | tf_op jit(solution)/shard_map/all_to_all | solution.py:50
  377.2 3.9 copy-start.1
  377.2 6.6 %copy-start.4 = (f32[1,32,16,4,512]{4,1,2,3,0:T(8,128)S(1)}, f32[1,32,16,4,512]{4,1,2,3,0:T(8,128)}, u32[]{:S(2)}) copy-start(f32[1,32,16,4,512]{4,1,2,3,0:T(8,128)} %copy-done.3) | copy-start | bytes 12582916
  377.2 6.6 %copy-start.8 = (f32[512,64]{1,0:T(8,128)S(1)}, f32[512,64]{1,0:T(8,128)}, u32[]{:S(2)}) copy-start(f32[512,64]{1,0:T(8,128)} %shard_map.38) | copy-start | bytes 393220
  381.0 4.4 copy-start.6
  449.7 3.5 copy-start.7
  478.5 24.1 %all-to-all-start.8 = ((f32[128,4,512]{2,1,0:T(4,128)}), f32[128,4,512]{2,1,0:T(4,128)S(1)}, u32[]{:S(2)}, u32[]{:S(2)}) async-start(f32[128,4,512]{2,1,0:T(4,128)} %broadcast_in_dim.5), calls=%async_computation.8 | async-start | bytes 2097152 | tf_op jit(solution)/shard_map/all_to_all | solution.py:50

commit v5 on v4

--- a/solution.py
+++ b/solution.py
@@ -11,7 +11,7 @@
 GRID = 512
 RANK = 64
 ITERS = 4
-CHUNK = 1
+CHUNK = 4
 
 
 def start_table(order, width):
@@ -110,9 +110,11 @@
         )
         for k in range(pieces)
     ]
-    gram_z = mode_products(fibres[0], fibres[0], 1)
-    for part in fibres[1:]:
-        gram_z = gram_z + mode_products(part, part, 1)
+    gram_z = None
+    for part in fibres:
+        for one in range(part.shape[0]):
+            term = mode_products(part[one : one + 1], part[one : one + 1], 1)
+            gram_z = term if gram_z is None else gram_z + term
     basis_z = leaf_basis(gram_z)
     reduced = jnp.concatenate(
         [

time: 557 us -> 508 us (0.912)
  waiting for transfers between devices: 228 us -> 36.4 us
  blocking collectives: 88.9 us -> 277 us
  local copies, waits for them, and re-layouts: 80.7 us -> 56.5 us
  starting transfers between devices: 31.5 us -> 9.4 us
    all_to_all x0 -> x1, blocking collectives: none -> 193 us  [body(): lax.all_to_all(species_field[CHUNK * k:CHUNK * (k + 1)], 'gz', split_axis...]
    all_to_all x4 -> x0, waiting for transfers between devices: 192 us -> none  [body(): lax.all_to_all(species_field[CHUNK * k:CHUNK * (k + 1)], 'gz', split_axis...]
    all_to_all x4 -> x0, starting transfers between devices: 22.5 us -> none  [body(): lax.all_to_all(species_field[CHUNK * k:CHUNK * (k + 1)], 'gz', split_axis...]
    all_to_all x4 -> x1, local copies, waits for them, and re-layouts: 15.3 us -> 1.88 us  [body(): lax.all_to_all(species_field[CHUNK * k:CHUNK * (k + 1)], 'gz', split_axis...]
    slice x1, local copies, waits for them, and re-layouts: 11.4 us -> 5.4 us  [body(): term = mode_products(part[one:one + 1], part[one:one + 1], 1)]
    unnamed x26 -> x15, local copies, waits for them, and re-layouts: 36.9 us -> 31.9 us
  transfers between devices with their start and end apart: 6 -> 2, of which waited for: 6 -> 2; matrix products, arithmetic and copies ran while one was open for 8% -> 0% of each run, Pallas kernels for 0% -> 0%
where the time goes in v5:
time: 508 us; the launch traced here: 502 us
  blocking collectives  277 us (55%)
  Pallas kernels  77 us (15%)
  local copies, waits for them, and re-layouts  56.5 us (11%)
  waiting for transfers between devices  36.4 us (7%)
  matrix products  34.8 us (7%)
  starting transfers between devices  9.4 us (2%)
  other arithmetic  9.37 us (2%)
    all_to_all x1, blocking collectives, body(): lax.all_to_all(species_field[CHUNK * k:CHUNK * (k + 1)], 'gz', split_axis...  193 us
    pallas_call x2, Pallas kernels, basis_pallas(): pl.pallas_call(functools.partial(_basis_kernel, iters), out_shape=jax.Sha...  77 us
    all_to_all x2, blocking collectives, sum_over_mesh(): lax.all_to_all(gram.reshape(count, rows // count, rows), axes, 0, 0, tile...  49.4 us
    all_to_all x2, waiting for transfers between devices, sum_over_mesh(): return lax.all_to_all(tiled, axes, 0, 0, tiled=True).reshape(rows, rows)  36.4 us
    all_to_all x1, blocking collectives, body(): lax.all_to_all(reduced, ('gz', 'gy'), split_axis=3, concat_axis=2, tiled=...  35 us
    unnamed x15, local copies, waits for them, and re-layouts  31.9 us
    dot_general x5, matrix products, mode_products(): lax.dot_general(left, right, ((others, others), ((), ())), precision=lax....  21.7 us
  transfers between devices with their start and end apart: 2, of which 2 were waited for; matrix products, arithmetic and copies ran while one was open for 0% of the time, Pallas kernels for 0%

profile of v5, /device:TPU:1, one launch (start us, length us, event | category | flops | bytes accessed | tf_op | source)
XLA Modules:
  0.0 502.3 jit_solution(16411443857960607758)
XLA Ops:
  0.6 15.2 %copy.22 = f32[4,32,64,512]{3,1,0,2:T(8,128)S(1)} copy(f32[4,32,64,512]{3,2,1,0:T(8,128)} %param.1) | data formatting | bytes 33554432 | tf_op args[0]
  15.9 193.1 %all_to_all.53 = f32[4,32,64,512]{3,1,0,2:T(8,128)S(1)} all-to-all(f32[4,32,64,512]{3,1,0,2:T(8,128)S(1)} %copy.22), channel_id=1, replica_groups=mesh['gz'=16,'gy'=8] {'gz'}, dimensions={2} | all-to-all | bytes 33554432 | tf_op jit(solution)/shard_map/all_to_all | solution.py:108
  210.8 5.4 %fusion.10 = (f32[1,16,32,4,512]{4,2,1,3,0:T(8,128)S(1)}, f32[1,16,32,4,512]{4,2,1,3,0:T(8,128)}, f32[1,16,32,4,512]{4,2,1,3,0:T(8,128)}, f32[1,16,32,4,512]{4,2,1,3,0:T(8,128)}) fusion(f32[4,16,32,4,512]{4,2,1,3,0:T(8,128)S(1)} %bitcast.67), kind=kLoop, calls=%fused_computation.18 | loop fusion | bytes 33554432 | tf_op jit(solution)/shard_map/slice | solution.py:116
  216.2 4.4 copy-done
  220.7 7.4 %convolution_bitcast_fusion.2 = f32[512,512]{1,0:T(8,128)S(1)} fusion(f32[512,4,512]{2,0,1:T(8,128)} %bitcast.76), kind=kOutput, calls=%fused_computation.5 | convolution fusion | flops 3221225472 | bytes 5242880 | tf_op jit(solution)/shard_map/dot_general | solution.py:36
  228.1 3.6 convolution_bitcast_fusion.3
  231.7 3.6 fusion.6
  235.3 3.6 fusion.7
  239.3 26.2 %all_to_all.54 = f32[128,4,512]{2,1,0:T(4,128)S(1)} all-to-all(f32[128,4,512]{2,1,0:T(4,128)S(1)} %reshape.73), channel_id=1, replica_groups=mesh['gz'=16,'gy'=8] {'gz','gy'}, dimensions={0} | all-to-all | bytes 2097152 | tf_op jit(solution)/shard_map/all_to_all | solution.py:45
  266.8 4.7 all-to-all-start.2
  273.2 17.8 %all-to-all-done.2 = f32[128,4,512]{2,1,0:T(4,128)S(1)} async-done(((f32[128,4,512]{2,1,0:T(4,128)}), f32[128,4,512]{2,1,0:T(4,128)S(1)}, u32[]{:S(2)}, u32[]{:S(2)}) %all-to-all-start.2) | async-done | bytes 1048608 | tf_op jit(solution)/shard_map/all_to_all | solution.py:50
  292.4 38.5 %shard_map.38 = f32[512,64]{1,0:T(8,128)} custom-call(f32[512,512]{1,0:T(8,128)} %reshape.74.g_ref, f32[512,64]{1,0:T(8,128)} %multiply_cosine_fusion.q_ref), custom_call_target="tpu_custom_call" | custom-call | tf_op jit(solution)/shard_map/pallas_call | solution.py:91
  330.9 9.3 %convolution_bitcast_fusion = f32[4,64,4,512]{3,1,2,0:T(8,128)S(1)} fusion(f32[4,512,4,512]{3,1,2,0:T(8,128)} %bitcast.68, f32[512,64]{1,0:T(8,128)} %shard_map.38), kind=kOutput, calls=%fused_computation.2 | convolution fusion | flops 1610612736 | bytes 19005440 | tf_op jit(solution)/shard_map/szyx,zr->sryx/dot_general | solution.py:121
  340.3 3.6 copy.25
  343.9 5.3 %reshape.87 = f32[128,1,4096]{2,1,0:T(1,128)S(1)} reshape(f32[512,4,4,64]{3,2,1,0:T(4,128)} %bitcast.77) | data formatting | bytes 4194304
  349.2 35.0 %all_to_all.55 = f32[128,1,4096]{2,1,0:T(1,128)} all-to-all(f32[128,1,4096]{2,1,0:T(1,128)S(1)} %reshape.87), channel_id=1, replica_groups=mesh['gz'=16,'gy'=8] {'gz','gy'}, dimensions={0} | all-to-all | bytes 4194304 | tf_op jit(solution)/shard_map/all_to_all | solution.py:126
  384.7 7.3 %reduce = f32[128,4096]{1,0:T(8,128)S(1)} reduce(f32[128,1,4096]{2,1,0:T(1,128)} %all_to_all.55, f32[]{:T(128)} %broadcast.28), dimensions={1}, to_apply=%all_to_all.42.reduce_sub_computation | reduce | bytes 4194308 | tf_op jit(solution)/shard_map/all_to_all | solution.py:126
  392.0 4.4 reshape.88
  396.4 3.5 copy.26
  406.8 23.2 %all_to_all.56 = f32[128,4,512]{2,1,0:T(4,128)S(1)} all-to-all(f32[128,4,512]{2,1,0:T(4,128)S(1)} %copy.30), channel_id=1, replica_groups=mesh['gz'=16,'gy'=8] {'gz','gy'}, dimensions={0} | all-to-all | bytes 2097152 | tf_op jit(solution)/shard_map/all_to_all | solution.py:45
  431.4 4.7 all-to-all-start.5
  436.8 18.6 %all-to-all-done.5 = f32[128,4,512]{2,1,0:T(4,128)S(1)} async-done(((f32[128,4,512]{2,1,0:T(4,128)}), f32[128,4,512]{2,1,0:T(4,128)S(1)}, u32[]{:S(2)}, u32[]{:S(2)}) %all-to-all-start.5) | async-done | bytes 1048608 | tf_op jit(solution)/shard_map/all_to_all | solution.py:50
  456.7 38.5 %shard_map.39 = f32[512,64]{1,0:T(8,128)} custom-call(f32[512,512]{1,0:T(8,128)} %reshape.77.g_ref, f32[512,64]{1,0:T(8,128)} %multiply_cosine_fusion.q_ref), custom_call_target="tpu_custom_call" | custom-call | tf_op jit(solution)/shard_map/pallas_call | solution.py:91
  497.0 3.7 convolution_bitcast_fusion.5
  (28 shorter events, 20.1 us)
Async XLA Ops:
  210.8 9.8 %copy-start = (f32[4,32,16,4,512]{4,1,2,3,0:T(8,128)}, f32[4,32,16,4,512]{4,1,2,3,0:T(8,128)S(1)}, u32[]{:S(2)}) copy-start(f32[4,32,16,4,512]{4,1,2,3,0:T(8,128)S(1)} %copy.50) | copy-start | bytes 50331652
  220.6 7.4 %copy-start.3 = (f32[1,16,32,4,512]{4,2,1,3,0:T(8,128)S(1)}, f32[1,16,32,4,512]{4,2,1,3,0:T(8,128)}, u32[]{:S(2)}) copy-start(f32[1,16,32,4,512]{4,2,1,3,0:T(8,128)} %get-tuple-element.14) | copy-start | bytes 12582916
  228.1 3.6 copy-start.2
  266.8 24.2 %all-to-all-start.2 = ((f32[128,4,512]{2,1,0:T(4,128)}), f32[128,4,512]{2,1,0:T(4,128)S(1)}, u32[]{:S(2)}, u32[]{:S(2)}) async-start(f32[128,4,512]{2,1,0:T(4,128)} %broadcast_in_dim.4), calls=%async_computation.2 | async-start | bytes 2097152 | tf_op jit(solution)/shard_map/all_to_all | solution.py:50
  402.6 3.5 copy-start.1
  406.2 29.9 %copy-start.4 = (f32[512,64]{1,0:T(8,128)S(1)}, f32[512,64]{1,0:T(8,128)}, u32[]{:S(2)}) copy-start(f32[512,64]{1,0:T(8,128)} %shard_map.38) | copy-start | bytes 393220
  431.4 24.1 %all-to-all-start.5 = ((f32[128,4,512]{2,1,0:T(4,128)}), f32[128,4,512]{2,1,0:T(4,128)S(1)}, u32[]{:S(2)}, u32[]{:S(2)}) async-start(f32[128,4,512]{2,1,0:T(4,128)} %broadcast_in_dim.5), calls=%async_computation.5 | async-start | bytes 2097152 | tf_op jit(solution)/shard_map/all_to_all | solution.py:50

commit v6 on v3

--- a/solution.py
+++ b/solution.py
@@ -95,26 +95,42 @@
     )(gram, start)
 
 
-def leaf_basis(fibres, mode):
-    basis_now = start_table(GRID, RANK)
-    gram_total = sum_over_mesh(mode_products(fibres, fibres, mode))
+def leaf_basis(gram_part, basis_now):
+    gram_total = sum_over_mesh(gram_part)
     return basis_pallas(gram_total, basis_now, ITERS)
 
 
 def body(species_field):
-    fibres_z = lax.all_to_all(species_field, "gz", split_axis=2, concat_axis=1, tiled=True)
-    basis_z = leaf_basis(fibres_z, 1)
-    reduced = jnp.einsum("szyx,zr->sryx", fibres_z, basis_z, precision=lax.Precision.HIGH)
-    mixed = lax.all_to_all(reduced, ("gz", "gy"), split_axis=3, concat_axis=2, tiled=True)
     count_gz = lax.axis_size("gz")
     count_gy = lax.axis_size("gy")
-    shape_now = mixed.shape
-    y_local = shape_now[2] // (count_gz * count_gy)
-    blocks = mixed.reshape(shape_now[0], shape_now[1], count_gz, count_gy, y_local, shape_now[3])
-    fibres_y = jnp.transpose(blocks, (0, 1, 3, 2, 4, 5)).reshape(shape_now)
-    basis_y = leaf_basis(fibres_y, 2)
-    core_tensor = jnp.einsum("sryx,yq->sxrq", fibres_y, basis_y, precision=lax.Precision.HIGH)
-    core_tensor = core_tensor.reshape(fibres_y.shape[0], fibres_y.shape[3], RANK * RANK)
+    count = count_gz * count_gy
+    fibres = lax.all_to_all(species_field, "gz", split_axis=2, concat_axis=1, tiled=True)
+    species, _, y_local, x_size = fibres.shape
+    gram_z = None
+    for one in range(species):
+        term = mode_products(fibres[one : one + 1], fibres[one : one + 1], 1)
+        gram_z = term if gram_z is None else gram_z + term
+    basis_z = leaf_basis(gram_z, start_table(GRID, RANK))
+    reduced = jnp.einsum("szyx,zr->xysr", fibres, basis_z, precision=lax.Precision.HIGH)
+    x_part = x_size // count
+    send = reduced.reshape(count, x_part, y_local, species, RANK)
+    send = jnp.transpose(send, (0, 2, 1, 3, 4)).reshape(count, -1)
+    mixed = lax.all_to_all(send, ("gz", "gy"), 0, 0, tiled=True)
+    fibres_y = mixed.reshape(count, y_local, -1)
+    fibres_y = jnp.transpose(fibres_y, (1, 0, 2)).reshape(count * y_local, -1)
+    gram_y = lax.dot_general(
+        fibres_y, fibres_y, (((1,), (1,)), ((), ())), precision=lax.Precision.HIGH
+    )
+    start_y = start_table(GRID, RANK).reshape(count_gy, count_gz, y_local, RANK)
+    start_y = jnp.transpose(start_y, (2, 1, 0, 3)).reshape(GRID, RANK)
+    basis_perm = leaf_basis(gram_y, start_y)
+    core_rows = lax.dot_general(
+        fibres_y, basis_perm, (((0,), (0,)), ((), ())), precision=lax.Precision.HIGH
+    )
+    core_tensor = core_rows.reshape(x_part, species, RANK, RANK)
+    core_tensor = jnp.transpose(core_tensor, (1, 0, 2, 3)).reshape(species, x_part, RANK * RANK)
+    basis_y = basis_perm.reshape(y_local, count_gz, count_gy, RANK)
+    basis_y = jnp.transpose(basis_y, (2, 1, 0, 3)).reshape(GRID, RANK)
     return (core_tensor, basis_z, basis_y)
 
 

time: 524 us -> 497 us (0.948)
  local copies, waits for them, and re-layouts: 70.7 us -> 55.8 us
  other arithmetic: 9.37 us -> 3.01 us
    dot_general x3, local copies, waits for them, and re-layouts: 20.4 us -> 4.23 us  [the longest x2 2.36 us: body(): lax.dot_general(fibres_y, fibres_y, (((1,), (1,)), ((), ())), precision=l...]
    all_to_all x1 -> x0, other arithmetic: 7.31 us -> none  [body(): lax.all_to_all(reduced, ('gz', 'gy'), split_axis=3, concat_axis=2, tiled=...]
    dot_general x2 -> x4, matrix products: 25.2 us -> 18.2 us  [mode_products(): lax.dot_general(left, right, ((others, others), ((), ())), precision=lax....]
    unnamed x9 -> x16, local copies, waits for them, and re-layouts: 27.6 us -> 22.1 us
    slice x0 -> x1, local copies, waits for them, and re-layouts: none -> 5.43 us  [body(): term = mode_products(fibres[one:one + 1], fibres[one:one + 1], 1)]
    dot_general x2 -> x3, matrix products: 13.1 us -> 15.6 us  [the longest x1 9.29 us: body(): jnp.einsum('szyx,zr->xysr', fibres, basis_z, precision=lax.Precision.HIGH)]
  transfers between devices with their start and end apart: 2 -> 2, of which waited for: 2 -> 2; matrix products, arithmetic and copies ran while one was open for 0% -> 1% of each run, Pallas kernels for 0% -> 0%
where the time goes in v6:
time: 497 us; the launch traced here: 491 us
  blocking collectives  278 us (56%)
  Pallas kernels  77 us (15%)
  local copies, waits for them, and re-layouts  55.8 us (11%)
  matrix products  33.8 us (7%)
  waiting for transfers between devices  33.5 us (7%)
  starting transfers between devices  9.12 us (2%)
    all_to_all x1, blocking collectives, body(): lax.all_to_all(species_field, 'gz', split_axis=2, concat_axis=1, tiled=True)  193 us
    pallas_call x2, Pallas kernels, basis_pallas(): pl.pallas_call(functools.partial(_basis_kernel, iters), out_shape=jax.Sha...  77 us
    all_to_all x2, blocking collectives, sum_over_mesh(): lax.all_to_all(gram.reshape(count, rows // count, rows), axes, 0, 0, tile...  49.4 us
    all_to_all x1, blocking collectives, body(): mixed = lax.all_to_all(send, ('gz', 'gy'), 0, 0, tiled=True)  35.2 us
    all_to_all x2, waiting for transfers between devices, sum_over_mesh(): return lax.all_to_all(tiled, axes, 0, 0, tiled=True).reshape(rows, rows)  33.5 us
    unnamed x16, local copies, waits for them, and re-layouts  22.1 us
    dot_general x4, matrix products, mode_products(): lax.dot_general(left, right, ((others, others), ((), ())), precision=lax....  18.2 us
  transfers between devices with their start and end apart: 2, of which 2 were waited for; matrix products, arithmetic and copies ran while one was open for 1% of the time, Pallas kernels for 0%

profile of v6, /device:TPU:1, one launch (start us, length us, event | category | flops | bytes accessed | tf_op | source)
XLA Modules:
  0.0 491.0 jit_solution(7651652787390450238)
XLA Ops:
  0.6 15.2 %copy.24 = f32[4,32,64,512]{3,1,0,2:T(8,128)S(1)} copy(f32[4,32,64,512]{3,2,1,0:T(8,128)} %param.1) | data formatting | bytes 33554432 | tf_op args[0]
  15.9 193.1 %all_to_all.47 = f32[4,32,64,512]{3,1,0,2:T(8,128)S(1)} all-to-all(f32[4,32,64,512]{3,1,0,2:T(8,128)S(1)} %copy.24), channel_id=1, replica_groups=mesh['gz'=16,'gy'=8] {'gz'}, dimensions={2} | all-to-all | bytes 33554432 | tf_op jit(solution)/shard_map/all_to_all | solution.py:107
  210.8 5.4 %fusion.7 = (f32[1,16,32,4,512]{4,2,1,3,0:T(8,128)S(1)}, f32[1,16,32,4,512]{4,2,1,3,0:T(8,128)}, f32[1,16,32,4,512]{4,2,1,3,0:T(8,128)}, f32[1,16,32,4,512]{4,2,1,3,0:T(8,128)}) fusion(f32[4,16,32,4,512]{4,2,1,3,0:T(8,128)S(1)} %bitcast.66), kind=kLoop, calls=%fused_computation.19 | loop fusion | bytes 33554432 | tf_op jit(solution)/shard_map/slice | solution.py:111
  216.3 4.4 copy-done
  220.7 7.4 %convolution_bitcast_fusion.2 = f32[512,512]{1,0:T(8,128)S(1)} fusion(f32[512,4,512]{2,0,1:T(8,128)} %bitcast.72), kind=kOutput, calls=%fused_computation.4 | convolution fusion | flops 3221225472 | bytes 5242880 | tf_op jit(solution)/shard_map/dot_general | solution.py:35
  228.0 3.6 convolution_bitcast_fusion.3
  231.7 3.6 fusion.3
  235.3 3.6 fusion.4
  239.2 26.2 %all_to_all.48 = f32[128,4,512]{2,1,0:T(4,128)S(1)} all-to-all(f32[128,4,512]{2,1,0:T(4,128)S(1)} %reshape.113), channel_id=1, replica_groups=mesh['gz'=16,'gy'=8] {'gz','gy'}, dimensions={0} | all-to-all | bytes 2097152 | tf_op jit(solution)/shard_map/all_to_all | solution.py:44
  266.8 4.5 all-to-all-start.2
  271.4 2.6 multiply_cosine_fusion
  274.0 16.8 %all-to-all-done.2 = f32[128,4,512]{2,1,0:T(4,128)S(1)} async-done(((f32[128,4,512]{2,1,0:T(4,128)}), f32[128,4,512]{2,1,0:T(4,128)S(1)}, u32[]{:S(2)}, u32[]{:S(2)}) %all-to-all-start.2) | async-done | bytes 1048608 | tf_op jit(solution)/shard_map/all_to_all | solution.py:49
  292.1 38.5 %shard_map.38 = f32[512,64]{1,0:T(8,128)} custom-call(f32[512,512]{1,0:T(8,128)} %reshape.114.g_ref, f32[512,64]{1,0:T(8,128)} %get-tuple-element.19.q_ref), custom_call_target="tpu_custom_call" | custom-call | tf_op jit(solution)/shard_map/pallas_call | solution.py:90
  330.7 9.3 %convolution_bitcast_fusion = f32[512,4,4,64]{0,3,1,2:T(8,128)S(1)} fusion(f32[4,512,4,512]{3,1,2,0:T(8,128)} %bitcast.67, f32[512,64]{1,0:T(8,128)} %shard_map.38), kind=kOutput, calls=%fused_computation.2 | convolution fusion | flops 1610612736 | bytes 19005440 | tf_op jit(solution)/shard_map/szyx,zr->xysr/dot_general | solution.py:114
  339.9 3.1 copy.27
  343.1 3.5 copy.28
  346.6 4.1 copy.29
  350.7 35.2 %all_to_all.49 = f32[128,1,4096]{2,1,0:T(1,128)S(1)} all-to-all(f32[128,1,4096]{2,1,0:T(1,128)} %copy.29), channel_id=1, replica_groups=mesh['gz'=16,'gy'=8] {'gz','gy'}, dimensions={0} | all-to-all | bytes 4194304 | tf_op jit(solution)/shard_map/all_to_all | solution.py:118
  385.9 3.8 copy.30
  393.3 4.3 fusion
  398.4 23.2 %all_to_all.50 = f32[128,4,512]{2,1,0:T(4,128)S(1)} all-to-all(f32[128,4,512]{2,1,0:T(4,128)S(1)} %copy.35), channel_id=1, replica_groups=mesh['gz'=16,'gy'=8] {'gz','gy'}, dimensions={0} | all-to-all | bytes 2097152 | tf_op jit(solution)/shard_map/all_to_all | solution.py:44
  422.9 4.6 all-to-all-start.5
  430.2 16.7 %all-to-all-done.5 = f32[128,4,512]{2,1,0:T(4,128)S(1)} async-done(((f32[128,4,512]{2,1,0:T(4,128)}), f32[128,4,512]{2,1,0:T(4,128)S(1)}, u32[]{:S(2)}, u32[]{:S(2)}) %all-to-all-start.5) | async-done | bytes 1048608 | tf_op jit(solution)/shard_map/all_to_all | solution.py:49
  448.3 38.5 %shard_map.39 = f32[512,64]{1,0:T(8,128)} custom-call(f32[512,512]{1,0:T(8,128)} %reshape.118.g_ref, f32[512,64]{1,0:T(8,128)} %get-tuple-element.18.q_ref), custom_call_target="tpu_custom_call" | custom-call | tf_op jit(solution)/shard_map/pallas_call | solution.py:90
  (33 shorter events, 18.7 us)
Async XLA Ops:
  210.8 9.8 %copy-start = (f32[4,32,16,4,512]{4,1,2,3,0:T(8,128)}, f32[4,32,16,4,512]{4,1,2,3,0:T(8,128)S(1)}, u32[]{:S(2)}) copy-start(f32[4,32,16,4,512]{4,1,2,3,0:T(8,128)S(1)} %copy.49) | copy-start | bytes 50331652
  220.6 7.4 %copy-start.2 = (f32[1,16,32,4,512]{4,2,1,3,0:T(8,128)S(1)}, f32[1,16,32,4,512]{4,2,1,3,0:T(8,128)}, u32[]{:S(2)}) copy-start(f32[1,16,32,4,512]{4,2,1,3,0:T(8,128)} %get-tuple-element.14) | copy-start | bytes 12582916
  228.0 3.6 copy-start.1
  266.8 24.0 %all-to-all-start.2 = ((f32[128,4,512]{2,1,0:T(4,128)}), f32[128,4,512]{2,1,0:T(4,128)S(1)}, u32[]{:S(2)}, u32[]{:S(2)}) async-start(f32[128,4,512]{2,1,0:T(4,128)} %broadcast_in_dim.4), calls=%async_computation.2 | async-start | bytes 2097152 | tf_op jit(solution)/shard_map/all_to_all | solution.py:49
  397.7 29.9 %copy-start.4 = (f32[512,64]{1,0:T(8,128)S(1)}, f32[512,64]{1,0:T(8,128)}, u32[]{:S(2)}) copy-start(f32[512,64]{1,0:T(8,128)} %shard_map.38) | copy-start | bytes 393220
  422.9 24.0 %all-to-all-start.5 = ((f32[128,4,512]{2,1,0:T(4,128)}), f32[128,4,512]{2,1,0:T(4,128)S(1)}, u32[]{:S(2)}, u32[]{:S(2)}) async-start(f32[128,4,512]{2,1,0:T(4,128)} %broadcast_in_dim.5), calls=%async_computation.5 | async-start | bytes 2097152 | tf_op jit(solution)/shard_map/all_to_all | solution.py:49
  430.2 56.6 %copy-start.3 = (f32[1024,512]{1,0:T(8,128)S(1)}, f32[1024,512]{1,0:T(8,128)}, u32[]{:S(2)}) copy-start(f32[1024,512]{1,0:T(8,128)} %copy.32) | copy-start | bytes 6291460
  486.8 3.1 copy-start.5

commit v7 on v6

--- a/solution.py
+++ b/solution.py
@@ -53,47 +53,45 @@
     n = c.shape[0]
     row = lax.broadcasted_iota(jnp.int32, (n, n), 0)
     lane = lax.broadcasted_iota(jnp.int32, (n, n), 1)
-    right = (row == lane).astype(jnp.float32)
+    row_col = row[:, :1]
+    right = jnp.where(row == lane, 1.0, 0.0)
+    diag = jnp.sum(jnp.where(row == lane, c, 0.0), axis=1, keepdims=True)
 
     def step(j, carry):
-        left, right = carry
+        left, right, diag = carry
         at_row = row == j
         row_l = jnp.sum(jnp.where(at_row, left, 0.0), axis=0, keepdims=True)
         row_r = jnp.sum(jnp.where(at_row, right, 0.0), axis=0, keepdims=True)
         col = jnp.sum(jnp.where(lane == j, left, 0.0), axis=1, keepdims=True)
-        pivot = jnp.sum(jnp.where(row[:, :1] == j, col, 0.0), axis=0, keepdims=True)
-        factor = jnp.where(row[:, :1] > j, col / pivot, 0.0)
-        left = left - factor * row_l
-        right = right - factor * row_r
-        return left, right
+        pivot = jnp.sum(jnp.where(row_col == j, diag, 0.0), axis=0, keepdims=True)
+        factor = jnp.where(row_col > j, col / pivot, 0.0)
+        return (left - factor * row_l, right - factor * row_r, diag - factor * col)
 
-    left, right = lax.fori_loop(0, n, step, (c, right), unroll=8)
-    diag = jnp.sum(jnp.where(row == lane, left, 0.0), axis=1, keepdims=True)
+    _, right, diag = lax.fori_loop(0, n, step, (c, right, diag), unroll=8)
     return right / jnp.sqrt(diag)
 
 
 def _basis_kernel(iters, g_ref, q_ref, out_ref):
     gram = g_ref[...]
-    basis = q_ref[...]
+    basis_t = q_ref[...]
     for _ in range(iters):
-        product = jnp.dot(gram, basis, precision=lax.Precision.HIGHEST, preferred_element_type=jnp.float32)
-        inner = lax.dot_general(product, product, (((0,), (0,)), ((), ())),
+        product_t = jnp.dot(basis_t, gram, precision=lax.Precision.HIGHEST, preferred_element_type=jnp.float32)
+        inner = lax.dot_general(product_t, product_t, (((1,), (1,)), ((), ())),
                                 precision=lax.Precision.HIGHEST, preferred_element_type=jnp.float32)
-        inverse = _eliminate(inner)
-        basis = lax.dot_general(product, inverse, (((1,), (1,)), ((), ())),
-                                precision=lax.Precision.HIGHEST, preferred_element_type=jnp.float32)
-    out_ref[...] = basis
+        basis_t = jnp.dot(_eliminate(inner), product_t, precision=lax.Precision.HIGHEST,
+                          preferred_element_type=jnp.float32)
+    out_ref[...] = basis_t
 
 
 def basis_pallas(gram, start, iters=4):
-    n, r = start.shape
-    return pl.pallas_call(
+    size, n = start.shape
+    out = pl.pallas_call(
         functools.partial(_basis_kernel, iters),
-        out_shape=jax.ShapeDtypeStruct((n, r), jnp.float32),
+        out_shape=jax.ShapeDtypeStruct((n, size), jnp.float32),
         in_specs=[pl.BlockSpec(memory_space=pltpu.VMEM)] * 2,
         out_specs=pl.BlockSpec(memory_space=pltpu.VMEM),
-    )(gram, start)
-
+    )(gram, start.T)
+    return out.T
 
 def leaf_basis(gram_part, basis_now):
     gram_total = sum_over_mesh(gram_part)

time: 497 us -> 477 us (0.960)
  Pallas kernels: 77 us -> 56.8 us
    pallas_call x2, Pallas kernels: 77 us -> 56.8 us  [basis_pallas(): pl.pallas_call(functools.partial(_basis_kernel, iters), out_shape=jax.Sha...]
    unnamed x16 -> x11, local copies, waits for them, and re-layouts: 22.1 us -> 21.3 us
where the time goes in v7:
time: 477 us; the launch traced here: 472 us
  blocking collectives  278 us (58%)
  Pallas kernels  56.8 us (12%)
  local copies, waits for them, and re-layouts  55.6 us (12%)
  waiting for transfers between devices  35.2 us (7%)
  matrix products  33.9 us (7%)
  starting transfers between devices  9.16 us (2%)
    all_to_all x1, blocking collectives, body(): lax.all_to_all(species_field, 'gz', split_axis=2, concat_axis=1, tiled=True)  193 us
    pallas_call x2, Pallas kernels, basis_pallas(): pl.pallas_call(functools.partial(_basis_kernel, iters), out_shape=jax.Sha...  56.8 us
    all_to_all x2, blocking collectives, sum_over_mesh(): lax.all_to_all(gram.reshape(count, rows // count, rows), axes, 0, 0, tile...  49.4 us
    all_to_all x1, blocking collectives, body(): mixed = lax.all_to_all(send, ('gz', 'gy'), 0, 0, tiled=True)  35.4 us
    all_to_all x2, waiting for transfers between devices, sum_over_mesh(): return lax.all_to_all(tiled, axes, 0, 0, tiled=True).reshape(rows, rows)  35.2 us
    unnamed x11, local copies, waits for them, and re-layouts  21.3 us
    dot_general x4, matrix products, mode_products(): lax.dot_general(left, right, ((others, others), ((), ())), precision=lax....  18.5 us
  transfers between devices with their start and end apart: 2, of which 2 were waited for; matrix products, arithmetic and copies ran while one was open for 1% of the time, Pallas kernels for 0%

profile of v7, /device:TPU:1, one launch (start us, length us, event | category | flops | bytes accessed | tf_op | source)
XLA Modules:
  0.0 471.6 jit_solution(1457485364624052470)
XLA Ops:
  0.6 15.2 %copy.19 = f32[4,32,64,512]{3,1,0,2:T(8,128)S(1)} copy(f32[4,32,64,512]{3,2,1,0:T(8,128)} %param.1) | data formatting | bytes 33554432 | tf_op args[0]
  15.9 193.1 %all_to_all.47 = f32[4,32,64,512]{3,1,0,2:T(8,128)S(1)} all-to-all(f32[4,32,64,512]{3,1,0,2:T(8,128)S(1)} %copy.19), channel_id=1, replica_groups=mesh['gz'=16,'gy'=8] {'gz'}, dimensions={2} | all-to-all | bytes 33554432 | tf_op jit(solution)/shard_map/all_to_all | solution.py:105
  210.8 5.4 %fusion.7 = (f32[1,16,32,4,512]{4,2,1,3,0:T(8,128)S(1)}, f32[1,16,32,4,512]{4,2,1,3,0:T(8,128)}, f32[1,16,32,4,512]{4,2,1,3,0:T(8,128)}, f32[1,16,32,4,512]{4,2,1,3,0:T(8,128)}) fusion(f32[4,16,32,4,512]{4,2,1,3,0:T(8,128)S(1)} %bitcast.72), kind=kLoop, calls=%fused_computation.19 | loop fusion | bytes 33554432 | tf_op jit(solution)/shard_map/slice | solution.py:109
  216.3 4.4 copy-done
  220.7 7.7 %convolution_bitcast_fusion.2 = f32[512,512]{1,0:T(8,128)S(1)} fusion(f32[512,4,512]{2,0,1:T(8,128)} %bitcast.78), kind=kOutput, calls=%fused_computation.4 | convolution fusion | flops 3221225472 | bytes 5242880 | tf_op jit(solution)/shard_map/dot_general | solution.py:35
  228.3 3.6 convolution_bitcast_fusion.3
  232.0 3.6 fusion.3
  235.6 3.6 fusion.4
  239.5 26.2 %all_to_all.48 = f32[128,4,512]{2,1,0:T(4,128)S(1)} all-to-all(f32[128,4,512]{2,1,0:T(4,128)S(1)} %reshape.113), channel_id=1, replica_groups=mesh['gz'=16,'gy'=8] {'gz','gy'}, dimensions={0} | all-to-all | bytes 2097152 | tf_op jit(solution)/shard_map/all_to_all | solution.py:44
  267.1 4.5 all-to-all-start.2
  273.3 17.7 %all-to-all-done.2 = f32[128,4,512]{2,1,0:T(4,128)S(1)} async-done(((f32[128,4,512]{2,1,0:T(4,128)}), f32[128,4,512]{2,1,0:T(4,128)S(1)}, u32[]{:S(2)}, u32[]{:S(2)}) %all-to-all-start.2) | async-done | bytes 1048608 | tf_op jit(solution)/shard_map/all_to_all | solution.py:49
  292.4 28.4 %shard_map.38 = f32[64,512]{1,0:T(8,128)} custom-call(f32[512,512]{1,0:T(8,128)} %reshape.114.g_ref, f32[64,512]{1,0:T(8,128)} %get-tuple-element.19.q_ref), custom_call_target="tpu_custom_call" | custom-call | tf_op jit(solution)/shard_map/pallas_call | solution.py:88
  320.7 9.2 %convolution_bitcast_fusion = f32[512,4,4,64]{0,3,1,2:T(8,128)S(1)} fusion(f32[4,512,4,512]{3,1,2,0:T(8,128)} %bitcast.73, f32[64,512]{1,0:T(8,128)} %shard_map.38), kind=kOutput, calls=%fused_computation.2 | convolution fusion | flops 1610612736 | bytes 19005440 | tf_op jit(solution)/shard_map/szyx,zr->xysr/dot_general | solution.py:112
  329.9 2.7 copy.21
  332.6 3.5 copy.22
  336.1 4.1 copy.23
  340.2 35.4 %all_to_all.49 = f32[128,1,4096]{2,1,0:T(1,128)S(1)} all-to-all(f32[128,1,4096]{2,1,0:T(1,128)} %copy.23), channel_id=1, replica_groups=mesh['gz'=16,'gy'=8] {'gz','gy'}, dimensions={0} | all-to-all | bytes 4194304 | tf_op jit(solution)/shard_map/all_to_all | solution.py:116
  375.6 3.8 copy.24
  379.5 1.9 copy.25
  383.0 4.3 fusion
  388.1 23.2 %all_to_all.50 = f32[128,4,512]{2,1,0:T(4,128)S(1)} all-to-all(f32[128,4,512]{2,1,0:T(4,128)S(1)} %copy.29), channel_id=1, replica_groups=mesh['gz'=16,'gy'=8] {'gz','gy'}, dimensions={0} | all-to-all | bytes 2097152 | tf_op jit(solution)/shard_map/all_to_all | solution.py:44
  412.6 4.7 all-to-all-start.5
  419.2 17.5 %all-to-all-done.5 = f32[128,4,512]{2,1,0:T(4,128)S(1)} async-done(((f32[128,4,512]{2,1,0:T(4,128)}), f32[128,4,512]{2,1,0:T(4,128)S(1)}, u32[]{:S(2)}, u32[]{:S(2)}) %all-to-all-start.5) | async-done | bytes 1048608 | tf_op jit(solution)/shard_map/all_to_all | solution.py:49
  438.0 28.4 %shard_map.39 = f32[64,512]{1,0:T(8,128)} custom-call(f32[512,512]{1,0:T(8,128)} %reshape.118.g_ref, f32[64,512]{1,0:T(8,128)} %get-tuple-element.18.q_ref), custom_call_target="tpu_custom_call" | custom-call | tf_op jit(solution)/shard_map/pallas_call | solution.py:88
  (29 shorter events, 18.4 us)
Async XLA Ops:
  210.8 9.8 %copy-start = (f32[4,32,16,4,512]{4,1,2,3,0:T(8,128)}, f32[4,32,16,4,512]{4,1,2,3,0:T(8,128)S(1)}, u32[]{:S(2)}) copy-start(f32[4,32,16,4,512]{4,1,2,3,0:T(8,128)S(1)} %copy.40) | copy-start | bytes 50331652
  220.6 7.7 %copy-start.2 = (f32[1,16,32,4,512]{4,2,1,3,0:T(8,128)S(1)}, f32[1,16,32,4,512]{4,2,1,3,0:T(8,128)}, u32[]{:S(2)}) copy-start(f32[1,16,32,4,512]{4,2,1,3,0:T(8,128)} %get-tuple-element.14) | copy-start | bytes 12582916
  228.3 3.6 copy-start.1
  267.1 24.0 %all-to-all-start.2 = ((f32[128,4,512]{2,1,0:T(4,128)}), f32[128,4,512]{2,1,0:T(4,128)S(1)}, u32[]{:S(2)}, u32[]{:S(2)}) async-start(f32[128,4,512]{2,1,0:T(4,128)} %broadcast_in_dim.4), calls=%async_computation.2 | async-start | bytes 2097152 | tf_op jit(solution)/shard_map/all_to_all | solution.py:49
  412.6 24.1 %all-to-all-start.5 = ((f32[128,4,512]{2,1,0:T(4,128)}), f32[128,4,512]{2,1,0:T(4,128)S(1)}, u32[]{:S(2)}, u32[]{:S(2)}) async-start(f32[128,4,512]{2,1,0:T(4,128)} %broadcast_in_dim.5), calls=%async_computation.5 | async-start | bytes 2097152 | tf_op jit(solution)/shard_map/all_to_all | solution.py:49
  419.2 47.2 %copy-start.3 = (f32[1024,512]{1,0:T(8,128)S(1)}, f32[1024,512]{1,0:T(8,128)}, u32[]{:S(2)}) copy-start(f32[1024,512]{1,0:T(8,128)} %copy.26) | copy-start | bytes 6291460

commit v8 on v7

--- a/solution.py
+++ b/solution.py
@@ -93,6 +93,38 @@
     )(gram, start.T)
     return out.T
 
+def _reduce_kernel(count, x_part, rank, fib_ref, bz_ref, out_ref, t_ref):
+    y = pl.program_id(0)
+    species = fib_ref.shape[1]
+    per = 128 // rank
+    for s in range(species):
+        t_ref[s // per, :, (s % per) * rank : (s % per + 1) * rank] = jnp.dot(
+            bz_ref[...], fib_ref[0, s],
+            precision=lax.Precision.HIGH, preferred_element_type=jnp.float32).T
+    width = species * rank
+    for xl in range(x_part):
+        for h in range(species // per):
+            rows = t_ref[h, pl.ds(xl, count, stride=x_part), :]
+            col = pl.multiple_of((y * x_part + xl) * width + h * 128, 128)
+            out_ref[:, 0, pl.ds(col, 128)] = rows
+
+
+def reduce_send(fib_ys, basis_z, count):
+    ys, species, zs, xs = fib_ys.shape
+    rank = basis_z.shape[1]
+    x_part = xs // count
+    return pl.pallas_call(
+        functools.partial(_reduce_kernel, count, x_part, rank),
+        grid=(ys,),
+        in_specs=[pl.BlockSpec((1, species, zs, xs), lambda y: (y, 0, 0, 0)),
+                  pl.BlockSpec((rank, zs), lambda y: (0, 0))],
+        out_specs=pl.BlockSpec((count, 1, ys * x_part * species * rank), lambda y: (0, 0, 0)),
+        out_shape=jax.ShapeDtypeStruct((count, 1, ys * x_part * species * rank), jnp.float32),
+        scratch_shapes=[pltpu.VMEM((species * rank // 128, xs, 128), jnp.float32)],
+        compiler_params=pltpu.CompilerParams(vmem_limit_bytes=48 * 1024 * 1024),
+    )(fib_ys, basis_z.T)
+
+
 def leaf_basis(gram_part, basis_now):
     gram_total = sum_over_mesh(gram_part)
     return basis_pallas(gram_total, basis_now, ITERS)
@@ -109,10 +141,8 @@
         term = mode_products(fibres[one : one + 1], fibres[one : one + 1], 1)
         gram_z = term if gram_z is None else gram_z + term
     basis_z = leaf_basis(gram_z, start_table(GRID, RANK))
-    reduced = jnp.einsum("szyx,zr->xysr", fibres, basis_z, precision=lax.Precision.HIGH)
     x_part = x_size // count
-    send = reduced.reshape(count, x_part, y_local, species, RANK)
-    send = jnp.transpose(send, (0, 2, 1, 3, 4)).reshape(count, -1)
+    send = reduce_send(jnp.transpose(fibres, (2, 0, 1, 3)), basis_z, count)
     mixed = lax.all_to_all(send, ("gz", "gy"), 0, 0, tiled=True)
     fibres_y = mixed.reshape(count, y_local, -1)
     fibres_y = jnp.transpose(fibres_y, (1, 0, 2)).reshape(count * y_local, -1)

time: 477 us -> 472 us (0.990)
  local copies, waits for them, and re-layouts: 55.6 us -> 42.2 us
  Pallas kernels: 56.8 us -> 67.2 us
  matrix products: 33.9 us -> 24.4 us
  other arithmetic: 2.05 us -> 9.32 us
    pallas_call x0 -> x1, Pallas kernels: none -> 10.4 us  [reduce_send(): pl.pallas_call(functools.partial(_reduce_kernel, count, x_part, rank), gr...]
    dot_general x1 -> x0, matrix products: 9.17 us -> none  [body(): jnp.einsum('szyx,zr->xysr', fibres, basis_z, precision=lax.Precision.HIGH)]
    transpose x3 -> x0, local copies, waits for them, and re-layouts: 8.13 us -> none  [the longest x1 3.51 us: body(): send = jnp.transpose(send, (0, 2, 1, 3, 4)).reshape(count, -1)]
    all_to_all x2 -> x0, local copies, waits for them, and re-layouts: 7.92 us -> none  [body(): mixed = lax.all_to_all(send, ('gz', 'gy'), 0, 0, tiled=True)]
    all_to_all x0 -> x1, other arithmetic: none -> 7.27 us  [body(): mixed = lax.all_to_all(send, ('gz', 'gy'), 0, 0, tiled=True)]
    unnamed x11 -> x13, local copies, waits for them, and re-layouts: 21.3 us -> 22.2 us
where the time goes in v8:
time: 472 us; the launch traced here: 466 us
  blocking collectives  278 us (59%)
  Pallas kernels  67.2 us (14%)
  local copies, waits for them, and re-layouts  42.2 us (9%)
  waiting for transfers between devices  35.2 us (7%)
  matrix products  24.4 us (5%)
  other arithmetic  9.32 us (2%)
  starting transfers between devices  9.12 us (2%)
    all_to_all x1, blocking collectives, body(): lax.all_to_all(species_field, 'gz', split_axis=2, concat_axis=1, tiled=True)  193 us
    pallas_call x2, Pallas kernels, basis_pallas(): pl.pallas_call(functools.partial(_basis_kernel, iters), out_shape=jax.Sha...  56.7 us
    all_to_all x2, blocking collectives, sum_over_mesh(): lax.all_to_all(gram.reshape(count, rows // count, rows), axes, 0, 0, tile...  49.4 us
    all_to_all x2, waiting for transfers between devices, sum_over_mesh(): return lax.all_to_all(tiled, axes, 0, 0, tiled=True).reshape(rows, rows)  35.2 us
    all_to_all x1, blocking collectives, body(): mixed = lax.all_to_all(send, ('gz', 'gy'), 0, 0, tiled=True)  35.1 us
    unnamed x13, local copies, waits for them, and re-layouts  22.2 us
    dot_general x4, matrix products, mode_products(): lax.dot_general(left, right, ((others, others), ((), ())), precision=lax....  18.2 us
    pallas_call x1, Pallas kernels, reduce_send(): pl.pallas_call(functools.partial(_reduce_kernel, count, x_part, rank), gr...  10.4 us
  transfers between devices with their start and end apart: 2, of which 2 were waited for; matrix products, arithmetic and copies ran while one was open for 1% of the time, Pallas kernels for 0%

profile of v8, /device:TPU:1, one launch (start us, length us, event | category | flops | bytes accessed | tf_op | source)
XLA Modules:
  0.0 466.0 jit_solution(1355215539103665150)
XLA Ops:
  0.6 15.2 %copy.17 = f32[4,32,64,512]{3,1,0,2:T(8,128)S(1)} copy(f32[4,32,64,512]{3,2,1,0:T(8,128)} %param.1) | data formatting | bytes 33554432 | tf_op args[0]
  15.9 193.1 %all_to_all.43 = f32[4,32,64,512]{3,1,0,2:T(8,128)S(1)} all-to-all(f32[4,32,64,512]{3,1,0,2:T(8,128)S(1)} %copy.17), channel_id=1, replica_groups=mesh['gz'=16,'gy'=8] {'gz'}, dimensions={2} | all-to-all | bytes 33554432 | tf_op jit(solution)/shard_map/all_to_all | solution.py:137
  208.9 1.9 copy.37
  210.8 5.4 %fusion.7 = (f32[1,16,32,4,512]{4,2,1,0,3:T(8,128)S(1)}, f32[1,16,32,4,512]{4,2,1,0,3:T(8,128)}, f32[1,16,32,4,512]{4,2,1,0,3:T(8,128)}, f32[1,16,32,4,512]{4,2,1,0,3:T(8,128)}) fusion(f32[4,16,32,4,512]{4,2,1,0,3:T(8,128)S(1)} %bitcast.70), kind=kLoop, calls=%fused_computation.19 | loop fusion | bytes 33554432 | tf_op jit(solution)/shard_map/slice | solution.py:141
  216.2 4.4 copy-done.1
  220.7 7.4 %convolution_bitcast_fusion.1 = f32[512,512]{1,0:T(8,128)S(1)} fusion(f32[512,4,512]{2,0,1:T(8,128)} %bitcast.76), kind=kOutput, calls=%fused_computation.4 | convolution fusion | flops 3221225472 | bytes 5242880 | tf_op jit(solution)/shard_map/dot_general | solution.py:35
  228.0 3.6 convolution_bitcast_fusion.2
  231.7 3.6 fusion.3
  235.3 3.6 fusion.4
  239.2 26.2 %all_to_all.44 = f32[128,4,512]{2,1,0:T(4,128)S(1)} all-to-all(f32[128,4,512]{2,1,0:T(4,128)S(1)} %reshape.105), channel_id=1, replica_groups=mesh['gz'=16,'gy'=8] {'gz','gy'}, dimensions={0} | all-to-all | bytes 2097152 | tf_op jit(solution)/shard_map/all_to_all | solution.py:44
  266.8 4.5 all-to-all-start.2
  273.1 17.7 %all-to-all-done.2 = f32[128,4,512]{2,1,0:T(4,128)S(1)} async-done(((f32[128,4,512]{2,1,0:T(4,128)}), f32[128,4,512]{2,1,0:T(4,128)S(1)}, u32[]{:S(2)}, u32[]{:S(2)}) %all-to-all-start.2) | async-done | bytes 1048608 | tf_op jit(solution)/shard_map/all_to_all | solution.py:49
  292.1 28.4 %shard_map.38.bz_ref = f32[64,512]{1,0:T(8,128)} custom-call(f32[512,512]{1,0:T(8,128)} %reshape.106.g_ref, f32[64,512]{1,0:T(8,128)} %get-tuple-element.21.q_ref), custom_call_target="tpu_custom_call" | custom-call | tf_op jit(solution)/shard_map/pallas_call | solution.py:88
  321.4 10.4 %shard_map.39 = f32[128,1,4096]{2,1,0:T(1,128)S(1)} custom-call(f32[4,4,512,512]{3,2,1,0:T(8,128)} %bitcast.71, f32[64,512]{1,0:T(8,128)S(1)} %copy-done), custom_call_target="tpu_custom_call" | custom-call | tf_op jit(solution)/shard_map/pallas_call | solution.py:116
  331.9 35.1 %all_to_all.45 = f32[128,1,4096]{2,1,0:T(1,128)S(1)} all-to-all(f32[128,1,4096]{2,1,0:T(1,128)S(1)} %shard_map.39), channel_id=1, replica_groups=mesh['gz'=16,'gy'=8] {'gz','gy'}, dimensions={0} | all-to-all | bytes 4194304 | tf_op jit(solution)/shard_map/all_to_all | solution.py:146
  366.9 7.3 %reduce = f32[128,4096]{1,0:T(8,128)} reduce(f32[128,1,4096]{2,1,0:T(1,128)S(1)} %all_to_all.45, f32[]{:T(128)} %constant.13), dimensions={1}, to_apply=%all_to_all.34.reduce_sub_computation | reduce | bytes 4194308 | tf_op jit(solution)/shard_map/all_to_all | solution.py:146
  374.2 1.7 copy.36
  377.6 4.3 fusion
  382.6 23.2 %all_to_all.46 = f32[128,4,512]{2,1,0:T(4,128)S(1)} all-to-all(f32[128,4,512]{2,1,0:T(4,128)S(1)} %copy.22), channel_id=1, replica_groups=mesh['gz'=16,'gy'=8] {'gz','gy'}, dimensions={0} | all-to-all | bytes 2097152 | tf_op jit(solution)/shard_map/all_to_all | solution.py:44
  407.2 4.6 all-to-all-start.5
  411.8 1.9 copy.20
  413.7 17.5 %all-to-all-done.5 = f32[128,4,512]{2,1,0:T(4,128)S(1)} async-done(((f32[128,4,512]{2,1,0:T(4,128)}), f32[128,4,512]{2,1,0:T(4,128)S(1)}, u32[]{:S(2)}, u32[]{:S(2)}) %all-to-all-start.5) | async-done | bytes 1048608 | tf_op jit(solution)/shard_map/all_to_all | solution.py:49
  432.5 28.4 %shard_map.40 = f32[64,512]{1,0:T(8,128)} custom-call(f32[512,512]{1,0:T(8,128)} %reshape.109.g_ref, f32[64,512]{1,0:T(8,128)} %get-tuple-element.20.q_ref), custom_call_target="tpu_custom_call" | custom-call | tf_op jit(solution)/shard_map/pallas_call | solution.py:88
  460.9 1.9 convolution_bitcast_fusion.4
  (28 shorter events, 13.7 us)
Async XLA Ops:
  210.8 9.8 %copy-start.1 = (f32[4,32,16,4,512]{4,1,2,0,3:T(8,128)}, f32[4,32,16,4,512]{4,1,2,0,3:T(8,128)S(1)}, u32[]{:S(2)}) copy-start(f32[4,32,16,4,512]{4,1,2,0,3:T(8,128)S(1)} %copy.37) | copy-start | bytes 50331652
  220.6 7.4 %copy-start.3 = (f32[1,16,32,4,512]{4,2,1,0,3:T(8,128)S(1)}, f32[1,16,32,4,512]{4,2,1,0,3:T(8,128)}, u32[]{:S(2)}) copy-start(f32[1,16,32,4,512]{4,2,1,0,3:T(8,128)} %get-tuple-element.14) | copy-start | bytes 12582916
  228.0 3.6 copy-start.2
  266.8 24.0 %all-to-all-start.2 = ((f32[128,4,512]{2,1,0:T(4,128)}), f32[128,4,512]{2,1,0:T(4,128)S(1)}, u32[]{:S(2)}, u32[]{:S(2)}) async-start(f32[128,4,512]{2,1,0:T(4,128)} %broadcast_in_dim.4), calls=%async_computation.2 | async-start | bytes 2097152 | tf_op jit(solution)/shard_map/all_to_all | solution.py:49
  320.5 0.9 copy-start
  407.2 24.0 %all-to-all-start.5 = ((f32[128,4,512]{2,1,0:T(4,128)}), f32[128,4,512]{2,1,0:T(4,128)S(1)}, u32[]{:S(2)}, u32[]{:S(2)}) async-start(f32[128,4,512]{2,1,0:T(4,128)} %broadcast_in_dim.5), calls=%async_computation.5 | async-start | bytes 2097152 | tf_op jit(solution)/shard_map/all_to_all | solution.py:49
  413.7 47.2 %copy-start.4 = (f32[1024,512]{1,0:T(8,128)S(1)}, f32[1024,512]{1,0:T(8,128)}, u32[]{:S(2)}) copy-start(f32[1024,512]{1,0:T(8,128)} %copy.20) | copy-start | bytes 6291460

commit v9 on v8

--- a/solution.py
+++ b/solution.py
@@ -67,7 +67,7 @@
         factor = jnp.where(row_col > j, col / pivot, 0.0)
         return (left - factor * row_l, right - factor * row_r, diag - factor * col)
 
-    _, right, diag = lax.fori_loop(0, n, step, (c, right, diag), unroll=8)
+    _, right, diag = lax.fori_loop(0, n, step, (c, right, diag), unroll=64)
     return right / jnp.sqrt(diag)
 
 

time: 472 us -> 468 us (level)
  no operation moved by 1% of the time
where the time goes in v9:
time: 468 us; the launch traced here: 462 us
  blocking collectives  277 us (59%)
  Pallas kernels  63.8 us (14%)
  local copies, waits for them, and re-layouts  42.4 us (9%)
  waiting for transfers between devices  35.1 us (8%)
  matrix products  24.4 us (5%)
  other arithmetic  9.32 us (2%)
  starting transfers between devices  9.03 us (2%)
    all_to_all x1, blocking collectives, body(): lax.all_to_all(species_field, 'gz', split_axis=2, concat_axis=1, tiled=True)  193 us
    pallas_call x2, Pallas kernels, basis_pallas(): pl.pallas_call(functools.partial(_basis_kernel, iters), out_shape=jax.Sha...  53.2 us
    all_to_all x2, blocking collectives, sum_over_mesh(): lax.all_to_all(gram.reshape(count, rows // count, rows), axes, 0, 0, tile...  49.4 us
    all_to_all x2, waiting for transfers between devices, sum_over_mesh(): return lax.all_to_all(tiled, axes, 0, 0, tiled=True).reshape(rows, rows)  35.1 us
    all_to_all x1, blocking collectives, body(): mixed = lax.all_to_all(send, ('gz', 'gy'), 0, 0, tiled=True)  34.7 us
    unnamed x13, local copies, waits for them, and re-layouts  22.2 us
    dot_general x4, matrix products, mode_products(): lax.dot_general(left, right, ((others, others), ((), ())), precision=lax....  18.2 us
    pallas_call x1, Pallas kernels, reduce_send(): pl.pallas_call(functools.partial(_reduce_kernel, count, x_part, rank), gr...  10.6 us
  transfers between devices with their start and end apart: 2, of which 2 were waited for; matrix products, arithmetic and copies ran while one was open for 1% of the time, Pallas kernels for 0%

profile of v9, /device:TPU:1, one launch (start us, length us, event | category | flops | bytes accessed | tf_op | source)
XLA Modules:
  0.0 462.3 jit_solution(7178113207227429439)
XLA Ops:
  0.6 15.2 %copy.17 = f32[4,32,64,512]{3,1,0,2:T(8,128)S(1)} copy(f32[4,32,64,512]{3,2,1,0:T(8,128)} %param.1) | data formatting | bytes 33554432 | tf_op args[0]
  15.9 193.1 %all_to_all.43 = f32[4,32,64,512]{3,1,0,2:T(8,128)S(1)} all-to-all(f32[4,32,64,512]{3,1,0,2:T(8,128)S(1)} %copy.17), channel_id=1, replica_groups=mesh['gz'=16,'gy'=8] {'gz'}, dimensions={2} | all-to-all | bytes 33554432 | tf_op jit(solution)/shard_map/all_to_all | solution.py:137
  208.9 1.9 copy.37
  210.8 5.4 %fusion.7 = (f32[1,16,32,4,512]{4,2,1,0,3:T(8,128)S(1)}, f32[1,16,32,4,512]{4,2,1,0,3:T(8,128)}, f32[1,16,32,4,512]{4,2,1,0,3:T(8,128)}, f32[1,16,32,4,512]{4,2,1,0,3:T(8,128)}) fusion(f32[4,16,32,4,512]{4,2,1,0,3:T(8,128)S(1)} %bitcast.70), kind=kLoop, calls=%fused_computation.19 | loop fusion | bytes 33554432 | tf_op jit(solution)/shard_map/slice | solution.py:141
  216.2 4.4 copy-done.1
  220.7 7.4 %convolution_bitcast_fusion.1 = f32[512,512]{1,0:T(8,128)S(1)} fusion(f32[512,4,512]{2,0,1:T(8,128)} %bitcast.76), kind=kOutput, calls=%fused_computation.4 | convolution fusion | flops 3221225472 | bytes 5242880 | tf_op jit(solution)/shard_map/dot_general | solution.py:35
  228.0 3.6 convolution_bitcast_fusion.2
  231.7 3.6 fusion.3
  235.3 3.6 fusion.4
  239.3 26.2 %all_to_all.44 = f32[128,4,512]{2,1,0:T(4,128)S(1)} all-to-all(f32[128,4,512]{2,1,0:T(4,128)S(1)} %reshape.105), channel_id=1, replica_groups=mesh['gz'=16,'gy'=8] {'gz','gy'}, dimensions={0} | all-to-all | bytes 2097152 | tf_op jit(solution)/shard_map/all_to_all | solution.py:44
  266.8 4.7 %all-to-all-start.2 = ((f32[128,4,512]{2,1,0:T(4,128)}), f32[128,4,512]{2,1,0:T(4,128)S(1)}, u32[]{:S(2)}, u32[]{:S(2)}) async-start(f32[128,4,512]{2,1,0:T(4,128)} %broadcast_in_dim.4), calls=%async_computation.2 | async-start | bytes 2097152 | tf_op jit(solution)/shard_map/all_to_all | solution.py:49
  273.2 17.7 %all-to-all-done.2 = f32[128,4,512]{2,1,0:T(4,128)S(1)} async-done(((f32[128,4,512]{2,1,0:T(4,128)}), f32[128,4,512]{2,1,0:T(4,128)S(1)}, u32[]{:S(2)}, u32[]{:S(2)}) %all-to-all-start.2) | async-done | bytes 1048608 | tf_op jit(solution)/shard_map/all_to_all | solution.py:49
  292.3 26.6 %shard_map.38.bz_ref = f32[64,512]{1,0:T(8,128)} custom-call(f32[512,512]{1,0:T(8,128)} %reshape.106.g_ref, f32[64,512]{1,0:T(8,128)} %get-tuple-element.21.q_ref), custom_call_target="tpu_custom_call" | custom-call | tf_op jit(solution)/shard_map/pallas_call | solution.py:88
  319.8 10.6 %shard_map.39 = f32[128,1,4096]{2,1,0:T(1,128)S(1)} custom-call(f32[4,4,512,512]{3,2,1,0:T(8,128)} %bitcast.71, f32[64,512]{1,0:T(8,128)S(1)} %copy-done), custom_call_target="tpu_custom_call" | custom-call | tf_op jit(solution)/shard_map/pallas_call | solution.py:116
  330.4 34.7 %all_to_all.45 = f32[128,1,4096]{2,1,0:T(1,128)S(1)} all-to-all(f32[128,1,4096]{2,1,0:T(1,128)S(1)} %shard_map.39), channel_id=1, replica_groups=mesh['gz'=16,'gy'=8] {'gz','gy'}, dimensions={0} | all-to-all | bytes 4194304 | tf_op jit(solution)/shard_map/all_to_all | solution.py:146
  365.1 7.3 %reduce = f32[128,4096]{1,0:T(8,128)} reduce(f32[128,1,4096]{2,1,0:T(1,128)S(1)} %all_to_all.45, f32[]{:T(128)} %constant.13), dimensions={1}, to_apply=%all_to_all.34.reduce_sub_computation | reduce | bytes 4194308 | tf_op jit(solution)/shard_map/all_to_all | solution.py:146
  372.4 1.7 copy.36
  375.7 4.3 fusion
  380.8 23.2 %all_to_all.46 = f32[128,4,512]{2,1,0:T(4,128)S(1)} all-to-all(f32[128,4,512]{2,1,0:T(4,128)S(1)} %copy.22), channel_id=1, replica_groups=mesh['gz'=16,'gy'=8] {'gz','gy'}, dimensions={0} | all-to-all | bytes 2097152 | tf_op jit(solution)/shard_map/all_to_all | solution.py:44
  405.3 4.3 all-to-all-start.5
  409.7 2.1 copy.20
  411.7 17.4 %all-to-all-done.5 = f32[128,4,512]{2,1,0:T(4,128)S(1)} async-done(((f32[128,4,512]{2,1,0:T(4,128)}), f32[128,4,512]{2,1,0:T(4,128)S(1)}, u32[]{:S(2)}, u32[]{:S(2)}) %all-to-all-start.5) | async-done | bytes 1048608 | tf_op jit(solution)/shard_map/all_to_all | solution.py:49
  430.5 26.6 %shard_map.40 = f32[64,512]{1,0:T(8,128)} custom-call(f32[512,512]{1,0:T(8,128)} %reshape.109.g_ref, f32[64,512]{1,0:T(8,128)} %get-tuple-element.20.q_ref), custom_call_target="tpu_custom_call" | custom-call | tf_op jit(solution)/shard_map/pallas_call | solution.py:88
  457.1 1.9 convolution_bitcast_fusion.4
  (28 shorter events, 13.7 us)
Async XLA Ops:
  210.8 9.8 %copy-start.1 = (f32[4,32,16,4,512]{4,1,2,0,3:T(8,128)}, f32[4,32,16,4,512]{4,1,2,0,3:T(8,128)S(1)}, u32[]{:S(2)}) copy-start(f32[4,32,16,4,512]{4,1,2,0,3:T(8,128)S(1)} %copy.37) | copy-start | bytes 50331652
  220.6 7.4 %copy-start.3 = (f32[1,16,32,4,512]{4,2,1,0,3:T(8,128)S(1)}, f32[1,16,32,4,512]{4,2,1,0,3:T(8,128)}, u32[]{:S(2)}) copy-start(f32[1,16,32,4,512]{4,2,1,0,3:T(8,128)} %get-tuple-element.14) | copy-start | bytes 12582916
  228.0 3.6 copy-start.2
  266.8 24.2 %all-to-all-start.2 = ((f32[128,4,512]{2,1,0:T(4,128)}), f32[128,4,512]{2,1,0:T(4,128)S(1)}, u32[]{:S(2)}, u32[]{:S(2)}) async-start(f32[128,4,512]{2,1,0:T(4,128)} %broadcast_in_dim.4), calls=%async_computation.2 | async-start | bytes 2097152 | tf_op jit(solution)/shard_map/all_to_all | solution.py:49
  318.9 0.9 copy-start
  405.3 23.8 %all-to-all-start.5 = ((f32[128,4,512]{2,1,0:T(4,128)}), f32[128,4,512]{2,1,0:T(4,128)S(1)}, u32[]{:S(2)}, u32[]{:S(2)}) async-start(f32[128,4,512]{2,1,0:T(4,128)} %broadcast_in_dim.5), calls=%async_computation.5 | async-start | bytes 2097152 | tf_op jit(solution)/shard_map/all_to_all | solution.py:49
  411.7 45.3 %copy-start.4 = (f32[1024,512]{1,0:T(8,128)S(1)}, f32[1024,512]{1,0:T(8,128)}, u32[]{:S(2)}) copy-start(f32[1024,512]{1,0:T(8,128)} %copy.20) | copy-start | bytes 6291460

commit v10 on v9

--- a/solution.py
+++ b/solution.py
@@ -125,6 +125,49 @@
     )(fib_ys, basis_z.T)
 
 
+def _gram_y_kernel(y_local, m_ref, g_ref):
+    count = m_ref.shape[0]
+    width = m_ref.shape[2] // y_local
+    parts = [m_ref[:, 0, a * width : (a + 1) * width] for a in range(y_local)]
+    for a in range(y_local):
+        for b in range(y_local):
+            g_ref[a * count : (a + 1) * count, b * count : (b + 1) * count] = lax.dot_general(
+                parts[a], parts[b], (((1,), (1,)), ((), ())),
+                precision=lax.Precision.HIGH, preferred_element_type=jnp.float32)
+
+
+def gram_y_pallas(mixed, y_local):
+    size = mixed.shape[0] * y_local
+    return pl.pallas_call(
+        functools.partial(_gram_y_kernel, y_local),
+        out_shape=jax.ShapeDtypeStruct((size, size), jnp.float32),
+        in_specs=[pl.BlockSpec(memory_space=pltpu.VMEM)],
+        out_specs=pl.BlockSpec(memory_space=pltpu.VMEM),
+    )(mixed)
+
+
+def _core_kernel(y_local, m_ref, b_ref, out_ref):
+    count = m_ref.shape[0]
+    width = m_ref.shape[2] // y_local
+    total = None
+    for a in range(y_local):
+        term = jnp.dot(b_ref[:, a * count : (a + 1) * count], m_ref[:, 0, a * width : (a + 1) * width],
+                       precision=lax.Precision.HIGH, preferred_element_type=jnp.float32)
+        total = term if total is None else total + term
+    out_ref[...] = total
+
+
+def core_pallas(mixed, basis_perm, y_local):
+    rank = basis_perm.shape[1]
+    width = mixed.shape[2] // y_local
+    return pl.pallas_call(
+        functools.partial(_core_kernel, y_local),
+        out_shape=jax.ShapeDtypeStruct((rank, width), jnp.float32),
+        in_specs=[pl.BlockSpec(memory_space=pltpu.VMEM)] * 2,
+        out_specs=pl.BlockSpec(memory_space=pltpu.VMEM),
+    )(mixed, basis_perm.T)
+
+
 def leaf_basis(gram_part, basis_now):
     gram_total = sum_over_mesh(gram_part)
     return basis_pallas(gram_total, basis_now, ITERS)
@@ -144,19 +187,13 @@
     x_part = x_size // count
     send = reduce_send(jnp.transpose(fibres, (2, 0, 1, 3)), basis_z, count)
     mixed = lax.all_to_all(send, ("gz", "gy"), 0, 0, tiled=True)
-    fibres_y = mixed.reshape(count, y_local, -1)
-    fibres_y = jnp.transpose(fibres_y, (1, 0, 2)).reshape(count * y_local, -1)
-    gram_y = lax.dot_general(
-        fibres_y, fibres_y, (((1,), (1,)), ((), ())), precision=lax.Precision.HIGH
-    )
+    gram_y = gram_y_pallas(mixed, y_local)
     start_y = start_table(GRID, RANK).reshape(count_gy, count_gz, y_local, RANK)
     start_y = jnp.transpose(start_y, (2, 1, 0, 3)).reshape(GRID, RANK)
     basis_perm = leaf_basis(gram_y, start_y)
-    core_rows = lax.dot_general(
-        fibres_y, basis_perm, (((0,), (0,)), ((), ())), precision=lax.Precision.HIGH
-    )
-    core_tensor = core_rows.reshape(x_part, species, RANK, RANK)
-    core_tensor = jnp.transpose(core_tensor, (1, 0, 2, 3)).reshape(species, x_part, RANK * RANK)
+    core_t = core_pallas(mixed, basis_perm, y_local)
+    core_tensor = core_t.reshape(RANK, x_part, species, RANK)
+    core_tensor = jnp.transpose(core_tensor, (2, 1, 3, 0)).reshape(species, x_part, RANK * RANK)
     basis_y = basis_perm.reshape(y_local, count_gz, count_gy, RANK)
     basis_y = jnp.transpose(basis_y, (2, 1, 0, 3)).reshape(GRID, RANK)
     return (core_tensor, basis_z, basis_y)

time: 468 us -> 461 us (0.985)
  blocking collectives: 277 us -> 301 us
  waiting for transfers between devices: 35.1 us -> 17.7 us
  Pallas kernels: 63.8 us -> 73.6 us
  other arithmetic: 9.32 us -> 2.05 us
  matrix products: 24.4 us -> 18.2 us
  local copies, waits for them, and re-layouts: 42.4 us -> 37.3 us
    all_to_all x0 -> x1, blocking collectives: none -> 23.5 us  [sum_over_mesh(): return lax.all_to_all(tiled, axes, 0, 0, tiled=True).reshape(rows, rows)]
    all_to_all x2 -> x1, waiting for transfers between devices: 35.1 us -> 17.7 us  [sum_over_mesh(): return lax.all_to_all(tiled, axes, 0, 0, tiled=True).reshape(rows, rows)]
    pallas_call x0 -> x2, Pallas kernels: none -> 9.61 us  [the longest x1 6.24 us: gram_y_pallas(): pl.pallas_call(functools.partial(_gram_y_kernel, y_local), out_shape=jax....]
    all_to_all x1 -> x0, other arithmetic: 7.27 us -> none  [body(): mixed = lax.all_to_all(send, ('gz', 'gy'), 0, 0, tiled=True)]
    dot_general x2 -> x0, matrix products: 6.2 us -> none  [the longest x1 4.34 us: body(): lax.dot_general(fibres_y, fibres_y, (((1,), (1,)), ((), ())), precision=l...]
    unnamed x13 -> x12, local copies, waits for them, and re-layouts: 22.2 us -> 21.3 us
  transfers between devices with their start and end apart: 2 -> 1, of which waited for: 2 -> 1; matrix products, arithmetic and copies ran while one was open for 1% -> 0% of each run, Pallas kernels for 0% -> 0%
where the time goes in v10:
time: 461 us; the launch traced here: 455 us
  blocking collectives  301 us (65%)
  Pallas kernels  73.6 us (16%)
  local copies, waits for them, and re-layouts  37.3 us (8%)
  matrix products  18.2 us (4%)
  waiting for transfers between devices  17.7 us (4%)
    all_to_all x1, blocking collectives, body(): lax.all_to_all(species_field, 'gz', split_axis=2, concat_axis=1, tiled=True)  193 us
    pallas_call x2, Pallas kernels, basis_pallas(): pl.pallas_call(functools.partial(_basis_kernel, iters), out_shape=jax.Sha...  53.2 us
    all_to_all x2, blocking collectives, sum_over_mesh(): lax.all_to_all(gram.reshape(count, rows // count, rows), axes, 0, 0, tile...  49.4 us
    all_to_all x1, blocking collectives, body(): mixed = lax.all_to_all(send, ('gz', 'gy'), 0, 0, tiled=True)  35 us
    all_to_all x1, blocking collectives, sum_over_mesh(): return lax.all_to_all(tiled, axes, 0, 0, tiled=True).reshape(rows, rows)  23.5 us
    unnamed x12, local copies, waits for them, and re-layouts  21.3 us
    dot_general x4, matrix products, mode_products(): lax.dot_general(left, right, ((others, others), ((), ())), precision=lax....  18.2 us
    all_to_all x1, waiting for transfers between devices, sum_over_mesh(): return lax.all_to_all(tiled, axes, 0, 0, tiled=True).reshape(rows, rows)  17.7 us
  transfers between devices with their start and end apart: 1, of which 1 were waited for; matrix products, arithmetic and copies ran while one was open for 0% of the time, Pallas kernels for 0%

profile of v10, /device:TPU:1, one launch (start us, length us, event | category | flops | bytes accessed | tf_op | source)
XLA Modules:
  0.0 455.3 jit_solution(9738952935106739512)
XLA Ops:
  0.6 15.2 %copy.12 = f32[4,32,64,512]{3,1,0,2:T(8,128)S(1)} copy(f32[4,32,64,512]{3,2,1,0:T(8,128)} %param.1) | data formatting | bytes 33554432 | tf_op args[0]
  15.9 193.1 %all_to_all.43 = f32[4,32,64,512]{3,1,0,2:T(8,128)S(1)} all-to-all(f32[4,32,64,512]{3,1,0,2:T(8,128)S(1)} %copy.12), channel_id=1, replica_groups=mesh['gz'=16,'gy'=8] {'gz'}, dimensions={2} | all-to-all | bytes 33554432 | tf_op jit(solution)/shard_map/all_to_all | solution.py:180
  208.9 1.9 copy.20
  210.8 5.4 %fusion.3 = (f32[1,16,32,4,512]{4,2,1,0,3:T(8,128)S(1)}, f32[1,16,32,4,512]{4,2,1,0,3:T(8,128)}, f32[1,16,32,4,512]{4,2,1,0,3:T(8,128)}, f32[1,16,32,4,512]{4,2,1,0,3:T(8,128)}) fusion(f32[4,16,32,4,512]{4,2,1,0,3:T(8,128)S(1)} %bitcast.44), kind=kLoop, calls=%fused_computation.13 | loop fusion | bytes 33554432 | tf_op jit(solution)/shard_map/slice | solution.py:184
  216.2 4.4 copy-done.1
  220.7 7.4 %convolution_bitcast_fusion.1 = f32[512,512]{1,0:T(8,128)S(1)} fusion(f32[512,4,512]{2,0,1:T(8,128)} %bitcast.50), kind=kOutput, calls=%fused_computation.1 | convolution fusion | flops 3221225472 | bytes 5242880 | tf_op jit(solution)/shard_map/dot_general | solution.py:35
  228.0 3.6 convolution_bitcast_fusion.2
  231.7 3.6 fusion.1
  235.3 3.6 fusion.2
  239.2 26.2 %all_to_all.44 = f32[128,4,512]{2,1,0:T(4,128)S(1)} all-to-all(f32[128,4,512]{2,1,0:T(4,128)S(1)} %reshape.100), channel_id=1, replica_groups=mesh['gz'=16,'gy'=8] {'gz','gy'}, dimensions={0} | all-to-all | bytes 2097152 | tf_op jit(solution)/shard_map/all_to_all | solution.py:44
  266.8 4.5 all-to-all-start.2
  271.4 1.6 multiply_cosine_fusion
  273.0 17.7 %all-to-all-done.2 = f32[128,4,512]{2,1,0:T(4,128)S(1)} async-done(((f32[128,4,512]{2,1,0:T(4,128)}), f32[128,4,512]{2,1,0:T(4,128)S(1)}, u32[]{:S(2)}, u32[]{:S(2)}) %all-to-all-start.2) | async-done | bytes 1048608 | tf_op jit(solution)/shard_map/all_to_all | solution.py:49
  290.8 1.3 reshape.101.g_ref
  292.1 26.6 %shard_map.38.bz_ref = f32[64,512]{1,0:T(8,128)} custom-call(f32[512,512]{1,0:T(8,128)} %reshape.101.g_ref, f32[64,512]{1,0:T(8,128)} %get-tuple-element.16.q_ref), custom_call_target="tpu_custom_call" | custom-call | tf_op jit(solution)/shard_map/pallas_call | solution.py:88
  319.6 10.8 %shard_map.39 = f32[128,1,4096]{2,1,0:T(1,128)S(1)} custom-call(f32[4,4,512,512]{3,2,1,0:T(8,128)} %bitcast.45, f32[64,512]{1,0:T(8,128)S(1)} %copy-done), custom_call_target="tpu_custom_call" | custom-call | tf_op jit(solution)/shard_map/pallas_call | solution.py:116
  330.4 35.0 %all_to_all.45.m_ref = f32[128,1,4096]{2,1,0:T(1,128)} all-to-all(f32[128,1,4096]{2,1,0:T(1,128)S(1)} %shard_map.39), channel_id=1, replica_groups=mesh['gz'=16,'gy'=8] {'gz','gy'}, dimensions={0} | all-to-all | bytes 4194304 | tf_op jit(solution)/shard_map/all_to_all | solution.py:189
  365.4 6.2 %shard_map.40 = f32[512,512]{1,0:T(8,128)} custom-call(f32[128,1,4096]{2,1,0:T(1,128)} %all_to_all.45.m_ref), custom_call_target="tpu_custom_call" | custom-call | tf_op jit(solution)/shard_map/pallas_call | solution.py:141
  371.7 1.5 reshape.102
  373.2 23.2 %all_to_all.46 = f32[128,4,512]{2,1,0:T(4,128)S(1)} all-to-all(f32[128,4,512]{2,1,0:T(4,128)S(1)} %reshape.102), channel_id=1, replica_groups=mesh['gz'=16,'gy'=8] {'gz','gy'}, dimensions={0} | all-to-all | bytes 2097152 | tf_op jit(solution)/shard_map/all_to_all | solution.py:44
  396.8 23.5 %all_to_all.47 = f32[128,4,512]{2,1,0:T(4,128)S(1)} all-to-all(f32[128,4,512]{2,1,0:T(4,128)S(1)} %broadcast_in_dim.5), channel_id=1, replica_groups=mesh['gz'=16,'gy'=8] {'gz','gy'}, dimensions={0} | all-to-all | bytes 2097152 | tf_op jit(solution)/shard_map/all_to_all | solution.py:49
  420.3 1.4 reshape.103.g_ref
  421.6 26.6 %shard_map.41.b_ref = f32[64,512]{1,0:T(8,128)} custom-call(f32[512,512]{1,0:T(8,128)} %reshape.103.g_ref, f32[64,512]{1,0:T(8,128)} %get-tuple-element.15.q_ref), custom_call_target="tpu_custom_call" | custom-call | tf_op jit(solution)/shard_map/pallas_call | solution.py:88
  448.2 3.4 shard_map.42
  (24 shorter events, 6.5 us)
Async XLA Ops:
  210.8 9.8 %copy-start.1 = (f32[4,32,16,4,512]{4,1,2,0,3:T(8,128)}, f32[4,32,16,4,512]{4,1,2,0,3:T(8,128)S(1)}, u32[]{:S(2)}) copy-start(f32[4,32,16,4,512]{4,1,2,0,3:T(8,128)S(1)} %copy.20) | copy-start | bytes 50331652
  220.6 7.4 %copy-start.3 = (f32[1,16,32,4,512]{4,2,1,0,3:T(8,128)S(1)}, f32[1,16,32,4,512]{4,2,1,0,3:T(8,128)}, u32[]{:S(2)}) copy-start(f32[1,16,32,4,512]{4,2,1,0,3:T(8,128)} %get-tuple-element.11) | copy-start | bytes 12582916
  228.0 3.6 copy-start.2
  266.8 24.0 %all-to-all-start.2 = ((f32[128,4,512]{2,1,0:T(4,128)}), f32[128,4,512]{2,1,0:T(4,128)S(1)}, u32[]{:S(2)}, u32[]{:S(2)}) async-start(f32[128,4,512]{2,1,0:T(4,128)} %broadcast_in_dim.4), calls=%async_computation.2 | async-start | bytes 2097152 | tf_op jit(solution)/shard_map/all_to_all | solution.py:49
  318.7 0.9 copy-start
  448.2 5.9 %copy-start.4 = (f32[64,512]{1,0:T(8,128)S(1)}, f32[64,512]{1,0:T(8,128)}, u32[]{:S(2)}) copy-start(f32[64,512]{1,0:T(8,128)} %shard_map.41.b_ref) | copy-start | bytes 393220

commit v11 on v10

--- a/solution.py
+++ b/solution.py
@@ -95,11 +95,13 @@
 
 def _reduce_kernel(count, x_part, rank, fib_ref, bz_ref, out_ref, t_ref):
     y = pl.program_id(0)
-    species = fib_ref.shape[1]
+    species = fib_ref.shape[2]
     per = 128 // rank
     for s in range(species):
+        block = fib_ref[:, 0, s]
+        block = block.reshape(block.shape[0] * block.shape[1], block.shape[2])
         t_ref[s // per, :, (s % per) * rank : (s % per + 1) * rank] = jnp.dot(
-            bz_ref[...], fib_ref[0, s],
+            bz_ref[...], block,
             precision=lax.Precision.HIGH, preferred_element_type=jnp.float32).T
     width = species * rank
     for xl in range(x_part):
@@ -110,19 +112,44 @@
 
 
 def reduce_send(fib_ys, basis_z, count):
-    ys, species, zs, xs = fib_ys.shape
+    blocks, ys, species, z_local, xs = fib_ys.shape
+    zs = blocks * z_local
     rank = basis_z.shape[1]
     x_part = xs // count
     return pl.pallas_call(
         functools.partial(_reduce_kernel, count, x_part, rank),
         grid=(ys,),
-        in_specs=[pl.BlockSpec((1, species, zs, xs), lambda y: (y, 0, 0, 0)),
+        in_specs=[pl.BlockSpec((blocks, 1, species, z_local, xs), lambda y: (0, y, 0, 0, 0)),
                   pl.BlockSpec((rank, zs), lambda y: (0, 0))],
         out_specs=pl.BlockSpec((count, 1, ys * x_part * species * rank), lambda y: (0, 0, 0)),
         out_shape=jax.ShapeDtypeStruct((count, 1, ys * x_part * species * rank), jnp.float32),
         scratch_shapes=[pltpu.VMEM((species * rank // 128, xs, 128), jnp.float32)],
         compiler_params=pltpu.CompilerParams(vmem_limit_bytes=48 * 1024 * 1024),
     )(fib_ys, basis_z.T)
+
+
+def _gram_z_kernel(fib_ref, g_ref):
+    @pl.when((pl.program_id(0) == 0) & (pl.program_id(1) == 0))
+    def _():
+        g_ref[...] = jnp.zeros_like(g_ref)
+
+    block = fib_ref[:, 0, 0]
+    block = block.reshape(block.shape[0] * block.shape[1], block.shape[2])
+    g_ref[...] += lax.dot_general(block, block, (((1,), (1,)), ((), ())),
+                                  precision=lax.Precision.HIGH,
+                                  preferred_element_type=jnp.float32)
+
+
+def gram_z_pallas(fib):
+    blocks, ys, species, z_local, xs = fib.shape
+    size = blocks * z_local
+    return pl.pallas_call(
+        _gram_z_kernel,
+        grid=(ys, species),
+        in_specs=[pl.BlockSpec((blocks, 1, 1, z_local, xs), lambda y, s: (0, y, s, 0, 0))],
+        out_specs=pl.BlockSpec((size, size), lambda y, s: (0, 0)),
+        out_shape=jax.ShapeDtypeStruct((size, size), jnp.float32),
+    )(fib)
 
 
 def _gram_y_kernel(y_local, m_ref, g_ref):
@@ -179,13 +206,12 @@
     count = count_gz * count_gy
     fibres = lax.all_to_all(species_field, "gz", split_axis=2, concat_axis=1, tiled=True)
     species, _, y_local, x_size = fibres.shape
-    gram_z = None
-    for one in range(species):
-        term = mode_products(fibres[one : one + 1], fibres[one : one + 1], 1)
-        gram_z = term if gram_z is None else gram_z + term
+    fib5 = fibres.reshape(species, count_gz, -1, y_local, x_size)
+    fib5 = jnp.transpose(fib5, (1, 3, 0, 2, 4))
+    gram_z = gram_z_pallas(fib5)
     basis_z = leaf_basis(gram_z, start_table(GRID, RANK))
     x_part = x_size // count
-    send = reduce_send(jnp.transpose(fibres, (2, 0, 1, 3)), basis_z, count)
+    send = reduce_send(fib5, basis_z, count)
     mixed = lax.all_to_all(send, ("gz", "gy"), 0, 0, tiled=True)
     gram_y = gram_y_pallas(mixed, y_local)
     start_y = start_table(GRID, RANK).reshape(count_gy, count_gz, y_local, RANK)

time: 461 us -> 454 us (0.985)
  Pallas kernels: 73.6 us -> 93.8 us
  matrix products: 18.2 us -> 0 us
  local copies, waits for them, and re-layouts: 37.3 us -> 27.7 us
    pallas_call x0 -> x1, Pallas kernels: none -> 20.5 us  [gram_z_pallas(): pl.pallas_call(_gram_z_kernel, grid=(ys, species), in_specs=[pl.BlockSpec...]
    dot_general x4 -> x0, matrix products: 18.2 us -> none  [mode_products(): lax.dot_general(left, right, ((others, others), ((), ())), precision=lax....]
    slice x1 -> x0, local copies, waits for them, and re-layouts: 5.41 us -> none  [body(): term = mode_products(fibres[one:one + 1], fibres[one:one + 1], 1)]
    unnamed x12 -> x4, local copies, waits for them, and re-layouts: 21.3 us -> 16.9 us
where the time goes in v11:
time: 454 us; the launch traced here: 448 us
  blocking collectives  301 us (66%)
  Pallas kernels  93.8 us (21%)
  local copies, waits for them, and re-layouts  27.7 us (6%)
  waiting for transfers between devices  17.6 us (4%)
  starting transfers between devices  4.91 us (1%)
    all_to_all x1, blocking collectives, body(): lax.all_to_all(species_field, 'gz', split_axis=2, concat_axis=1, tiled=True)  193 us
    pallas_call x2, Pallas kernels, basis_pallas(): pl.pallas_call(functools.partial(_basis_kernel, iters), out_shape=jax.Sha...  53.2 us
    all_to_all x2, blocking collectives, sum_over_mesh(): lax.all_to_all(gram.reshape(count, rows // count, rows), axes, 0, 0, tile...  49.4 us
    all_to_all x1, blocking collectives, body(): mixed = lax.all_to_all(send, ('gz', 'gy'), 0, 0, tiled=True)  35 us
    all_to_all x1, blocking collectives, sum_over_mesh(): return lax.all_to_all(tiled, axes, 0, 0, tiled=True).reshape(rows, rows)  23.5 us
    pallas_call x1, Pallas kernels, gram_z_pallas(): pl.pallas_call(_gram_z_kernel, grid=(ys, species), in_specs=[pl.BlockSpec...  20.5 us
    all_to_all x1, waiting for transfers between devices, sum_over_mesh(): return lax.all_to_all(tiled, axes, 0, 0, tiled=True).reshape(rows, rows)  17.6 us
    unnamed x4, local copies, waits for them, and re-layouts  16.9 us
  transfers between devices with their start and end apart: 1, of which 1 were waited for; matrix products, arithmetic and copies ran while one was open for 0% of the time, Pallas kernels for 0%

profile of v11, /device:TPU:1, one launch (start us, length us, event | category | flops | bytes accessed | tf_op | source)
XLA Modules:
  0.0 448.1 jit_solution(340298298901251611)
XLA Ops:
  0.6 15.2 %copy.12 = f32[4,32,64,512]{3,1,0,2:T(8,128)S(1)} copy(f32[4,32,64,512]{3,2,1,0:T(8,128)} %param.1) | data formatting | bytes 33554432 | tf_op args[0]
  15.9 193.2 %all_to_all.37 = f32[4,32,64,512]{3,1,0,2:T(8,128)} all-to-all(f32[4,32,64,512]{3,1,0,2:T(8,128)S(1)} %copy.12), channel_id=1, replica_groups=mesh['gz'=16,'gy'=8] {'gz'}, dimensions={2} | all-to-all | bytes 33554432 | tf_op jit(solution)/shard_map/all_to_all | solution.py:207
  209.0 20.5 %shard_map.38 = f32[512,512]{1,0:T(8,128)} custom-call(f32[16,4,4,32,512]{4,3,2,1,0:T(8,128)} %bitcast.13), custom_call_target="tpu_custom_call" | custom-call | tf_op jit(solution)/shard_map/pallas_call | solution.py:146
  229.5 1.5 reshape.70
  231.1 26.2 %all_to_all.38 = f32[128,4,512]{2,1,0:T(4,128)S(1)} all-to-all(f32[128,4,512]{2,1,0:T(4,128)S(1)} %reshape.70), channel_id=1, replica_groups=mesh['gz'=16,'gy'=8] {'gz','gy'}, dimensions={0} | all-to-all | bytes 2097152 | tf_op jit(solution)/shard_map/all_to_all | solution.py:44
  257.5 1.1 broadcast_in_dim.4
  258.6 4.9 %all-to-all-start.2 = ((f32[128,4,512]{2,1,0:T(4,128)}), f32[128,4,512]{2,1,0:T(4,128)S(1)}, u32[]{:S(2)}, u32[]{:S(2)}) async-start(f32[128,4,512]{2,1,0:T(4,128)} %broadcast_in_dim.4), calls=%async_computation.2 | async-start | bytes 2097152 | tf_op jit(solution)/shard_map/all_to_all | solution.py:49
  263.7 1.6 multiply_cosine_fusion
  265.3 17.6 %all-to-all-done.2 = f32[128,4,512]{2,1,0:T(4,128)S(1)} async-done(((f32[128,4,512]{2,1,0:T(4,128)}), f32[128,4,512]{2,1,0:T(4,128)S(1)}, u32[]{:S(2)}, u32[]{:S(2)}) %all-to-all-start.2) | async-done | bytes 1048608 | tf_op jit(solution)/shard_map/all_to_all | solution.py:49
  282.9 1.4 reshape.71.g_ref
  284.3 26.6 %shard_map.39.bz_ref = f32[64,512]{1,0:T(8,128)} custom-call(f32[512,512]{1,0:T(8,128)} %reshape.71.g_ref, f32[64,512]{1,0:T(8,128)} %get-tuple-element.10.q_ref), custom_call_target="tpu_custom_call" | custom-call | tf_op jit(solution)/shard_map/pallas_call | solution.py:88
  310.9 0.9 copy-done
  311.8 10.6 %shard_map.40 = f32[128,1,4096]{2,1,0:T(1,128)S(1)} custom-call(f32[16,4,4,32,512]{4,3,2,1,0:T(8,128)} %bitcast.14, f32[64,512]{1,0:T(8,128)S(1)} %copy-done), custom_call_target="tpu_custom_call" | custom-call | tf_op jit(solution)/shard_map/pallas_call | solution.py:119
  322.4 35.0 %all_to_all.39.m_ref = f32[128,1,4096]{2,1,0:T(1,128)} all-to-all(f32[128,1,4096]{2,1,0:T(1,128)S(1)} %shard_map.40), channel_id=1, replica_groups=mesh['gz'=16,'gy'=8] {'gz','gy'}, dimensions={0} | all-to-all | bytes 4194304 | tf_op jit(solution)/shard_map/all_to_all | solution.py:215
  357.3 6.2 %shard_map.41 = f32[512,512]{1,0:T(8,128)} custom-call(f32[128,1,4096]{2,1,0:T(1,128)} %all_to_all.39.m_ref), custom_call_target="tpu_custom_call" | custom-call | tf_op jit(solution)/shard_map/pallas_call | solution.py:168
  363.6 1.5 reshape.72
  365.1 23.2 %all_to_all.40 = f32[128,4,512]{2,1,0:T(4,128)S(1)} all-to-all(f32[128,4,512]{2,1,0:T(4,128)S(1)} %reshape.72), channel_id=1, replica_groups=mesh['gz'=16,'gy'=8] {'gz','gy'}, dimensions={0} | all-to-all | bytes 2097152 | tf_op jit(solution)/shard_map/all_to_all | solution.py:44
  388.6 23.5 %all_to_all.41 = f32[128,4,512]{2,1,0:T(4,128)S(1)} all-to-all(f32[128,4,512]{2,1,0:T(4,128)S(1)} %broadcast_in_dim.5), channel_id=1, replica_groups=mesh['gz'=16,'gy'=8] {'gz','gy'}, dimensions={0} | all-to-all | bytes 2097152 | tf_op jit(solution)/shard_map/all_to_all | solution.py:49
  412.1 1.3 reshape.73.g_ref
  413.5 26.6 %shard_map.42.b_ref = f32[64,512]{1,0:T(8,128)} custom-call(f32[512,512]{1,0:T(8,128)} %reshape.73.g_ref, f32[64,512]{1,0:T(8,128)} %get-tuple-element.9.q_ref), custom_call_target="tpu_custom_call" | custom-call | tf_op jit(solution)/shard_map/pallas_call | solution.py:88
  440.1 3.3 shard_map.43
  443.4 1.3 reshape.74
  445.0 0.9 reshape.75
  445.9 1.0 copy.14
  (11 shorter events, 1.9 us)
Async XLA Ops:
  258.6 24.3 %all-to-all-start.2 = ((f32[128,4,512]{2,1,0:T(4,128)}), f32[128,4,512]{2,1,0:T(4,128)S(1)}, u32[]{:S(2)}, u32[]{:S(2)}) async-start(f32[128,4,512]{2,1,0:T(4,128)} %broadcast_in_dim.4), calls=%async_computation.2 | async-start | bytes 2097152 | tf_op jit(solution)/shard_map/all_to_all | solution.py:49
  310.9 0.9 copy-start

commit v12 on v11

--- a/solution.py
+++ b/solution.py
@@ -129,15 +129,26 @@
 
 
 def _gram_z_kernel(fib_ref, g_ref):
-    @pl.when((pl.program_id(0) == 0) & (pl.program_id(1) == 0))
+    first = (pl.program_id(0) == 0) & (pl.program_id(1) == 0)
+    last = (pl.program_id(0) == pl.num_programs(0) - 1) & (
+        pl.program_id(1) == pl.num_programs(1) - 1)
+
+    @pl.when(first)
     def _():
         g_ref[...] = jnp.zeros_like(g_ref)
 
     block = fib_ref[:, 0, 0]
     block = block.reshape(block.shape[0] * block.shape[1], block.shape[2])
-    g_ref[...] += lax.dot_general(block, block, (((1,), (1,)), ((), ())),
-                                  precision=lax.Precision.HIGH,
-                                  preferred_element_type=jnp.float32)
+    half = block.shape[0] // 2
+    for a, b in ((0, 0), (0, 1), (1, 1)):
+        g_ref[a * half : (a + 1) * half, b * half : (b + 1) * half] += lax.dot_general(
+            block[a * half : (a + 1) * half], block[b * half : (b + 1) * half],
+            (((1,), (1,)), ((), ())), precision=lax.Precision.HIGH,
+            preferred_element_type=jnp.float32)
+
+    @pl.when(last)
+    def _():
+        g_ref[half:, :half] = g_ref[:half, half:].T
 
 
 def gram_z_pallas(fib):

time: 454 us -> 453 us (level)
  no operation moved by 1% of the time
where the time goes in v12:
time: 453 us; the launch traced here: 447 us
  blocking collectives  301 us (66%)
  Pallas kernels  92.4 us (20%)
  local copies, waits for them, and re-layouts  27.7 us (6%)
  waiting for transfers between devices  17.6 us (4%)
  starting transfers between devices  4.91 us (1%)
    all_to_all x1, blocking collectives, body(): lax.all_to_all(species_field, 'gz', split_axis=2, concat_axis=1, tiled=True)  193 us
    pallas_call x2, Pallas kernels, basis_pallas(): pl.pallas_call(functools.partial(_basis_kernel, iters), out_shape=jax.Sha...  53.2 us
    all_to_all x2, blocking collectives, sum_over_mesh(): lax.all_to_all(gram.reshape(count, rows // count, rows), axes, 0, 0, tile...  49.4 us
    all_to_all x1, blocking collectives, body(): mixed = lax.all_to_all(send, ('gz', 'gy'), 0, 0, tiled=True)  35 us
    all_to_all x1, blocking collectives, sum_over_mesh(): return lax.all_to_all(tiled, axes, 0, 0, tiled=True).reshape(rows, rows)  23.5 us
    pallas_call x1, Pallas kernels, gram_z_pallas(): pl.pallas_call(_gram_z_kernel, grid=(ys, species), in_specs=[pl.BlockSpec...  19.1 us
    all_to_all x1, waiting for transfers between devices, sum_over_mesh(): return lax.all_to_all(tiled, axes, 0, 0, tiled=True).reshape(rows, rows)  17.6 us
    unnamed x4, local copies, waits for them, and re-layouts  16.9 us
  transfers between devices with their start and end apart: 1, of which 1 were waited for; matrix products, arithmetic and copies ran while one was open for 0% of the time, Pallas kernels for 0%

profile of v12, /device:TPU:1, one launch (start us, length us, event | category | flops | bytes accessed | tf_op | source)
XLA Modules:
  0.0 446.7 jit_solution(5649430497443445130)
XLA Ops:
  0.6 15.2 %copy.12 = f32[4,32,64,512]{3,1,0,2:T(8,128)S(1)} copy(f32[4,32,64,512]{3,2,1,0:T(8,128)} %param.1) | data formatting | bytes 33554432 | tf_op args[0]
  15.9 193.2 %all_to_all.37 = f32[4,32,64,512]{3,1,0,2:T(8,128)} all-to-all(f32[4,32,64,512]{3,1,0,2:T(8,128)S(1)} %copy.12), channel_id=1, replica_groups=mesh['gz'=16,'gy'=8] {'gz'}, dimensions={2} | all-to-all | bytes 33554432 | tf_op jit(solution)/shard_map/all_to_all | solution.py:218
  209.0 19.1 %shard_map.38 = f32[512,512]{1,0:T(8,128)} custom-call(f32[16,4,4,32,512]{4,3,2,1,0:T(8,128)} %bitcast.13), custom_call_target="tpu_custom_call" | custom-call | tf_op jit(solution)/shard_map/pallas_call | solution.py:157
  228.1 1.5 reshape.70
  229.7 26.2 %all_to_all.38 = f32[128,4,512]{2,1,0:T(4,128)S(1)} all-to-all(f32[128,4,512]{2,1,0:T(4,128)S(1)} %reshape.70), channel_id=1, replica_groups=mesh['gz'=16,'gy'=8] {'gz','gy'}, dimensions={0} | all-to-all | bytes 2097152 | tf_op jit(solution)/shard_map/all_to_all | solution.py:44
  256.1 1.1 broadcast_in_dim.4
  257.2 4.9 %all-to-all-start.2 = ((f32[128,4,512]{2,1,0:T(4,128)}), f32[128,4,512]{2,1,0:T(4,128)S(1)}, u32[]{:S(2)}, u32[]{:S(2)}) async-start(f32[128,4,512]{2,1,0:T(4,128)} %broadcast_in_dim.4), calls=%async_computation.2 | async-start | bytes 2097152 | tf_op jit(solution)/shard_map/all_to_all | solution.py:49
  262.3 1.6 multiply_cosine_fusion
  263.9 17.6 %all-to-all-done.2 = f32[128,4,512]{2,1,0:T(4,128)S(1)} async-done(((f32[128,4,512]{2,1,0:T(4,128)}), f32[128,4,512]{2,1,0:T(4,128)S(1)}, u32[]{:S(2)}, u32[]{:S(2)}) %all-to-all-start.2) | async-done | bytes 1048608 | tf_op jit(solution)/shard_map/all_to_all | solution.py:49
  281.5 1.4 reshape.71.g_ref
  282.8 26.6 %shard_map.39.bz_ref = f32[64,512]{1,0:T(8,128)} custom-call(f32[512,512]{1,0:T(8,128)} %reshape.71.g_ref, f32[64,512]{1,0:T(8,128)} %get-tuple-element.10.q_ref), custom_call_target="tpu_custom_call" | custom-call | tf_op jit(solution)/shard_map/pallas_call | solution.py:88
  309.4 0.9 copy-done
  310.3 10.6 %shard_map.40 = f32[128,1,4096]{2,1,0:T(1,128)S(1)} custom-call(f32[16,4,4,32,512]{4,3,2,1,0:T(8,128)} %bitcast.14, f32[64,512]{1,0:T(8,128)S(1)} %copy-done), custom_call_target="tpu_custom_call" | custom-call | tf_op jit(solution)/shard_map/pallas_call | solution.py:119
  321.0 35.0 %all_to_all.39.m_ref = f32[128,1,4096]{2,1,0:T(1,128)} all-to-all(f32[128,1,4096]{2,1,0:T(1,128)S(1)} %shard_map.40), channel_id=1, replica_groups=mesh['gz'=16,'gy'=8] {'gz','gy'}, dimensions={0} | all-to-all | bytes 4194304 | tf_op jit(solution)/shard_map/all_to_all | solution.py:226
  355.9 6.2 %shard_map.41 = f32[512,512]{1,0:T(8,128)} custom-call(f32[128,1,4096]{2,1,0:T(1,128)} %all_to_all.39.m_ref), custom_call_target="tpu_custom_call" | custom-call | tf_op jit(solution)/shard_map/pallas_call | solution.py:179
  362.1 1.5 reshape.72
  363.7 23.2 %all_to_all.40 = f32[128,4,512]{2,1,0:T(4,128)S(1)} all-to-all(f32[128,4,512]{2,1,0:T(4,128)S(1)} %reshape.72), channel_id=1, replica_groups=mesh['gz'=16,'gy'=8] {'gz','gy'}, dimensions={0} | all-to-all | bytes 2097152 | tf_op jit(solution)/shard_map/all_to_all | solution.py:44
  387.2 23.5 %all_to_all.41 = f32[128,4,512]{2,1,0:T(4,128)S(1)} all-to-all(f32[128,4,512]{2,1,0:T(4,128)S(1)} %broadcast_in_dim.5), channel_id=1, replica_groups=mesh['gz'=16,'gy'=8] {'gz','gy'}, dimensions={0} | all-to-all | bytes 2097152 | tf_op jit(solution)/shard_map/all_to_all | solution.py:49
  410.7 1.3 reshape.73.g_ref
  412.1 26.6 %shard_map.42.b_ref = f32[64,512]{1,0:T(8,128)} custom-call(f32[512,512]{1,0:T(8,128)} %reshape.73.g_ref, f32[64,512]{1,0:T(8,128)} %get-tuple-element.9.q_ref), custom_call_target="tpu_custom_call" | custom-call | tf_op jit(solution)/shard_map/pallas_call | solution.py:88
  438.7 3.3 shard_map.43
  442.0 1.3 reshape.74
  443.6 0.9 reshape.75
  444.5 1.0 copy.14
  (11 shorter events, 1.9 us)
Async XLA Ops:
  257.2 24.3 %all-to-all-start.2 = ((f32[128,4,512]{2,1,0:T(4,128)}), f32[128,4,512]{2,1,0:T(4,128)S(1)}, u32[]{:S(2)}, u32[]{:S(2)}) async-start(f32[128,4,512]{2,1,0:T(4,128)} %broadcast_in_dim.4), calls=%async_computation.2 | async-start | bytes 2097152 | tf_op jit(solution)/shard_map/all_to_all | solution.py:49
  309.4 0.9 copy-start

commit v13 on v12

--- a/solution.py
+++ b/solution.py
@@ -75,10 +75,10 @@
     gram = g_ref[...]
     basis_t = q_ref[...]
     for _ in range(iters):
-        product_t = jnp.dot(basis_t, gram, precision=lax.Precision.HIGHEST, preferred_element_type=jnp.float32)
+        product_t = jnp.dot(basis_t, gram, precision=lax.Precision.HIGH, preferred_element_type=jnp.float32)
         inner = lax.dot_general(product_t, product_t, (((1,), (1,)), ((), ())),
-                                precision=lax.Precision.HIGHEST, preferred_element_type=jnp.float32)
-        basis_t = jnp.dot(_eliminate(inner), product_t, precision=lax.Precision.HIGHEST,
+                                precision=lax.Precision.HIGH, preferred_element_type=jnp.float32)
+        basis_t = jnp.dot(_eliminate(inner), product_t, precision=lax.Precision.HIGH,
                           preferred_element_type=jnp.float32)
     out_ref[...] = basis_t
 
@@ -168,10 +168,14 @@
     width = m_ref.shape[2] // y_local
     parts = [m_ref[:, 0, a * width : (a + 1) * width] for a in range(y_local)]
     for a in range(y_local):
-        for b in range(y_local):
+        for b in range(a, y_local):
             g_ref[a * count : (a + 1) * count, b * count : (b + 1) * count] = lax.dot_general(
                 parts[a], parts[b], (((1,), (1,)), ((), ())),
                 precision=lax.Precision.HIGH, preferred_element_type=jnp.float32)
+    for a in range(y_local):
+        for b in range(a):
+            g_ref[a * count : (a + 1) * count, b * count : (b + 1) * count] = (
+                g_ref[b * count : (b + 1) * count, a * count : (a + 1) * count].T)
 
 
 def gram_y_pallas(mixed, y_local):

time: 453 us -> 443 us (0.978); the launches traced: 447 us -> 442 us
  no operation moved by 1% of the time
where the time goes in v13:
time: 443 us; the launch traced here: 442 us
  blocking collectives  301 us (68%)
  Pallas kernels  88.2 us (20%)
  local copies, waits for them, and re-layouts  27.7 us (6%)
  waiting for transfers between devices  17.7 us (4%)
    all_to_all x1, blocking collectives, body(): lax.all_to_all(species_field, 'gz', split_axis=2, concat_axis=1, tiled=True)  193 us
    pallas_call x2, Pallas kernels, basis_pallas(): pl.pallas_call(functools.partial(_basis_kernel, iters), out_shape=jax.Sha...  50.3 us
    all_to_all x2, blocking collectives, sum_over_mesh(): lax.all_to_all(gram.reshape(count, rows // count, rows), axes, 0, 0, tile...  49.4 us
    all_to_all x1, blocking collectives, body(): mixed = lax.all_to_all(send, ('gz', 'gy'), 0, 0, tiled=True)  35.2 us
    all_to_all x1, blocking collectives, sum_over_mesh(): return lax.all_to_all(tiled, axes, 0, 0, tiled=True).reshape(rows, rows)  23.5 us
    pallas_call x1, Pallas kernels, gram_z_pallas(): pl.pallas_call(_gram_z_kernel, grid=(ys, species), in_specs=[pl.BlockSpec...  19.1 us
    all_to_all x1, waiting for transfers between devices, sum_over_mesh(): return lax.all_to_all(tiled, axes, 0, 0, tiled=True).reshape(rows, rows)  17.7 us
    unnamed x4, local copies, waits for them, and re-layouts  16.9 us
  transfers between devices with their start and end apart: 1, of which 1 were waited for; matrix products, arithmetic and copies ran while one was open for 0% of the time, Pallas kernels for 0%

profile of v13, /device:TPU:1, one launch (start us, length us, event | category | flops | bytes accessed | tf_op | source)
XLA Modules:
  0.0 442.0 jit_solution(16952429823515573440)
XLA Ops:
  0.6 15.2 %copy.12 = f32[4,32,64,512]{3,1,0,2:T(8,128)S(1)} copy(f32[4,32,64,512]{3,2,1,0:T(8,128)} %param.1) | data formatting | bytes 33554432 | tf_op args[0]
  15.9 193.2 %all_to_all.37 = f32[4,32,64,512]{3,1,0,2:T(8,128)} all-to-all(f32[4,32,64,512]{3,1,0,2:T(8,128)S(1)} %copy.12), channel_id=1, replica_groups=mesh['gz'=16,'gy'=8] {'gz'}, dimensions={2} | all-to-all | bytes 33554432 | tf_op jit(solution)/shard_map/all_to_all | solution.py:222
  209.0 19.1 %shard_map.38 = f32[512,512]{1,0:T(8,128)} custom-call(f32[16,4,4,32,512]{4,3,2,1,0:T(8,128)} %bitcast.13), custom_call_target="tpu_custom_call" | custom-call | tf_op jit(solution)/shard_map/pallas_call | solution.py:157
  228.1 1.5 reshape.70
  229.6 26.2 %all_to_all.38 = f32[128,4,512]{2,1,0:T(4,128)S(1)} all-to-all(f32[128,4,512]{2,1,0:T(4,128)S(1)} %reshape.70), channel_id=1, replica_groups=mesh['gz'=16,'gy'=8] {'gz','gy'}, dimensions={0} | all-to-all | bytes 2097152 | tf_op jit(solution)/shard_map/all_to_all | solution.py:44
  256.1 1.1 broadcast_in_dim.4
  257.2 4.3 all-to-all-start.2
  261.7 1.6 multiply_cosine_fusion
  263.3 17.7 %all-to-all-done.2 = f32[128,4,512]{2,1,0:T(4,128)S(1)} async-done(((f32[128,4,512]{2,1,0:T(4,128)}), f32[128,4,512]{2,1,0:T(4,128)S(1)}, u32[]{:S(2)}, u32[]{:S(2)}) %all-to-all-start.2) | async-done | bytes 1048608 | tf_op jit(solution)/shard_map/all_to_all | solution.py:49
  281.0 1.4 reshape.71.g_ref
  282.4 25.2 %shard_map.39.bz_ref = f32[64,512]{1,0:T(8,128)} custom-call(f32[512,512]{1,0:T(8,128)} %reshape.71.g_ref, f32[64,512]{1,0:T(8,128)} %get-tuple-element.10.q_ref), custom_call_target="tpu_custom_call" | custom-call | tf_op jit(solution)/shard_map/pallas_call | solution.py:88
  307.5 0.9 copy-done
  308.4 10.4 %shard_map.40 = f32[128,1,4096]{2,1,0:T(1,128)S(1)} custom-call(f32[16,4,4,32,512]{4,3,2,1,0:T(8,128)} %bitcast.14, f32[64,512]{1,0:T(8,128)S(1)} %copy-done), custom_call_target="tpu_custom_call" | custom-call | tf_op jit(solution)/shard_map/pallas_call | solution.py:119
  318.9 35.2 %all_to_all.39.m_ref = f32[128,1,4096]{2,1,0:T(1,128)} all-to-all(f32[128,1,4096]{2,1,0:T(1,128)S(1)} %shard_map.40), channel_id=1, replica_groups=mesh['gz'=16,'gy'=8] {'gz','gy'}, dimensions={0} | all-to-all | bytes 4194304 | tf_op jit(solution)/shard_map/all_to_all | solution.py:230
  354.1 5.1 %shard_map.41 = f32[512,512]{1,0:T(8,128)} custom-call(f32[128,1,4096]{2,1,0:T(1,128)} %all_to_all.39.m_ref), custom_call_target="tpu_custom_call" | custom-call | tf_op jit(solution)/shard_map/pallas_call | solution.py:183
  359.2 1.5 reshape.72
  360.7 23.2 %all_to_all.40 = f32[128,4,512]{2,1,0:T(4,128)S(1)} all-to-all(f32[128,4,512]{2,1,0:T(4,128)S(1)} %reshape.72), channel_id=1, replica_groups=mesh['gz'=16,'gy'=8] {'gz','gy'}, dimensions={0} | all-to-all | bytes 2097152 | tf_op jit(solution)/shard_map/all_to_all | solution.py:44
  384.2 23.5 %all_to_all.41 = f32[128,4,512]{2,1,0:T(4,128)S(1)} all-to-all(f32[128,4,512]{2,1,0:T(4,128)S(1)} %broadcast_in_dim.5), channel_id=1, replica_groups=mesh['gz'=16,'gy'=8] {'gz','gy'}, dimensions={0} | all-to-all | bytes 2097152 | tf_op jit(solution)/shard_map/all_to_all | solution.py:49
  407.7 1.3 reshape.73.g_ref
  409.1 25.1 %shard_map.42.b_ref = f32[64,512]{1,0:T(8,128)} custom-call(f32[512,512]{1,0:T(8,128)} %reshape.73.g_ref, f32[64,512]{1,0:T(8,128)} %get-tuple-element.9.q_ref), custom_call_target="tpu_custom_call" | custom-call | tf_op jit(solution)/shard_map/pallas_call | solution.py:88
  434.2 3.3 shard_map.43
  437.6 1.3 reshape.74
  439.1 0.9 reshape.75
  440.1 1.0 copy.14
  (11 shorter events, 1.9 us)
Async XLA Ops:
  257.2 23.8 %all-to-all-start.2 = ((f32[128,4,512]{2,1,0:T(4,128)}), f32[128,4,512]{2,1,0:T(4,128)S(1)}, u32[]{:S(2)}, u32[]{:S(2)}) async-start(f32[128,4,512]{2,1,0:T(4,128)} %broadcast_in_dim.4), calls=%async_computation.2 | async-start | bytes 2097152 | tf_op jit(solution)/shard_map/all_to_all | solution.py:49
  307.5 0.9 copy-start

commit v14 on v13

--- a/solution.py
+++ b/solution.py
@@ -67,7 +67,7 @@
         factor = jnp.where(row_col > j, col / pivot, 0.0)
         return (left - factor * row_l, right - factor * row_r, diag - factor * col)
 
-    _, right, diag = lax.fori_loop(0, n, step, (c, right, diag), unroll=64)
+    _, right, diag = lax.fori_loop(0, n, step, (c, right, diag), unroll=32)
     return right / jnp.sqrt(diag)
 
 

time: 443 us -> 445 us (level)
  no operation moved by 1% of the time
where the time goes in v14:
time: 445 us; the launch traced here: 444 us
  blocking collectives  301 us (68%)
  Pallas kernels  90 us (20%)
  local copies, waits for them, and re-layouts  27.7 us (6%)
  waiting for transfers between devices  17.7 us (4%)
    all_to_all x1, blocking collectives, body(): lax.all_to_all(species_field, 'gz', split_axis=2, concat_axis=1, tiled=True)  193 us
    pallas_call x2, Pallas kernels, basis_pallas(): pl.pallas_call(functools.partial(_basis_kernel, iters), out_shape=jax.Sha...  52.1 us
    all_to_all x2, blocking collectives, sum_over_mesh(): lax.all_to_all(gram.reshape(count, rows // count, rows), axes, 0, 0, tile...  49.4 us
    all_to_all x1, blocking collectives, body(): mixed = lax.all_to_all(send, ('gz', 'gy'), 0, 0, tiled=True)  35 us
    all_to_all x1, blocking collectives, sum_over_mesh(): return lax.all_to_all(tiled, axes, 0, 0, tiled=True).reshape(rows, rows)  23.5 us
    pallas_call x1, Pallas kernels, gram_z_pallas(): pl.pallas_call(_gram_z_kernel, grid=(ys, species), in_specs=[pl.BlockSpec...  19.1 us
    all_to_all x1, waiting for transfers between devices, sum_over_mesh(): return lax.all_to_all(tiled, axes, 0, 0, tiled=True).reshape(rows, rows)  17.7 us
    unnamed x4, local copies, waits for them, and re-layouts  16.9 us
  transfers between devices with their start and end apart: 1, of which 1 were waited for; matrix products, arithmetic and copies ran while one was open for 0% of the time, Pallas kernels for 0%

profile of v14, /device:TPU:1, one launch (start us, length us, event | category | flops | bytes accessed | tf_op | source)
XLA Modules:
  0.0 443.6 jit_solution(7474161117436459723)
XLA Ops:
  0.6 15.2 %copy.12 = f32[4,32,64,512]{3,1,0,2:T(8,128)S(1)} copy(f32[4,32,64,512]{3,2,1,0:T(8,128)} %param.1) | data formatting | bytes 33554432 | tf_op args[0]
  15.9 193.2 %all_to_all.37 = f32[4,32,64,512]{3,1,0,2:T(8,128)} all-to-all(f32[4,32,64,512]{3,1,0,2:T(8,128)S(1)} %copy.12), channel_id=1, replica_groups=mesh['gz'=16,'gy'=8] {'gz'}, dimensions={2} | all-to-all | bytes 33554432 | tf_op jit(solution)/shard_map/all_to_all | solution.py:222
  209.0 19.1 %shard_map.38 = f32[512,512]{1,0:T(8,128)} custom-call(f32[16,4,4,32,512]{4,3,2,1,0:T(8,128)} %bitcast.13), custom_call_target="tpu_custom_call" | custom-call | tf_op jit(solution)/shard_map/pallas_call | solution.py:157
  228.1 1.5 reshape.70
  229.6 26.2 %all_to_all.38 = f32[128,4,512]{2,1,0:T(4,128)S(1)} all-to-all(f32[128,4,512]{2,1,0:T(4,128)S(1)} %reshape.70), channel_id=1, replica_groups=mesh['gz'=16,'gy'=8] {'gz','gy'}, dimensions={0} | all-to-all | bytes 2097152 | tf_op jit(solution)/shard_map/all_to_all | solution.py:44
  256.1 1.1 broadcast_in_dim.4
  257.2 4.3 all-to-all-start.2
  261.7 1.6 multiply_cosine_fusion
  263.3 17.7 %all-to-all-done.2 = f32[128,4,512]{2,1,0:T(4,128)S(1)} async-done(((f32[128,4,512]{2,1,0:T(4,128)}), f32[128,4,512]{2,1,0:T(4,128)S(1)}, u32[]{:S(2)}, u32[]{:S(2)}) %all-to-all-start.2) | async-done | bytes 1048608 | tf_op jit(solution)/shard_map/all_to_all | solution.py:49
  281.0 1.4 reshape.71.g_ref
  282.4 26.1 %shard_map.39.bz_ref = f32[64,512]{1,0:T(8,128)} custom-call(f32[512,512]{1,0:T(8,128)} %reshape.71.g_ref, f32[64,512]{1,0:T(8,128)} %get-tuple-element.10.q_ref), custom_call_target="tpu_custom_call" | custom-call | tf_op jit(solution)/shard_map/pallas_call | solution.py:88
  308.4 0.9 copy-done
  309.3 10.4 %shard_map.40 = f32[128,1,4096]{2,1,0:T(1,128)S(1)} custom-call(f32[16,4,4,32,512]{4,3,2,1,0:T(8,128)} %bitcast.14, f32[64,512]{1,0:T(8,128)S(1)} %copy-done), custom_call_target="tpu_custom_call" | custom-call | tf_op jit(solution)/shard_map/pallas_call | solution.py:119
  319.8 35.0 %all_to_all.39.m_ref = f32[128,1,4096]{2,1,0:T(1,128)} all-to-all(f32[128,1,4096]{2,1,0:T(1,128)S(1)} %shard_map.40), channel_id=1, replica_groups=mesh['gz'=16,'gy'=8] {'gz','gy'}, dimensions={0} | all-to-all | bytes 4194304 | tf_op jit(solution)/shard_map/all_to_all | solution.py:230
  354.8 5.1 %shard_map.41 = f32[512,512]{1,0:T(8,128)} custom-call(f32[128,1,4096]{2,1,0:T(1,128)} %all_to_all.39.m_ref), custom_call_target="tpu_custom_call" | custom-call | tf_op jit(solution)/shard_map/pallas_call | solution.py:183
  359.8 1.5 reshape.72
  361.4 23.2 %all_to_all.40 = f32[128,4,512]{2,1,0:T(4,128)S(1)} all-to-all(f32[128,4,512]{2,1,0:T(4,128)S(1)} %reshape.72), channel_id=1, replica_groups=mesh['gz'=16,'gy'=8] {'gz','gy'}, dimensions={0} | all-to-all | bytes 2097152 | tf_op jit(solution)/shard_map/all_to_all | solution.py:44
  384.9 23.5 %all_to_all.41 = f32[128,4,512]{2,1,0:T(4,128)S(1)} all-to-all(f32[128,4,512]{2,1,0:T(4,128)S(1)} %broadcast_in_dim.5), channel_id=1, replica_groups=mesh['gz'=16,'gy'=8] {'gz','gy'}, dimensions={0} | all-to-all | bytes 2097152 | tf_op jit(solution)/shard_map/all_to_all | solution.py:49
  408.4 1.3 reshape.73.g_ref
  409.8 26.0 %shard_map.42.b_ref = f32[64,512]{1,0:T(8,128)} custom-call(f32[512,512]{1,0:T(8,128)} %reshape.73.g_ref, f32[64,512]{1,0:T(8,128)} %get-tuple-element.9.q_ref), custom_call_target="tpu_custom_call" | custom-call | tf_op jit(solution)/shard_map/pallas_call | solution.py:88
  435.8 3.3 shard_map.43
  439.1 1.3 reshape.74
  440.7 0.9 reshape.75
  441.6 1.0 copy.14
  (11 shorter events, 1.9 us)
Async XLA Ops:
  257.2 23.8 %all-to-all-start.2 = ((f32[128,4,512]{2,1,0:T(4,128)}), f32[128,4,512]{2,1,0:T(4,128)S(1)}, u32[]{:S(2)}, u32[]{:S(2)}) async-start(f32[128,4,512]{2,1,0:T(4,128)} %broadcast_in_dim.4), calls=%async_computation.2 | async-start | bytes 2097152 | tf_op jit(solution)/shard_map/all_to_all | solution.py:49
  308.4 0.9 copy-start

commit v15 on v13

--- a/solution.py
+++ b/solution.py
@@ -139,16 +139,20 @@
 
     block = fib_ref[:, 0, 0]
     block = block.reshape(block.shape[0] * block.shape[1], block.shape[2])
-    half = block.shape[0] // 2
-    for a, b in ((0, 0), (0, 1), (1, 1)):
-        g_ref[a * half : (a + 1) * half, b * half : (b + 1) * half] += lax.dot_general(
-            block[a * half : (a + 1) * half], block[b * half : (b + 1) * half],
-            (((1,), (1,)), ((), ())), precision=lax.Precision.HIGH,
-            preferred_element_type=jnp.float32)
+    size = block.shape[0] // 4
+    for a in range(4):
+        for b in range(a, 4):
+            g_ref[a * size : (a + 1) * size, b * size : (b + 1) * size] += lax.dot_general(
+                block[a * size : (a + 1) * size], block[b * size : (b + 1) * size],
+                (((1,), (1,)), ((), ())), precision=lax.Precision.HIGH,
+                preferred_element_type=jnp.float32)
 
     @pl.when(last)
     def _():
-        g_ref[half:, :half] = g_ref[:half, half:].T
+        for a in range(4):
+            for b in range(a):
+                g_ref[a * size : (a + 1) * size, b * size : (b + 1) * size] = (
+                    g_ref[b * size : (b + 1) * size, a * size : (a + 1) * size].T)
 
 
 def gram_z_pallas(fib):

time: 443 us -> 446 us (level)
  no operation moved by 1% of the time
where the time goes in v15:
time: 446 us; the launch traced here: 445 us
  blocking collectives  301 us (67%)
  Pallas kernels  91.1 us (20%)
  local copies, waits for them, and re-layouts  27.7 us (6%)
  waiting for transfers between devices  17.7 us (4%)
    all_to_all x1, blocking collectives, body(): lax.all_to_all(species_field, 'gz', split_axis=2, concat_axis=1, tiled=True)  193 us
    pallas_call x2, Pallas kernels, basis_pallas(): pl.pallas_call(functools.partial(_basis_kernel, iters), out_shape=jax.Sha...  50.3 us
    all_to_all x2, blocking collectives, sum_over_mesh(): lax.all_to_all(gram.reshape(count, rows // count, rows), axes, 0, 0, tile...  49.4 us
    all_to_all x1, blocking collectives, body(): mixed = lax.all_to_all(send, ('gz', 'gy'), 0, 0, tiled=True)  35.2 us
    all_to_all x1, blocking collectives, sum_over_mesh(): return lax.all_to_all(tiled, axes, 0, 0, tiled=True).reshape(rows, rows)  23.5 us
    pallas_call x1, Pallas kernels, gram_z_pallas(): pl.pallas_call(_gram_z_kernel, grid=(ys, species), in_specs=[pl.BlockSpec...  22 us
    all_to_all x1, waiting for transfers between devices, sum_over_mesh(): return lax.all_to_all(tiled, axes, 0, 0, tiled=True).reshape(rows, rows)  17.7 us
    unnamed x4, local copies, waits for them, and re-layouts  16.9 us
  transfers between devices with their start and end apart: 1, of which 1 were waited for; matrix products, arithmetic and copies ran while one was open for 0% of the time, Pallas kernels for 0%

profile of v15, /device:TPU:1, one launch (start us, length us, event | category | flops | bytes accessed | tf_op | source)
XLA Modules:
  0.0 444.9 jit_solution(591977890400932241)
XLA Ops:
  0.6 15.2 %copy.12 = f32[4,32,64,512]{3,1,0,2:T(8,128)S(1)} copy(f32[4,32,64,512]{3,2,1,0:T(8,128)} %param.1) | data formatting | bytes 33554432 | tf_op args[0]
  15.9 193.2 %all_to_all.37 = f32[4,32,64,512]{3,1,0,2:T(8,128)} all-to-all(f32[4,32,64,512]{3,1,0,2:T(8,128)S(1)} %copy.12), channel_id=1, replica_groups=mesh['gz'=16,'gy'=8] {'gz'}, dimensions={2} | all-to-all | bytes 33554432 | tf_op jit(solution)/shard_map/all_to_all | solution.py:226
  209.0 22.0 %shard_map.38 = f32[512,512]{1,0:T(8,128)} custom-call(f32[16,4,4,32,512]{4,3,2,1,0:T(8,128)} %bitcast.13), custom_call_target="tpu_custom_call" | custom-call | tf_op jit(solution)/shard_map/pallas_call | solution.py:161
  231.0 1.5 reshape.70
  232.5 26.2 %all_to_all.38 = f32[128,4,512]{2,1,0:T(4,128)S(1)} all-to-all(f32[128,4,512]{2,1,0:T(4,128)S(1)} %reshape.70), channel_id=1, replica_groups=mesh['gz'=16,'gy'=8] {'gz','gy'}, dimensions={0} | all-to-all | bytes 2097152 | tf_op jit(solution)/shard_map/all_to_all | solution.py:44
  259.0 1.1 broadcast_in_dim.4
  260.1 4.3 all-to-all-start.2
  264.6 1.6 multiply_cosine_fusion
  266.2 17.7 %all-to-all-done.2 = f32[128,4,512]{2,1,0:T(4,128)S(1)} async-done(((f32[128,4,512]{2,1,0:T(4,128)}), f32[128,4,512]{2,1,0:T(4,128)S(1)}, u32[]{:S(2)}, u32[]{:S(2)}) %all-to-all-start.2) | async-done | bytes 1048608 | tf_op jit(solution)/shard_map/all_to_all | solution.py:49
  283.9 1.4 reshape.71.g_ref
  285.2 25.2 %shard_map.39.bz_ref = f32[64,512]{1,0:T(8,128)} custom-call(f32[512,512]{1,0:T(8,128)} %reshape.71.g_ref, f32[64,512]{1,0:T(8,128)} %get-tuple-element.10.q_ref), custom_call_target="tpu_custom_call" | custom-call | tf_op jit(solution)/shard_map/pallas_call | solution.py:88
  310.4 0.9 copy-done
  311.3 10.4 %shard_map.40 = f32[128,1,4096]{2,1,0:T(1,128)S(1)} custom-call(f32[16,4,4,32,512]{4,3,2,1,0:T(8,128)} %bitcast.14, f32[64,512]{1,0:T(8,128)S(1)} %copy-done), custom_call_target="tpu_custom_call" | custom-call | tf_op jit(solution)/shard_map/pallas_call | solution.py:119
  321.7 35.2 %all_to_all.39.m_ref = f32[128,1,4096]{2,1,0:T(1,128)} all-to-all(f32[128,1,4096]{2,1,0:T(1,128)S(1)} %shard_map.40), channel_id=1, replica_groups=mesh['gz'=16,'gy'=8] {'gz','gy'}, dimensions={0} | all-to-all | bytes 4194304 | tf_op jit(solution)/shard_map/all_to_all | solution.py:234
  357.0 5.1 %shard_map.41 = f32[512,512]{1,0:T(8,128)} custom-call(f32[128,1,4096]{2,1,0:T(1,128)} %all_to_all.39.m_ref), custom_call_target="tpu_custom_call" | custom-call | tf_op jit(solution)/shard_map/pallas_call | solution.py:187
  362.0 1.5 reshape.72
  363.6 23.2 %all_to_all.40 = f32[128,4,512]{2,1,0:T(4,128)S(1)} all-to-all(f32[128,4,512]{2,1,0:T(4,128)S(1)} %reshape.72), channel_id=1, replica_groups=mesh['gz'=16,'gy'=8] {'gz','gy'}, dimensions={0} | all-to-all | bytes 2097152 | tf_op jit(solution)/shard_map/all_to_all | solution.py:44
  387.1 23.5 %all_to_all.41 = f32[128,4,512]{2,1,0:T(4,128)S(1)} all-to-all(f32[128,4,512]{2,1,0:T(4,128)S(1)} %broadcast_in_dim.5), channel_id=1, replica_groups=mesh['gz'=16,'gy'=8] {'gz','gy'}, dimensions={0} | all-to-all | bytes 2097152 | tf_op jit(solution)/shard_map/all_to_all | solution.py:49
  410.6 1.3 reshape.73.g_ref
  411.9 25.1 %shard_map.42.b_ref = f32[64,512]{1,0:T(8,128)} custom-call(f32[512,512]{1,0:T(8,128)} %reshape.73.g_ref, f32[64,512]{1,0:T(8,128)} %get-tuple-element.9.q_ref), custom_call_target="tpu_custom_call" | custom-call | tf_op jit(solution)/shard_map/pallas_call | solution.py:88
  437.1 3.3 shard_map.43
  440.4 1.3 reshape.74
  442.0 0.9 reshape.75
  442.9 1.0 copy.14
  (11 shorter events, 1.9 us)
Async XLA Ops:
  260.1 23.8 %all-to-all-start.2 = ((f32[128,4,512]{2,1,0:T(4,128)}), f32[128,4,512]{2,1,0:T(4,128)S(1)}, u32[]{:S(2)}, u32[]{:S(2)}) async-start(f32[128,4,512]{2,1,0:T(4,128)} %broadcast_in_dim.4), calls=%async_computation.2 | async-start | bytes 2097152 | tf_op jit(solution)/shard_map/all_to_all | solution.py:49
  310.4 0.9 copy-start

commit v16 on v13

--- a/solution.py
+++ b/solution.py
@@ -41,9 +41,11 @@
     axes = ("gz", "gy")
     count = lax.axis_size("gz") * lax.axis_size("gy")
     rows = gram.shape[0]
-    parts = lax.all_to_all(
-        gram.reshape(count, rows // count, rows), axes, 0, 0, tiled=True
-    )
+    if gram.ndim == 2:
+        gram = gram.reshape(count, rows // count, rows)
+    else:
+        rows = gram.shape[2]
+    parts = lax.all_to_all(gram, axes, 0, 0, tiled=True)
     mine = parts.sum(0)
     tiled = jnp.broadcast_to(mine[None], (count,) + mine.shape)
     return lax.all_to_all(tiled, axes, 0, 0, tiled=True).reshape(rows, rows)
@@ -166,23 +168,28 @@
 def _gram_y_kernel(y_local, m_ref, g_ref):
     count = m_ref.shape[0]
     width = m_ref.shape[2] // y_local
+    rows = count // y_local
     parts = [m_ref[:, 0, a * width : (a + 1) * width] for a in range(y_local)]
+    blocks = {}
     for a in range(y_local):
         for b in range(a, y_local):
-            g_ref[a * count : (a + 1) * count, b * count : (b + 1) * count] = lax.dot_general(
+            blocks[a, b] = lax.dot_general(
                 parts[a], parts[b], (((1,), (1,)), ((), ())),
                 precision=lax.Precision.HIGH, preferred_element_type=jnp.float32)
     for a in range(y_local):
         for b in range(a):
-            g_ref[a * count : (a + 1) * count, b * count : (b + 1) * count] = (
-                g_ref[b * count : (b + 1) * count, a * count : (a + 1) * count].T)
+            blocks[a, b] = blocks[b, a].T
+    for a in range(y_local):
+        g_ref[a * rows : (a + 1) * rows] = jnp.concatenate(
+            [blocks[a, b] for b in range(y_local)], axis=1).reshape(rows, y_local, -1)
 
 
 def gram_y_pallas(mixed, y_local):
-    size = mixed.shape[0] * y_local
+    count = mixed.shape[0]
+    size = count * y_local
     return pl.pallas_call(
         functools.partial(_gram_y_kernel, y_local),
-        out_shape=jax.ShapeDtypeStruct((size, size), jnp.float32),
+        out_shape=jax.ShapeDtypeStruct((count, y_local, size), jnp.float32),
         in_specs=[pl.BlockSpec(memory_space=pltpu.VMEM)],
         out_specs=pl.BlockSpec(memory_space=pltpu.VMEM),
     )(mixed)

time: 443 us -> 442 us (level)
  no operation moved by 1% of the time
where the time goes in v16:
time: 442 us; the launch traced here: 441 us
  blocking collectives  302 us (68%)
  Pallas kernels  88.2 us (20%)
  local copies, waits for them, and re-layouts  26.2 us (6%)
  waiting for transfers between devices  17.7 us (4%)
    all_to_all x1, blocking collectives, body(): lax.all_to_all(species_field, 'gz', split_axis=2, concat_axis=1, tiled=True)  193 us
    all_to_all x2, blocking collectives, sum_over_mesh(): parts = lax.all_to_all(gram, axes, 0, 0, tiled=True)  50.3 us
    pallas_call x2, Pallas kernels, basis_pallas(): pl.pallas_call(functools.partial(_basis_kernel, iters), out_shape=jax.Sha...  50.3 us
    all_to_all x1, blocking collectives, body(): mixed = lax.all_to_all(send, ('gz', 'gy'), 0, 0, tiled=True)  35.2 us
    all_to_all x1, blocking collectives, sum_over_mesh(): return lax.all_to_all(tiled, axes, 0, 0, tiled=True).reshape(rows, rows)  23.5 us
    pallas_call x1, Pallas kernels, gram_z_pallas(): pl.pallas_call(_gram_z_kernel, grid=(ys, species), in_specs=[pl.BlockSpec...  19.1 us
    all_to_all x1, waiting for transfers between devices, sum_over_mesh(): return lax.all_to_all(tiled, axes, 0, 0, tiled=True).reshape(rows, rows)  17.7 us
    unnamed x4, local copies, waits for them, and re-layouts  16.9 us
  transfers between devices with their start and end apart: 1, of which 1 were waited for; matrix products, arithmetic and copies ran while one was open for 0% of the time, Pallas kernels for 0%

profile of v16, /device:TPU:1, one launch (start us, length us, event | category | flops | bytes accessed | tf_op | source)
XLA Modules:
  0.0 441.4 jit_solution(585957928152986556)
XLA Ops:
  0.6 15.2 %copy.12 = f32[4,32,64,512]{3,1,0,2:T(8,128)S(1)} copy(f32[4,32,64,512]{3,2,1,0:T(8,128)} %param.1) | data formatting | bytes 33554432 | tf_op args[0]
  15.9 193.2 %all_to_all.37 = f32[4,32,64,512]{3,1,0,2:T(8,128)} all-to-all(f32[4,32,64,512]{3,1,0,2:T(8,128)S(1)} %copy.12), channel_id=1, replica_groups=mesh['gz'=16,'gy'=8] {'gz'}, dimensions={2} | all-to-all | bytes 33554432 | tf_op jit(solution)/shard_map/all_to_all | solution.py:229
  209.0 19.1 %shard_map.38 = f32[512,512]{1,0:T(8,128)} custom-call(f32[16,4,4,32,512]{4,3,2,1,0:T(8,128)} %bitcast.13), custom_call_target="tpu_custom_call" | custom-call | tf_op jit(solution)/shard_map/pallas_call | solution.py:159
  228.1 1.5 reshape.67
  229.6 26.2 %all_to_all.38 = f32[128,4,512]{2,1,0:T(4,128)S(1)} all-to-all(f32[128,4,512]{2,1,0:T(4,128)S(1)} %reshape.67), channel_id=1, replica_groups=mesh['gz'=16,'gy'=8] {'gz','gy'}, dimensions={0} | all-to-all | bytes 2097152 | tf_op jit(solution)/shard_map/all_to_all | solution.py:48
  256.1 1.1 broadcast_in_dim.4
  257.2 4.3 all-to-all-start.2
  261.7 1.6 multiply_cosine_fusion
  263.3 17.7 %all-to-all-done.2 = f32[128,4,512]{2,1,0:T(4,128)S(1)} async-done(((f32[128,4,512]{2,1,0:T(4,128)}), f32[128,4,512]{2,1,0:T(4,128)S(1)}, u32[]{:S(2)}, u32[]{:S(2)}) %all-to-all-start.2) | async-done | bytes 1048608 | tf_op jit(solution)/shard_map/all_to_all | solution.py:51
  281.0 1.4 reshape.68.g_ref
  282.4 25.2 %shard_map.39.bz_ref = f32[64,512]{1,0:T(8,128)} custom-call(f32[512,512]{1,0:T(8,128)} %reshape.68.g_ref, f32[64,512]{1,0:T(8,128)} %get-tuple-element.10.q_ref), custom_call_target="tpu_custom_call" | custom-call | tf_op jit(solution)/shard_map/pallas_call | solution.py:90
  307.5 0.9 copy-done
  308.4 10.4 %shard_map.40 = f32[128,1,4096]{2,1,0:T(1,128)S(1)} custom-call(f32[16,4,4,32,512]{4,3,2,1,0:T(8,128)} %bitcast.14, f32[64,512]{1,0:T(8,128)S(1)} %copy-done), custom_call_target="tpu_custom_call" | custom-call | tf_op jit(solution)/shard_map/pallas_call | solution.py:121
  318.9 35.2 %all_to_all.39.m_ref = f32[128,1,4096]{2,1,0:T(1,128)} all-to-all(f32[128,1,4096]{2,1,0:T(1,128)S(1)} %shard_map.40), channel_id=1, replica_groups=mesh['gz'=16,'gy'=8] {'gz','gy'}, dimensions={0} | all-to-all | bytes 4194304 | tf_op jit(solution)/shard_map/all_to_all | solution.py:237
  354.1 5.1 %shard_map.41 = f32[128,4,512]{2,1,0:T(4,128)} custom-call(f32[128,1,4096]{2,1,0:T(1,128)} %all_to_all.39.m_ref), custom_call_target="tpu_custom_call" | custom-call | tf_op jit(solution)/shard_map/pallas_call | solution.py:190
  359.2 24.1 %all_to_all.40 = f32[128,4,512]{2,1,0:T(4,128)S(1)} all-to-all(f32[128,4,512]{2,1,0:T(4,128)} %shard_map.41), channel_id=1, replica_groups=mesh['gz'=16,'gy'=8] {'gz','gy'}, dimensions={0} | all-to-all | bytes 2097152 | tf_op jit(solution)/shard_map/all_to_all | solution.py:48
  383.6 23.5 %all_to_all.41 = f32[128,4,512]{2,1,0:T(4,128)S(1)} all-to-all(f32[128,4,512]{2,1,0:T(4,128)S(1)} %broadcast_in_dim.5), channel_id=1, replica_groups=mesh['gz'=16,'gy'=8] {'gz','gy'}, dimensions={0} | all-to-all | bytes 2097152 | tf_op jit(solution)/shard_map/all_to_all | solution.py:51
  407.1 1.3 reshape.69.g_ref
  408.4 25.1 %shard_map.42.b_ref = f32[64,512]{1,0:T(8,128)} custom-call(f32[512,512]{1,0:T(8,128)} %reshape.69.g_ref, f32[64,512]{1,0:T(8,128)} %get-tuple-element.9.q_ref), custom_call_target="tpu_custom_call" | custom-call | tf_op jit(solution)/shard_map/pallas_call | solution.py:90
  433.6 3.3 shard_map.43
  436.9 1.3 reshape.70
  438.5 0.9 reshape.71
  439.4 1.0 copy.14
  440.6 0.8 copy.16
  (10 shorter events, 1.1 us)
Async XLA Ops:
  257.2 23.8 %all-to-all-start.2 = ((f32[128,4,512]{2,1,0:T(4,128)}), f32[128,4,512]{2,1,0:T(4,128)S(1)}, u32[]{:S(2)}, u32[]{:S(2)}) async-start(f32[128,4,512]{2,1,0:T(4,128)} %broadcast_in_dim.4), calls=%async_computation.2 | async-start | bytes 2097152 | tf_op jit(solution)/shard_map/all_to_all | solution.py:51
  307.5 0.9 copy-start

commit v17 on v14

--- a/solution.py
+++ b/solution.py
@@ -46,7 +46,7 @@
     )
     mine = parts.sum(0)
     tiled = jnp.broadcast_to(mine[None], (count,) + mine.shape)
-    return lax.all_to_all(tiled, axes, 0, 0, tiled=True).reshape(rows, rows)
+    return lax.all_to_all(tiled, axes, 0, 0, tiled=True)
 
 
 def _eliminate(c):
@@ -67,12 +67,13 @@
         factor = jnp.where(row_col > j, col / pivot, 0.0)
         return (left - factor * row_l, right - factor * row_r, diag - factor * col)
 
-    _, right, diag = lax.fori_loop(0, n, step, (c, right, diag), unroll=32)
+    _, right, diag = lax.fori_loop(0, n - 1, step, (c, right, diag), unroll=64)
     return right / jnp.sqrt(diag)
 
 
 def _basis_kernel(iters, g_ref, q_ref, out_ref):
     gram = g_ref[...]
+    gram = gram.reshape(gram.shape[0] * gram.shape[1], gram.shape[2])
     basis_t = q_ref[...]
     for _ in range(iters):
         product_t = jnp.dot(basis_t, gram, precision=lax.Precision.HIGH, preferred_element_type=jnp.float32)

time: 445 us -> 448 us (level)
  Pallas kernels: 90 us -> 94.9 us
    pallas_call x2, Pallas kernels: 52.1 us -> 57 us  [basis_pallas(): pl.pallas_call(functools.partial(_basis_kernel, iters), out_shape=jax.Sha...]
    unnamed x4 -> x6, local copies, waits for them, and re-layouts: 16.9 us -> 17.9 us
where the time goes in v17:
time: 448 us; the launch traced here: 447 us
  blocking collectives  301 us (67%)
  Pallas kernels  94.9 us (21%)
  local copies, waits for them, and re-layouts  26 us (6%)
  waiting for transfers between devices  17.7 us (4%)
    all_to_all x1, blocking collectives, body(): lax.all_to_all(species_field, 'gz', split_axis=2, concat_axis=1, tiled=True)  193 us
    pallas_call x2, Pallas kernels, basis_pallas(): pl.pallas_call(functools.partial(_basis_kernel, iters), out_shape=jax.Sha...  57 us
    all_to_all x2, blocking collectives, sum_over_mesh(): lax.all_to_all(gram.reshape(count, rows // count, rows), axes, 0, 0, tile...  49.4 us
    all_to_all x1, blocking collectives, body(): mixed = lax.all_to_all(send, ('gz', 'gy'), 0, 0, tiled=True)  35 us
    all_to_all x1, blocking collectives, sum_over_mesh(): return lax.all_to_all(tiled, axes, 0, 0, tiled=True)  23.8 us
    pallas_call x1, Pallas kernels, gram_z_pallas(): pl.pallas_call(_gram_z_kernel, grid=(ys, species), in_specs=[pl.BlockSpec...  19.1 us
    unnamed x6, local copies, waits for them, and re-layouts  17.9 us
    all_to_all x1, waiting for transfers between devices, sum_over_mesh(): return lax.all_to_all(tiled, axes, 0, 0, tiled=True)  17.7 us
  transfers between devices with their start and end apart: 1, of which 1 were waited for; matrix products, arithmetic and copies ran while one was open for 0% of the time, Pallas kernels for 0%

profile of v17, /device:TPU:1, one launch (start us, length us, event | category | flops | bytes accessed | tf_op | source)
XLA Modules:
  0.0 447.1 jit_solution(16768669978719779699)
XLA Ops:
  0.6 15.2 %copy.12 = f32[4,32,64,512]{3,1,0,2:T(8,128)S(1)} copy(f32[4,32,64,512]{3,2,1,0:T(8,128)} %param.1) | data formatting | bytes 33554432 | tf_op args[0]
  15.9 193.2 %all_to_all.37 = f32[4,32,64,512]{3,1,0,2:T(8,128)} all-to-all(f32[4,32,64,512]{3,1,0,2:T(8,128)S(1)} %copy.12), channel_id=1, replica_groups=mesh['gz'=16,'gy'=8] {'gz'}, dimensions={2} | all-to-all | bytes 33554432 | tf_op jit(solution)/shard_map/all_to_all | solution.py:223
  209.0 19.1 %shard_map.38 = f32[512,512]{1,0:T(8,128)} custom-call(f32[16,4,4,32,512]{4,3,2,1,0:T(8,128)} %bitcast.13), custom_call_target="tpu_custom_call" | custom-call | tf_op jit(solution)/shard_map/pallas_call | solution.py:158
  228.1 1.5 reshape.64
  229.6 26.2 %all_to_all.38 = f32[128,4,512]{2,1,0:T(4,128)S(1)} all-to-all(f32[128,4,512]{2,1,0:T(4,128)S(1)} %reshape.64), channel_id=1, replica_groups=mesh['gz'=16,'gy'=8] {'gz','gy'}, dimensions={0} | all-to-all | bytes 2097152 | tf_op jit(solution)/shard_map/all_to_all | solution.py:44
  256.1 1.1 broadcast_in_dim.4
  257.2 4.3 all-to-all-start.2
  261.7 1.6 multiply_cosine_fusion
  263.3 17.7 %all-to-all-done.2.g_ref = f32[128,4,512]{2,1,0:T(4,128)S(1)} async-done(((f32[128,4,512]{2,1,0:T(4,128)}), f32[128,4,512]{2,1,0:T(4,128)S(1)}, u32[]{:S(2)}, u32[]{:S(2)}) %all-to-all-start.2) | async-done | bytes 1048608 | tf_op jit(solution)/shard_map/all_to_all | solution.py:49
  281.0 1.0 copy-done.1
  282.0 28.5 %shard_map.39.bz_ref = f32[64,512]{1,0:T(8,128)} custom-call(f32[128,4,512]{2,1,0:T(4,128)} %copy-done.1, f32[64,512]{1,0:T(8,128)} %get-tuple-element.10.q_ref), custom_call_target="tpu_custom_call" | custom-call | tf_op jit(solution)/shard_map/pallas_call | solution.py:89
  310.5 0.9 copy-done
  311.4 10.4 %shard_map.40 = f32[128,1,4096]{2,1,0:T(1,128)S(1)} custom-call(f32[16,4,4,32,512]{4,3,2,1,0:T(8,128)} %bitcast.14, f32[64,512]{1,0:T(8,128)S(1)} %copy-done), custom_call_target="tpu_custom_call" | custom-call | tf_op jit(solution)/shard_map/pallas_call | solution.py:120
  321.9 35.0 %all_to_all.39.m_ref = f32[128,1,4096]{2,1,0:T(1,128)} all-to-all(f32[128,1,4096]{2,1,0:T(1,128)S(1)} %shard_map.40), channel_id=1, replica_groups=mesh['gz'=16,'gy'=8] {'gz','gy'}, dimensions={0} | all-to-all | bytes 4194304 | tf_op jit(solution)/shard_map/all_to_all | solution.py:231
  356.9 5.1 %shard_map.41 = f32[512,512]{1,0:T(8,128)} custom-call(f32[128,1,4096]{2,1,0:T(1,128)} %all_to_all.39.m_ref), custom_call_target="tpu_custom_call" | custom-call | tf_op jit(solution)/shard_map/pallas_call | solution.py:184
  361.9 1.5 reshape.65
  363.5 23.2 %all_to_all.40 = f32[128,4,512]{2,1,0:T(4,128)S(1)} all-to-all(f32[128,4,512]{2,1,0:T(4,128)S(1)} %reshape.65), channel_id=1, replica_groups=mesh['gz'=16,'gy'=8] {'gz','gy'}, dimensions={0} | all-to-all | bytes 2097152 | tf_op jit(solution)/shard_map/all_to_all | solution.py:44
  387.0 23.8 %all_to_all.41.g_ref = f32[128,4,512]{2,1,0:T(4,128)} all-to-all(f32[128,4,512]{2,1,0:T(4,128)S(1)} %broadcast_in_dim.5), channel_id=1, replica_groups=mesh['gz'=16,'gy'=8] {'gz','gy'}, dimensions={0} | all-to-all | bytes 2097152 | tf_op jit(solution)/shard_map/all_to_all | solution.py:49
  410.8 28.5 %shard_map.42.b_ref = f32[64,512]{1,0:T(8,128)} custom-call(f32[128,4,512]{2,1,0:T(4,128)} %all_to_all.41.g_ref, f32[64,512]{1,0:T(8,128)} %get-tuple-element.9.q_ref), custom_call_target="tpu_custom_call" | custom-call | tf_op jit(solution)/shard_map/pallas_call | solution.py:89
  439.3 3.3 shard_map.43
  442.7 1.3 reshape.66
  444.2 0.9 reshape.67
  445.2 1.0 copy.14
  446.4 0.8 copy.16
  (11 shorter events, 1.1 us)
Async XLA Ops:
  257.2 23.8 %all-to-all-start.2 = ((f32[128,4,512]{2,1,0:T(4,128)}), f32[128,4,512]{2,1,0:T(4,128)S(1)}, u32[]{:S(2)}, u32[]{:S(2)}) async-start(f32[128,4,512]{2,1,0:T(4,128)} %broadcast_in_dim.4), calls=%async_computation.2 | async-start | bytes 2097152 | tf_op jit(solution)/shard_map/all_to_all | solution.py:49
  281.0 1.0 copy-start.1
  310.5 0.9 copy-start

commit v18 on v17

--- a/solution.py
+++ b/solution.py
@@ -67,7 +67,7 @@
         factor = jnp.where(row_col > j, col / pivot, 0.0)
         return (left - factor * row_l, right - factor * row_r, diag - factor * col)
 
-    _, right, diag = lax.fori_loop(0, n - 1, step, (c, right, diag), unroll=64)
+    _, right, diag = lax.fori_loop(0, n, step, (c, right, diag), unroll=64)
     return right / jnp.sqrt(diag)
 
 

time: 448 us -> 441 us (0.984)
  Pallas kernels: 94.9 us -> 88.2 us
    pallas_call x2, Pallas kernels: 57 us -> 50.3 us  [basis_pallas(): pl.pallas_call(functools.partial(_basis_kernel, iters), out_shape=jax.Sha...]
where the time goes in v18:
time: 441 us; the launch traced here: 440 us
  blocking collectives  301 us (68%)
  Pallas kernels  88.2 us (20%)
  local copies, waits for them, and re-layouts  26 us (6%)
  waiting for transfers between devices  17.7 us (4%)
    all_to_all x1, blocking collectives, body(): lax.all_to_all(species_field, 'gz', split_axis=2, concat_axis=1, tiled=True)  193 us
    pallas_call x2, Pallas kernels, basis_pallas(): pl.pallas_call(functools.partial(_basis_kernel, iters), out_shape=jax.Sha...  50.3 us
    all_to_all x2, blocking collectives, sum_over_mesh(): lax.all_to_all(gram.reshape(count, rows // count, rows), axes, 0, 0, tile...  49.4 us
    all_to_all x1, blocking collectives, body(): mixed = lax.all_to_all(send, ('gz', 'gy'), 0, 0, tiled=True)  35 us
    all_to_all x1, blocking collectives, sum_over_mesh(): return lax.all_to_all(tiled, axes, 0, 0, tiled=True)  23.8 us
    pallas_call x1, Pallas kernels, gram_z_pallas(): pl.pallas_call(_gram_z_kernel, grid=(ys, species), in_specs=[pl.BlockSpec...  19.1 us
    unnamed x6, local copies, waits for them, and re-layouts  17.9 us
    all_to_all x1, waiting for transfers between devices, sum_over_mesh(): return lax.all_to_all(tiled, axes, 0, 0, tiled=True)  17.7 us
  transfers between devices with their start and end apart: 1, of which 1 were waited for; matrix products, arithmetic and copies ran while one was open for 0% of the time, Pallas kernels for 0%

profile of v18, /device:TPU:1, one launch (start us, length us, event | category | flops | bytes accessed | tf_op | source)
XLA Modules:
  0.0 440.4 jit_solution(10164951030639885018)
XLA Ops:
  0.6 15.2 %copy.12 = f32[4,32,64,512]{3,1,0,2:T(8,128)S(1)} copy(f32[4,32,64,512]{3,2,1,0:T(8,128)} %param.1) | data formatting | bytes 33554432 | tf_op args[0]
  15.9 193.2 %all_to_all.37 = f32[4,32,64,512]{3,1,0,2:T(8,128)} all-to-all(f32[4,32,64,512]{3,1,0,2:T(8,128)S(1)} %copy.12), channel_id=1, replica_groups=mesh['gz'=16,'gy'=8] {'gz'}, dimensions={2} | all-to-all | bytes 33554432 | tf_op jit(solution)/shard_map/all_to_all | solution.py:223
  209.0 19.1 %shard_map.38 = f32[512,512]{1,0:T(8,128)} custom-call(f32[16,4,4,32,512]{4,3,2,1,0:T(8,128)} %bitcast.13), custom_call_target="tpu_custom_call" | custom-call | tf_op jit(solution)/shard_map/pallas_call | solution.py:158
  228.1 1.5 reshape.64
  229.6 26.2 %all_to_all.38 = f32[128,4,512]{2,1,0:T(4,128)S(1)} all-to-all(f32[128,4,512]{2,1,0:T(4,128)S(1)} %reshape.64), channel_id=1, replica_groups=mesh['gz'=16,'gy'=8] {'gz','gy'}, dimensions={0} | all-to-all | bytes 2097152 | tf_op jit(solution)/shard_map/all_to_all | solution.py:44
  256.1 1.1 broadcast_in_dim.4
  257.2 4.3 all-to-all-start.2
  261.7 1.6 multiply_cosine_fusion
  263.3 17.7 %all-to-all-done.2.g_ref = f32[128,4,512]{2,1,0:T(4,128)S(1)} async-done(((f32[128,4,512]{2,1,0:T(4,128)}), f32[128,4,512]{2,1,0:T(4,128)S(1)}, u32[]{:S(2)}, u32[]{:S(2)}) %all-to-all-start.2) | async-done | bytes 1048608 | tf_op jit(solution)/shard_map/all_to_all | solution.py:49
  281.0 1.0 copy-done.1
  282.0 25.2 %shard_map.39.bz_ref = f32[64,512]{1,0:T(8,128)} custom-call(f32[128,4,512]{2,1,0:T(4,128)} %copy-done.1, f32[64,512]{1,0:T(8,128)} %get-tuple-element.10.q_ref), custom_call_target="tpu_custom_call" | custom-call | tf_op jit(solution)/shard_map/pallas_call | solution.py:89
  307.2 0.9 copy-done
  308.1 10.4 %shard_map.40 = f32[128,1,4096]{2,1,0:T(1,128)S(1)} custom-call(f32[16,4,4,32,512]{4,3,2,1,0:T(8,128)} %bitcast.14, f32[64,512]{1,0:T(8,128)S(1)} %copy-done), custom_call_target="tpu_custom_call" | custom-call | tf_op jit(solution)/shard_map/pallas_call | solution.py:120
  318.5 35.0 %all_to_all.39.m_ref = f32[128,1,4096]{2,1,0:T(1,128)} all-to-all(f32[128,1,4096]{2,1,0:T(1,128)S(1)} %shard_map.40), channel_id=1, replica_groups=mesh['gz'=16,'gy'=8] {'gz','gy'}, dimensions={0} | all-to-all | bytes 4194304 | tf_op jit(solution)/shard_map/all_to_all | solution.py:231
  353.5 5.1 %shard_map.41 = f32[512,512]{1,0:T(8,128)} custom-call(f32[128,1,4096]{2,1,0:T(1,128)} %all_to_all.39.m_ref), custom_call_target="tpu_custom_call" | custom-call | tf_op jit(solution)/shard_map/pallas_call | solution.py:184
  358.6 1.5 reshape.65
  360.1 23.2 %all_to_all.40 = f32[128,4,512]{2,1,0:T(4,128)S(1)} all-to-all(f32[128,4,512]{2,1,0:T(4,128)S(1)} %reshape.65), channel_id=1, replica_groups=mesh['gz'=16,'gy'=8] {'gz','gy'}, dimensions={0} | all-to-all | bytes 2097152 | tf_op jit(solution)/shard_map/all_to_all | solution.py:44
  383.7 23.8 %all_to_all.41.g_ref = f32[128,4,512]{2,1,0:T(4,128)} all-to-all(f32[128,4,512]{2,1,0:T(4,128)S(1)} %broadcast_in_dim.5), channel_id=1, replica_groups=mesh['gz'=16,'gy'=8] {'gz','gy'}, dimensions={0} | all-to-all | bytes 2097152 | tf_op jit(solution)/shard_map/all_to_all | solution.py:49
  407.5 25.1 %shard_map.42.b_ref = f32[64,512]{1,0:T(8,128)} custom-call(f32[128,4,512]{2,1,0:T(4,128)} %all_to_all.41.g_ref, f32[64,512]{1,0:T(8,128)} %get-tuple-element.9.q_ref), custom_call_target="tpu_custom_call" | custom-call | tf_op jit(solution)/shard_map/pallas_call | solution.py:89
  432.6 3.3 shard_map.43
  436.0 1.3 reshape.66
  437.5 0.9 reshape.67
  438.5 1.0 copy.14
  439.7 0.8 copy.16
  (11 shorter events, 1.1 us)
Async XLA Ops:
  257.2 23.8 %all-to-all-start.2 = ((f32[128,4,512]{2,1,0:T(4,128)}), f32[128,4,512]{2,1,0:T(4,128)S(1)}, u32[]{:S(2)}, u32[]{:S(2)}) async-start(f32[128,4,512]{2,1,0:T(4,128)} %broadcast_in_dim.4), calls=%async_computation.2 | async-start | bytes 2097152 | tf_op jit(solution)/shard_map/all_to_all | solution.py:49
  281.0 1.0 copy-start.1
  307.2 0.9 copy-start

commit v19 on v16

--- a/solution.py
+++ b/solution.py
@@ -48,7 +48,7 @@
     parts = lax.all_to_all(gram, axes, 0, 0, tiled=True)
     mine = parts.sum(0)
     tiled = jnp.broadcast_to(mine[None], (count,) + mine.shape)
-    return lax.all_to_all(tiled, axes, 0, 0, tiled=True).reshape(rows, rows)
+    return lax.all_to_all(tiled, axes, 0, 0, tiled=True)
 
 
 def _eliminate(c):
@@ -75,6 +75,7 @@
 
 def _basis_kernel(iters, g_ref, q_ref, out_ref):
     gram = g_ref[...]
+    gram = gram.reshape(gram.shape[0] * gram.shape[1], gram.shape[2])
     basis_t = q_ref[...]
     for _ in range(iters):
         product_t = jnp.dot(basis_t, gram, precision=lax.Precision.HIGH, preferred_element_type=jnp.float32)

time: 442 us -> 441 us (level)
    unnamed x4 -> x6, local copies, waits for them, and re-layouts: 16.9 us -> 17.9 us
where the time goes in v19:
time: 441 us; the launch traced here: 440 us
  blocking collectives  302 us (68%)
  Pallas kernels  88.2 us (20%)
  local copies, waits for them, and re-layouts  24.5 us (6%)
  waiting for transfers between devices  17.7 us (4%)
    all_to_all x1, blocking collectives, body(): lax.all_to_all(species_field, 'gz', split_axis=2, concat_axis=1, tiled=True)  193 us
    all_to_all x2, blocking collectives, sum_over_mesh(): parts = lax.all_to_all(gram, axes, 0, 0, tiled=True)  50.3 us
    pallas_call x2, Pallas kernels, basis_pallas(): pl.pallas_call(functools.partial(_basis_kernel, iters), out_shape=jax.Sha...  50.3 us
    all_to_all x1, blocking collectives, body(): mixed = lax.all_to_all(send, ('gz', 'gy'), 0, 0, tiled=True)  35 us
    all_to_all x1, blocking collectives, sum_over_mesh(): return lax.all_to_all(tiled, axes, 0, 0, tiled=True)  23.8 us
    pallas_call x1, Pallas kernels, gram_z_pallas(): pl.pallas_call(_gram_z_kernel, grid=(ys, species), in_specs=[pl.BlockSpec...  19.1 us
    unnamed x6, local copies, waits for them, and re-layouts  17.9 us
    all_to_all x1, waiting for transfers between devices, sum_over_mesh(): return lax.all_to_all(tiled, axes, 0, 0, tiled=True)  17.7 us
  transfers between devices with their start and end apart: 1, of which 1 were waited for; matrix products, arithmetic and copies ran while one was open for 0% of the time, Pallas kernels for 0%

profile of v19, /device:TPU:1, one launch (start us, length us, event | category | flops | bytes accessed | tf_op | source)
XLA Modules:
  0.0 439.8 jit_solution(4155325490275880397)
XLA Ops:
  0.6 15.2 %copy.12 = f32[4,32,64,512]{3,1,0,2:T(8,128)S(1)} copy(f32[4,32,64,512]{3,2,1,0:T(8,128)} %param.1) | data formatting | bytes 33554432 | tf_op args[0]
  15.9 193.2 %all_to_all.37 = f32[4,32,64,512]{3,1,0,2:T(8,128)} all-to-all(f32[4,32,64,512]{3,1,0,2:T(8,128)S(1)} %copy.12), channel_id=1, replica_groups=mesh['gz'=16,'gy'=8] {'gz'}, dimensions={2} | all-to-all | bytes 33554432 | tf_op jit(solution)/shard_map/all_to_all | solution.py:230
  209.0 19.1 %shard_map.38 = f32[512,512]{1,0:T(8,128)} custom-call(f32[16,4,4,32,512]{4,3,2,1,0:T(8,128)} %bitcast.13), custom_call_target="tpu_custom_call" | custom-call | tf_op jit(solution)/shard_map/pallas_call | solution.py:160
  228.1 1.5 reshape.61
  229.6 26.2 %all_to_all.38 = f32[128,4,512]{2,1,0:T(4,128)S(1)} all-to-all(f32[128,4,512]{2,1,0:T(4,128)S(1)} %reshape.61), channel_id=1, replica_groups=mesh['gz'=16,'gy'=8] {'gz','gy'}, dimensions={0} | all-to-all | bytes 2097152 | tf_op jit(solution)/shard_map/all_to_all | solution.py:48
  256.1 1.1 broadcast_in_dim.4
  257.2 4.3 all-to-all-start.2
  261.7 1.6 multiply_cosine_fusion
  263.3 17.7 %all-to-all-done.2.g_ref = f32[128,4,512]{2,1,0:T(4,128)S(1)} async-done(((f32[128,4,512]{2,1,0:T(4,128)}), f32[128,4,512]{2,1,0:T(4,128)S(1)}, u32[]{:S(2)}, u32[]{:S(2)}) %all-to-all-start.2) | async-done | bytes 1048608 | tf_op jit(solution)/shard_map/all_to_all | solution.py:51
  281.0 1.0 copy-done.1
  282.0 25.2 %shard_map.39.bz_ref = f32[64,512]{1,0:T(8,128)} custom-call(f32[128,4,512]{2,1,0:T(4,128)} %copy-done.1, f32[64,512]{1,0:T(8,128)} %get-tuple-element.10.q_ref), custom_call_target="tpu_custom_call" | custom-call | tf_op jit(solution)/shard_map/pallas_call | solution.py:91
  307.2 0.9 copy-done
  308.1 10.4 %shard_map.40 = f32[128,1,4096]{2,1,0:T(1,128)S(1)} custom-call(f32[16,4,4,32,512]{4,3,2,1,0:T(8,128)} %bitcast.14, f32[64,512]{1,0:T(8,128)S(1)} %copy-done), custom_call_target="tpu_custom_call" | custom-call | tf_op jit(solution)/shard_map/pallas_call | solution.py:122
  318.5 35.0 %all_to_all.39.m_ref = f32[128,1,4096]{2,1,0:T(1,128)} all-to-all(f32[128,1,4096]{2,1,0:T(1,128)S(1)} %shard_map.40), channel_id=1, replica_groups=mesh['gz'=16,'gy'=8] {'gz','gy'}, dimensions={0} | all-to-all | bytes 4194304 | tf_op jit(solution)/shard_map/all_to_all | solution.py:238
  353.5 5.1 %shard_map.41 = f32[128,4,512]{2,1,0:T(4,128)} custom-call(f32[128,1,4096]{2,1,0:T(1,128)} %all_to_all.39.m_ref), custom_call_target="tpu_custom_call" | custom-call | tf_op jit(solution)/shard_map/pallas_call | solution.py:191
  358.6 24.1 %all_to_all.40 = f32[128,4,512]{2,1,0:T(4,128)S(1)} all-to-all(f32[128,4,512]{2,1,0:T(4,128)} %shard_map.41), channel_id=1, replica_groups=mesh['gz'=16,'gy'=8] {'gz','gy'}, dimensions={0} | all-to-all | bytes 2097152 | tf_op jit(solution)/shard_map/all_to_all | solution.py:48
  383.0 23.8 %all_to_all.41.g_ref = f32[128,4,512]{2,1,0:T(4,128)} all-to-all(f32[128,4,512]{2,1,0:T(4,128)S(1)} %broadcast_in_dim.5), channel_id=1, replica_groups=mesh['gz'=16,'gy'=8] {'gz','gy'}, dimensions={0} | all-to-all | bytes 2097152 | tf_op jit(solution)/shard_map/all_to_all | solution.py:51
  406.8 25.1 %shard_map.42.b_ref = f32[64,512]{1,0:T(8,128)} custom-call(f32[128,4,512]{2,1,0:T(4,128)} %all_to_all.41.g_ref, f32[64,512]{1,0:T(8,128)} %get-tuple-element.9.q_ref), custom_call_target="tpu_custom_call" | custom-call | tf_op jit(solution)/shard_map/pallas_call | solution.py:91
  432.0 3.3 shard_map.43
  435.3 1.3 reshape.62
  436.6 0.3 copy.13
  436.9 0.9 reshape.63
  437.8 1.0 copy.14
  439.0 0.8 copy.16
  (10 shorter events, 0.8 us)
Async XLA Ops:
  257.2 23.8 %all-to-all-start.2 = ((f32[128,4,512]{2,1,0:T(4,128)}), f32[128,4,512]{2,1,0:T(4,128)S(1)}, u32[]{:S(2)}, u32[]{:S(2)}) async-start(f32[128,4,512]{2,1,0:T(4,128)} %broadcast_in_dim.4), calls=%async_computation.2 | async-start | bytes 2097152 | tf_op jit(solution)/shard_map/all_to_all | solution.py:51
  281.0 1.0 copy-start.1
  307.2 0.9 copy-start
